TPU v7x, 32 devices: a whole 2x2x4 slice. The times are simulated.
32 devices in a mesh: dp: 32 (over z, y, x, core).
Axes of the slice: x: 2, y: 2, z: 4, core: 2. Of those that a mesh axis runs over, the one named last changes fastest.
Arguments:
- layer_in: bfloat16 [3, 32768, 512], P(None, 'dp'), may hold values from -6 to 6
- memory: bfloat16 [3, 8192, 512], P(None, 'dp'), may hold values from -6 to 6
- seg_ids: int32 [3, 32, 1024], P(None, 'dp'), may hold values from 0 to 7, never falling along the last dimension, each value on 1 to 256 neighbouring positions
- offsets: int32 [3, 32, 8], P(None, 'dp'), may hold values from 1 to 1024
- cotangent: bfloat16 [3, 32768, 512], P(None, 'dp'), may hold values from -6 to 6
- attn_q: bfloat16 [2, 512, 512], P(None, 'dp'), may hold values from -0.5 to 0.5
- attn_k: bfloat16 [2, 512, 512], P(None, 'dp'), may hold values from -0.25 to 0.25
- attn_v: bfloat16 [2, 512, 512], P(None, 'dp'), may hold values from -0.25 to 0.25
- attn_o: bfloat16 [2, 512, 512], P(None, 'dp'), may hold values from -1 to 1
- w_in: bfloat16 [512, 2048], P('dp'), may hold values from -0.25 to 0.25
- w_out: bfloat16 [2048, 512], P('dp'), may hold values from -0.1875 to 0.1875
- ffn_bias: bfloat16 [2048], P('dp'), may hold values from -3 to 3
- out_bias: bfloat16 [3, 512], P(None, 'dp'), may hold values from -2 to 2
- omega: bfloat16 [3, 512], P(None, 'dp'), may hold values from 0.5 to 2
- ln_gain: bfloat16 [3, 512], P(None, 'dp'), may hold values from 0.25 to 1.75
- ln_bias: bfloat16 [3, 512], P(None, 'dp'), may hold values from -2 to 2
Outputs:
- layer_out: bfloat16 [3, 32768, 512], P(None, 'dp')
- input_grad: bfloat16 [3, 32768, 512], P(None, 'dp')
- memory_grad: bfloat16 [3, 8192, 512], P(None, 'dp')
- grad_q: float32 [2, 512, 512], P(None, 'dp')
- grad_k: float32 [2, 512, 512], P(None, 'dp')
- grad_v: float32 [2, 512, 512], P(None, 'dp')
- grad_o: float32 [2, 512, 512], P(None, 'dp')
- grad_w_in: float32 [512, 2048], P('dp')
- grad_w_out: float32 [2048, 512], P('dp')
- grad_ffn_bias: float32 [2048], P('dp')
- grad_out_bias: float32 [3, 512], P(None, 'dp')
- grad_omega: float32 [3, 512], P(None, 'dp')
- grad_gain: float32 [3, 512], P(None, 'dp')
- grad_shift: float32 [3, 512], P(None, 'dp')
Inputs may be any that keep to these rules, and one draw needn't show every extreme that they name: `seg_ids`: within each block of 1024 rows, the continuation that a row belongs to: never falling along the rows, every continuation present with 1 to 256 rows. Read only in blocks of even index. `offsets`: for each continuation, the number of leading prompt positions that it attends to. Read only in blocks of even index.
All inputs are finite; a program needn't handle non-finite values.
Results may differ from a plain program's by a relative error of at most 0.028.
The roundings to bfloat16 on the way count: a program that leaves them out, or rounds other values in their place, can miss the bound.
Values may be sent and summed in bfloat16 or wider, within the bound.
No kernel may reach another device: no remote copies, remote signals or barrier semaphores. Data moves between devices by JAX's collectives and lax.ppermute only.
A program may use at most 704 MiB of HBM per device.

v0:
```python
import jax
import jax.numpy as jnp
from jax import lax
from jax.sharding import PartitionSpec as P

HEADS = 8


EPS = 1e-05
NEG = -1e30


def passed_along(block, axis, distance):
    devices = range(lax.axis_size(axis))
    route = [(i - distance, i) for i in devices if i - distance in devices]
    return lax.ppermute(block, axis, route)


def from_partner(x, axis, bit):
    return lax.ppermute(x, axis, [(i, i ^ 1 << bit) for i in range(lax.axis_size(axis))])


def product(left, right):
    return jnp.dot(left, right, preferred_element_type=jnp.float32)


def product_tn(left, right):
    return lax.dot_general(
        left, right, (((0,), (0,)), ((), ())), preferred_element_type=jnp.float32
    )


def product_nt(left, right):
    return lax.dot_general(
        left, right, (((1,), (1,)), ((), ())), preferred_element_type=jnp.float32
    )


def to_low(values):
    return values.astype(jnp.bfloat16)


def smooth_gate(values):
    return jax.nn.gelu(values, approximate=True)


def split_heads(values):
    return values.reshape(values.shape[0], HEADS, values.shape[1] // HEADS)


def norm_forward(values, norm_gain, norm_shift):
    row_mean = jnp.mean(values, axis=-1, keepdims=True)
    centred = values - row_mean
    inv_std = lax.rsqrt(jnp.mean(centred * centred, axis=-1, keepdims=True) + EPS)
    normed = centred * inv_std
    return (normed * norm_gain + norm_shift, normed, inv_std)


def norm_backward(grad_in, normed, inv_std, norm_gain):
    scaled = grad_in * norm_gain
    centred = scaled - jnp.mean(scaled, axis=-1, keepdims=True)
    grad_z = inv_std * (centred - normed * jnp.mean(scaled * normed, axis=-1, keepdims=True))
    return (grad_z, jnp.sum(grad_in * normed, axis=0), jnp.sum(grad_in, axis=0))


def no_mask(row_start, block_rows):
    return None


def block_scores(queries, key_rows, allowed):
    score_scale = (key_rows.shape[1] // HEADS) ** (-0.5)
    raw_scores = (
        jnp.einsum(
            "qhd,khd->hqk",
            split_heads(queries),
            split_heads(key_rows),
            preferred_element_type=jnp.float32,
        )
        * score_scale
    )
    if allowed is None:
        return raw_scores
    return jnp.where(allowed[None], raw_scores, NEG)


def attend_forward(queries, key_rows, values, mask_at):
    row_count = queries.shape[0]
    block_rows = min(512, row_count)
    out_list = []
    totals = []
    for row_start in range(0, row_count, block_rows):
        scores = block_scores(
            queries[row_start : row_start + block_rows], key_rows, mask_at(row_start, block_rows)
        )
        log_total = jax.nn.logsumexp(scores, axis=-1, keepdims=True)
        prob_rows = to_low(jnp.exp(scores - log_total))
        mixed = jnp.einsum(
            "hqk,khd->qhd", prob_rows, split_heads(values), preferred_element_type=jnp.float32
        )
        out_list.append(mixed.reshape(block_rows, -1))
        totals.append(log_total)
    return (jnp.concatenate(out_list, axis=0), totals)


def attend_backward(queries, key_rows, values, grad_out, totals, mask_at):
    row_count = queries.shape[0]
    block_rows = min(512, row_count)
    score_scale = (key_rows.shape[1] // HEADS) ** (-0.5)
    heads_k = split_heads(key_rows)
    heads_v = split_heads(values)
    grad_q = []
    grad_k = jnp.zeros(key_rows.shape, jnp.float32)
    grad_v = jnp.zeros(values.shape, jnp.float32)
    for number, row_start in enumerate(range(0, row_count, block_rows)):
        query_blk = queries[row_start : row_start + block_rows]
        scores = block_scores(query_blk, key_rows, mask_at(row_start, block_rows))
        prob_rows = jnp.exp(scores - totals[number])
        grad_blk = split_heads(grad_out[row_start : row_start + block_rows])
        grad_prob = jnp.einsum(
            "qhd,khd->hqk", grad_blk, heads_v, preferred_element_type=jnp.float32
        )
        grad_score = to_low(
            prob_rows * (grad_prob - jnp.sum(grad_prob * prob_rows, axis=-1, keepdims=True))
        )
        grad_q.append(
            (
                jnp.einsum("hqk,khd->qhd", grad_score, heads_k, preferred_element_type=jnp.float32)
                * score_scale
            ).reshape(block_rows, -1)
        )
        grad_k = grad_k + (
            jnp.einsum(
                "hqk,qhd->khd",
                grad_score,
                split_heads(query_blk),
                preferred_element_type=jnp.float32,
            )
            * score_scale
        ).reshape(key_rows.shape)
        grad_v = grad_v + jnp.einsum(
            "hqk,qhd->khd", to_low(prob_rows), grad_blk, preferred_element_type=jnp.float32
        ).reshape(values.shape)
    return (jnp.concatenate(grad_q, axis=0), grad_k, grad_v)


def fetch_forward(shards):
    return (
        lax.all_gather(shards[0], "dp", axis=1, tiled=True),
        lax.all_gather(shards[1], "dp", axis=1, tiled=True),
        lax.all_gather(shards[2], "dp", axis=1, tiled=True),
        lax.all_gather(shards[3], "dp", axis=1, tiled=True),
        lax.all_gather(shards[4], "dp", axis=0, tiled=True),
        lax.all_gather(shards[5], "dp", axis=0, tiled=True),
        lax.all_gather(shards[6], "dp", axis=0, tiled=True),
        lax.all_gather(shards[7], "dp", axis=1, tiled=True),
        lax.all_gather(shards[8], "dp", axis=1, tiled=True),
        lax.all_gather(shards[9], "dp", axis=1, tiled=True),
        lax.all_gather(shards[10], "dp", axis=1, tiled=True),
    )


def fetch_backward(shards):
    return (
        lax.all_gather(shards[0], "dp", axis=1, tiled=True),
        lax.all_gather(shards[1], "dp", axis=1, tiled=True),
        lax.all_gather(shards[2], "dp", axis=1, tiled=True),
        lax.all_gather(shards[3], "dp", axis=1, tiled=True),
        lax.all_gather(shards[4], "dp", axis=0, tiled=True),
        lax.all_gather(shards[5], "dp", axis=0, tiled=True),
        lax.all_gather(shards[6], "dp", axis=0, tiled=True),
        lax.all_gather(shards[7], "dp", axis=1, tiled=True),
        lax.all_gather(shards[8], "dp", axis=1, tiled=True),
        lax.all_gather(shards[9], "dp", axis=1, tiled=True),
        lax.all_gather(shards[10], "dp", axis=1, tiled=True),
    )


def make_mask(seg_row, off_row, is_prompt):
    row_count = seg_row.shape[0]
    cont_index = jnp.arange(off_row.shape[0], dtype=jnp.int32)
    reach = jnp.sum(jnp.where(seg_row[:, None] == cont_index[None, :], off_row[None, :], 0), axis=1)
    places = jnp.arange(row_count, dtype=jnp.int32)

    def mask_at(row_start, block_rows):
        rows_here = places[row_start : row_start + block_rows]
        prefix_ok = jnp.logical_and(
            jnp.logical_not(is_prompt),
            places[None, :] < reach[row_start : row_start + block_rows, None],
        )
        same_cont = seg_row[None, :] == seg_row[row_start : row_start + block_rows, None]
        local_ok = jnp.logical_and(
            places[None, :] <= rows_here[:, None], jnp.logical_or(is_prompt, same_cont)
        )
        return jnp.concatenate([prefix_ok, local_ok], axis=1)

    return mask_at


def run_forward(rows_in, mem_rows, mask_at, weights, is_prompt):
    (
        w_query,
        w_key,
        w_value,
        w_outp,
        w_first,
        w_second,
        bias_ffn,
        bias_out,
        omega_res,
        gains,
        shifts,
    ) = weights
    rows_float = rows_in.astype(jnp.float32)
    self_q = to_low(product(rows_in, w_query[0]))
    self_k = to_low(product(rows_in, w_key[0]))
    self_v = to_low(product(rows_in, w_value[0]))
    prompt_k, prompt_v = passed_along((self_k, self_v), "dp", -1)
    key_rows = jnp.concatenate([prompt_k, self_k], axis=0)
    value_rows = jnp.concatenate([prompt_v, self_v], axis=0)
    self_out, self_totals = attend_forward(self_q, key_rows, value_rows, mask_at)
    self_low = to_low(self_out)
    first, normed_one, inv_one = norm_forward(
        rows_float * omega_res[0] + (product(self_low, w_outp[0]) + bias_out[0]),
        gains[0],
        shifts[0],
    )
    first_low = to_low(first)
    first_float = first_low.astype(jnp.float32)
    cross_q = to_low(product(first_low, w_query[1]))
    own_mk = to_low(product(mem_rows, w_key[1]))
    own_mv = to_low(product(mem_rows, w_value[1]))
    far_mk, far_mv = from_partner((own_mk, own_mv), "dp", 0)
    mem_keys = jnp.where(
        is_prompt,
        jnp.concatenate([own_mk, far_mk], axis=0),
        jnp.concatenate([far_mk, own_mk], axis=0),
    )
    mem_values = jnp.where(
        is_prompt,
        jnp.concatenate([own_mv, far_mv], axis=0),
        jnp.concatenate([far_mv, own_mv], axis=0),
    )
    cross_out, cross_totals = attend_forward(cross_q, mem_keys, mem_values, no_mask)
    cross_low = to_low(cross_out)
    second, normed_two, inv_two = norm_forward(
        first_float * omega_res[1] + (product(cross_low, w_outp[1]) + bias_out[1]),
        gains[1],
        shifts[1],
    )
    second_low = to_low(second)
    second_float = second_low.astype(jnp.float32)
    hidden_pre = product(second_low, w_first) + bias_ffn
    act_low = to_low(smooth_gate(hidden_pre))
    final, normed_three, inv_three = norm_forward(
        second_float * omega_res[2] + (product(act_low, w_second) + bias_out[2]),
        gains[2],
        shifts[2],
    )
    kept = (
        rows_float,
        self_q,
        key_rows,
        value_rows,
        self_totals,
        self_low,
        normed_one,
        inv_one,
        first_low,
        first_float,
        cross_q,
        mem_keys,
        mem_values,
        cross_totals,
        cross_low,
        normed_two,
        inv_two,
        second_low,
        second_float,
        hidden_pre,
        act_low,
        normed_three,
        inv_three,
    )
    return (kept, to_low(final))


def run_backward(rows_in, mem_rows, cot_rows, mask_at, weights, is_prompt, kept):
    (
        w_query,
        w_key,
        w_value,
        w_outp,
        w_first,
        w_second,
        bias_ffn,
        bias_out,
        omega_res,
        gains,
        shifts,
    ) = weights
    (
        rows_float,
        self_q,
        key_rows,
        value_rows,
        self_totals,
        self_low,
        normed_one,
        inv_one,
        first_low,
        first_float,
        cross_q,
        mem_keys,
        mem_values,
        cross_totals,
        cross_low,
        normed_two,
        inv_two,
        second_low,
        second_float,
        hidden_pre,
        act_low,
        normed_three,
        inv_three,
    ) = kept
    grad_top = cot_rows.astype(jnp.float32)
    grad_z3, grad_g3, grad_s3 = norm_backward(grad_top, normed_three, inv_three, gains[2])
    grad_om3 = jnp.sum(grad_z3 * second_float, axis=0)
    grad_f = to_low(grad_z3)
    grad_b3 = jnp.sum(grad_f.astype(jnp.float32), axis=0)
    grad_second_w = product_tn(act_low, grad_f)
    grad_act = to_low(product_nt(grad_f, w_second))
    gate_value, gate_pull = jax.vjp(smooth_gate, hidden_pre)
    grad_pre = to_low(gate_pull(grad_act.astype(jnp.float32))[0])
    grad_bias_ffn = jnp.sum(grad_pre.astype(jnp.float32), axis=0)
    grad_first_w = product_tn(second_low, grad_pre)
    grad_h2 = product_nt(grad_pre, w_first) + grad_z3 * omega_res[2]
    grad_z2, grad_g2, grad_s2 = norm_backward(grad_h2, normed_two, inv_two, gains[1])
    grad_om2 = jnp.sum(grad_z2 * first_float, axis=0)
    grad_c = to_low(grad_z2)
    grad_b2 = jnp.sum(grad_c.astype(jnp.float32), axis=0)
    grad_wo_cross = product_tn(cross_low, grad_c)
    grad_cross_out = to_low(product_nt(grad_c, w_outp[1]))
    grad_cq, grad_mk, grad_mv = attend_backward(
        cross_q, mem_keys, mem_values, grad_cross_out, cross_totals, no_mask
    )
    mem_count = mem_rows.shape[0]
    own_dk = jnp.where(is_prompt, grad_mk[:mem_count], grad_mk[mem_count:])
    own_dv = jnp.where(is_prompt, grad_mv[:mem_count], grad_mv[mem_count:])
    far_dk = jnp.where(is_prompt, grad_mk[mem_count:], grad_mk[:mem_count])
    far_dv = jnp.where(is_prompt, grad_mv[mem_count:], grad_mv[:mem_count])
    got_dk, got_dv = (
        from_partner(far_dk.astype(jnp.bfloat16), "dp", 0).astype(far_dk.dtype),
        from_partner(far_dv.astype(jnp.bfloat16), "dp", 0).astype(far_dv.dtype),
    )
    mem_dk = to_low(own_dk + got_dk)
    mem_dv = to_low(own_dv + got_dv)
    grad_wk_cross = product_tn(mem_rows, mem_dk)
    grad_wv_cross = product_tn(mem_rows, mem_dv)
    mem_grad = to_low(product_nt(mem_dk, w_key[1]) + product_nt(mem_dv, w_value[1]))
    cross_dq = to_low(grad_cq)
    grad_wq_cross = product_tn(first_low, cross_dq)
    grad_h1 = product_nt(cross_dq, w_query[1]) + grad_z2 * omega_res[1]
    grad_z1, grad_g1, grad_s1 = norm_backward(grad_h1, normed_one, inv_one, gains[0])
    grad_om1 = jnp.sum(grad_z1 * rows_float, axis=0)
    grad_a = to_low(grad_z1)
    grad_b1 = jnp.sum(grad_a.astype(jnp.float32), axis=0)
    grad_wo_self = product_tn(self_low, grad_a)
    grad_self_out = to_low(product_nt(grad_a, w_outp[0]))
    grad_sq, grad_sk, grad_sv = attend_backward(
        self_q, key_rows, value_rows, grad_self_out, self_totals, mask_at
    )
    row_count = self_q.shape[0]
    got_pk, got_pv = (
        passed_along(grad_sk[:row_count].astype(jnp.bfloat16), "dp", 1).astype(jnp.float32),
        passed_along(grad_sv[:row_count].astype(jnp.bfloat16), "dp", 1).astype(jnp.float32),
    )
    self_dk = to_low(grad_sk[row_count:] + jnp.where(is_prompt, got_pk, 0.0))
    self_dv = to_low(grad_sv[row_count:] + jnp.where(is_prompt, got_pv, 0.0))
    self_dq = to_low(grad_sq)
    grad_wq_self = product_tn(rows_in, self_dq)
    grad_wk_self = product_tn(rows_in, self_dk)
    grad_wv_self = product_tn(rows_in, self_dv)
    rows_grad = to_low(
        product_nt(self_dq, w_query[0])
        + product_nt(self_dk, w_key[0])
        + product_nt(self_dv, w_value[0])
        + grad_z1 * omega_res[0]
    )
    grads = (
        jnp.stack([grad_wq_self, grad_wq_cross]),
        jnp.stack([grad_wk_self, grad_wk_cross]),
        jnp.stack([grad_wv_self, grad_wv_cross]),
        jnp.stack([grad_wo_self, grad_wo_cross]),
        grad_first_w,
        grad_second_w,
        grad_bias_ffn,
        jnp.stack([grad_b1, grad_b2, grad_b3]),
        jnp.stack([grad_om1, grad_om2, grad_om3]),
        jnp.stack([grad_g1, grad_g2, grad_g3]),
        jnp.stack([grad_s1, grad_s2, grad_s3]),
    )
    return (grads, rows_grad, mem_grad)


def body(
    layer_in,
    memory,
    seg_ids,
    offsets,
    cotangent,
    attn_q,
    attn_k,
    attn_v,
    attn_o,
    w_in,
    w_out,
    ffn_bias,
    out_bias,
    omega,
    ln_gain,
    ln_bias,
):
    shards = (
        attn_q,
        attn_k,
        attn_v,
        attn_o,
        w_in,
        w_out,
        ffn_bias,
        out_bias,
        omega,
        ln_gain,
        ln_bias,
    )
    is_prompt = lax.axis_index("dp") % 2 == 1
    micro_count = layer_in.shape[0]
    grad_total = None
    out_rows, input_rows, memory_rows = ([], [], [])
    for number in range(micro_count):
        forward_w = fetch_forward(shards)
        mask_at = make_mask(seg_ids[number, 0], offsets[number, 0], is_prompt)
        kept, final = run_forward(layer_in[number], memory[number], mask_at, forward_w, is_prompt)
        backward_w = fetch_backward(shards)
        grads, rows_grad, mem_grad = run_backward(
            layer_in[number],
            memory[number],
            cotangent[number],
            mask_at,
            backward_w,
            is_prompt,
            kept,
        )
        grad_total = grads if grad_total is None else jax.tree.map(jnp.add, grad_total, grads)
        out_rows.append(final)
        input_rows.append(rows_grad)
        memory_rows.append(mem_grad)
    summed = (
        lax.psum_scatter(grad_total[0], "dp", scatter_dimension=1, tiled=True),
        lax.psum_scatter(grad_total[1], "dp", scatter_dimension=1, tiled=True),
        lax.psum_scatter(grad_total[2], "dp", scatter_dimension=1, tiled=True),
        lax.psum_scatter(grad_total[3], "dp", scatter_dimension=1, tiled=True),
        lax.psum_scatter(grad_total[4], "dp", scatter_dimension=0, tiled=True),
        lax.psum_scatter(grad_total[5], "dp", scatter_dimension=0, tiled=True),
        lax.psum_scatter(grad_total[6], "dp", scatter_dimension=0, tiled=True),
        lax.psum_scatter(grad_total[7], "dp", scatter_dimension=1, tiled=True),
        lax.psum_scatter(grad_total[8], "dp", scatter_dimension=1, tiled=True),
        lax.psum_scatter(grad_total[9], "dp", scatter_dimension=1, tiled=True),
        lax.psum_scatter(grad_total[10], "dp", scatter_dimension=1, tiled=True),
    )
    return (
        jnp.stack(out_rows),
        jnp.stack(input_rows),
        jnp.stack(memory_rows),
        summed[0],
        summed[1],
        summed[2],
        summed[3],
        summed[4],
        summed[5],
        summed[6],
        summed[7],
        summed[8],
        summed[9],
        summed[10],
    )


def solution(mesh):
    placed = (
        P(None, "dp", None),
        P(None, "dp", None),
        P(None, "dp", None),
        P(None, "dp", None),
        P(None, "dp", None),
        P(None, "dp", None),
        P(None, "dp", None),
        P(None, "dp", None),
        P(None, "dp", None),
        P("dp", None),
        P("dp", None),
        P("dp"),
        P(None, "dp"),
        P(None, "dp"),
        P(None, "dp"),
        P(None, "dp"),
    )
    return jax.shard_map(
        body,
        mesh=mesh,
        in_specs=placed,
        out_specs=(
            P(None, "dp", None),
            P(None, "dp", None),
            P(None, "dp", None),
            P(None, "dp", None),
            P(None, "dp", None),
            P(None, "dp", None),
            P(None, "dp", None),
            P("dp", None),
            P("dp", None),
            P("dp"),
            P(None, "dp"),
            P(None, "dp"),
            P(None, "dp"),
            P(None, "dp"),
        ),
        check_vma=False,
    )
```

profile of v0, /device:TPU:0, one launch (start us, length us, event | category | flops | bytes accessed | tf_op | source)
XLA Modules:
  0.0 2657.8 jit_solution(16691670665300049008)
XLA Ops:
  14.2 42.1 %all-reduce = bf16[2048]{0:T(1024)(128)(2,1)S(1)} all-reduce(bf16[2048]{0:T(1024)(128)(2,1)S(1)} %dynamic-update-slice), channel_id=1, replica_groups=mesh['dp'=32] {'dp'}, use_global_device_ids=true, to_apply=%add | all-reduce | flops 2048 | bytes 8192
  60.0 40.6 %all-gather.1 = bf16[32,16,3]{1,2,0:T(4,128)(2,1)S(1)} all-gather(bf16[1,16,3]{1,2,0:T(4,128)(2,1)} %bitcast.1036), channel_id=1, replica_groups=mesh['dp'=32] {'dp'}, dimensions={0}, use_global_device_ids=true | all-gather | bytes 3168 | tf_op jit(solution)/shard_map/all_gather | solution.py:155
  101.3 36.9 %all-gather = bf16[32,16,3]{1,2,0:T(4,128)(2,1)S(1)} all-gather(bf16[1,16,3]{1,2,0:T(4,128)(2,1)} %bitcast.1037), channel_id=1, replica_groups=mesh['dp'=32] {'dp'}, dimensions={0}, use_global_device_ids=true | all-gather | bytes 3168 | tf_op jit(solution)/shard_map/all_gather | solution.py:156
  138.9 38.2 %all-gather.2 = bf16[32,16,3]{1,2,0:T(4,128)(2,1)S(1)} all-gather(bf16[1,16,3]{1,2,0:T(4,128)(2,1)} %bitcast.1038), channel_id=1, replica_groups=mesh['dp'=32] {'dp'}, dimensions={0}, use_global_device_ids=true | all-gather | bytes 3168 | tf_op jit(solution)/shard_map/all_gather | solution.py:157
  177.9 36.9 %all-gather.3 = bf16[32,16,3]{1,2,0:T(4,128)(2,1)S(1)} all-gather(bf16[1,16,3]{1,2,0:T(4,128)(2,1)} %bitcast.1039), channel_id=1, replica_groups=mesh['dp'=32] {'dp'}, dimensions={0}, use_global_device_ids=true | all-gather | bytes 3168 | tf_op jit(solution)/shard_map/all_gather | solution.py:158
  1051.1 26.0 multiply_reduce_fusion.5
  1077.1 28.2 %multiply_convert_fusion.5 = bf16[8,512,2048]{2,1,0:T(8,128)(2,1)} fusion(f32[8,512,2048]{2,1,0:T(8,128)} %get-tuple-element.305, f32[8,512,2048]{2,1,0:T(8,128)} %get-tuple-element.240, f32[8,512]{1,0:T(8,128)S(1)} %get-tuple-element.304, f32[8,512]{1,0:T(8,128)S(1)} %copy-done.216, pred[512,2048]{1,0:T(8,128)(4,1)} %get-tuple-element.314), kind=kLoop, calls=%fused_computation.10 | loop fusion | flops 50331648 | bytes 84967424 | tf_op jit(solution)/shard_map/convert_element_type | solution.py:40
  1128.0 27.9 %multiply_convert_fusion.4 = bf16[8,512,2048]{2,1,0:T(8,128)(2,1)} fusion(f32[8,512,2048]{2,1,0:T(8,128)} %get-tuple-element.303, f32[8,512,2048]{2,1,0:T(8,128)} %get-tuple-element.238, f32[8,512]{1,0:T(8,128)S(1)} %get-tuple-element.302, f32[8,512]{1,0:T(8,128)S(1)} %copy-done.218, pred[512,2048]{1,0:T(8,128)(4,1)S(1)} %copy-done.26), kind=kLoop, calls=%fused_computation.8 | loop fusion | flops 50331648 | bytes 84967424 | tf_op jit(solution)/shard_map/convert_element_type | solution.py:40
  1180.4 25.6 multiply_reduce_fusion
  1206.1 25.6 multiply_reduce_fusion.1
  1231.7 28.4 %multiply_convert_fusion.1 = bf16[8,512,2048]{2,1,0:T(8,128)(2,1)} fusion(f32[8,512,2048]{2,1,0:T(8,128)} %get-tuple-element.297, f32[8,512,2048]{2,1,0:T(8,128)} %get-tuple-element.252, f32[8,512]{1,0:T(8,128)S(1)} %get-tuple-element.296, f32[8,512]{1,0:T(8,128)S(1)} %copy-done.224, pred[512,2048]{1,0:T(8,128)(4,1)} %pad_add_fusion.4), kind=kLoop, calls=%fused_computation.2 | loop fusion | flops 50331648 | bytes 84967424 | tf_op jit(solution)/shard_map/convert_element_type | solution.py:40
  1282.8 28.1 %multiply_convert_fusion = bf16[8,512,2048]{2,1,0:T(8,128)(2,1)} fusion(f32[8,512,2048]{2,1,0:T(8,128)} %get-tuple-element.295, f32[8,512,2048]{2,1,0:T(8,128)} %get-tuple-element.250, f32[8,512]{1,0:T(8,128)S(1)} %get-tuple-element.294, f32[8,512]{1,0:T(8,128)S(1)} %copy-done.221, pred[512,2048]{1,0:T(8,128)(4,1)S(1)} %copy-done.21), kind=kLoop, calls=%fused_computation | loop fusion | flops 50331648 | bytes 84967424 | tf_op jit(solution)/shard_map/convert_element_type | solution.py:40
  1335.4 25.5 multiply_reduce_fusion.2
  1361.0 25.6 multiply_reduce_fusion.3
  1386.6 28.4 %multiply_convert_fusion.3 = bf16[8,512,2048]{2,1,0:T(8,128)(2,1)} fusion(f32[8,512,2048]{2,1,0:T(8,128)} %get-tuple-element.301, f32[8,512,2048]{2,1,0:T(8,128)} %get-tuple-element.246, f32[8,512]{1,0:T(8,128)S(1)} %get-tuple-element.300, f32[8,512]{1,0:T(8,128)S(1)} %copy-done.211, pred[512,2048]{1,0:T(8,128)(4,1)} %pad_add_fusion.2), kind=kLoop, calls=%fused_computation.6 | loop fusion | flops 50331648 | bytes 84967424 | tf_op jit(solution)/shard_map/convert_element_type | solution.py:40
  1437.7 27.9 %multiply_convert_fusion.2 = bf16[8,512,2048]{2,1,0:T(8,128)(2,1)} fusion(f32[8,512,2048]{2,1,0:T(8,128)} %get-tuple-element.299, f32[8,512,2048]{2,1,0:T(8,128)} %get-tuple-element.244, f32[8,512]{1,0:T(8,128)S(1)} %get-tuple-element.298, f32[8,512]{1,0:T(8,128)S(1)} %copy-done.214, pred[512,2048]{1,0:T(8,128)(4,1)S(1)} %copy-done.14), kind=kLoop, calls=%fused_computation.4 | loop fusion | flops 50331648 | bytes 84967424 | tf_op jit(solution)/shard_map/convert_element_type | solution.py:40
  1601.0 82.6 %all-reduce.4 = f32[2048]{0:T(1024)S(1)} all-reduce(f32[2048]{0:T(1024)S(1)} %add_add_fusion.2), channel_id=8, replica_groups=mesh['dp'=32] {'dp'}, use_global_device_ids=true, to_apply=%region_84.85.clone | all-reduce | flops 2048 | bytes 16384
  1695.6 115.3 %reduce-scatter.22.cloned.1.call-done = f32[16,3]{1,0:T(8,128)} async-done(((f32[512,3]{1,0:T(8,128)}), f32[16,3]{1,0:T(8,128)}) %reduce-scatter.22.cloned.1.call-update) | async-done | bytes 208
  1812.2 130.2 %reduce-scatter.26.cloned.1.call-done = f32[16,3]{1,0:T(8,128)} async-done(((f32[512,3]{1,0:T(8,128)}), f32[16,3]{1,0:T(8,128)}) %reduce-scatter.26.cloned.1.call-update) | async-done | bytes 208
  1943.8 130.2 %reduce-scatter.28.cloned.1.call-done = f32[16,3]{1,0:T(8,128)} async-done(((f32[512,3]{1,0:T(8,128)}), f32[16,3]{1,0:T(8,128)}) %reduce-scatter.28.cloned.1.call-update) | async-done | bytes 208
  2092.9 139.6 %all-reduce.8.cloned.1.call-done = (f32[2,512,512]{2,0,1:T(2,128)}, f32[2,512,512]{2,0,1:T(2,128)}, f32[2,512,512]{2,0,1:T(2,128)}) async-done(((f32[2,512,512]{2,0,1:T(2,128)}, f32[2,512,512]{2,0,1:T(2,128)}, f32[2,512,512]{2,0,1:T(2,128)}), (f32[2,512,512]{2,0,1:T(2,128)}, f32[2,512,512]{2,0,1:T(2,128)}, f32[2,512,512]{2,0,1:T(2,128)})) %all-reduce.8.cloned.1.call-update) | async-done | bytes 6291472
  2237.0 134.7 %reduce-scatter.16.cloned.1.call-done = f32[2,16,512]{2,1,0:T(8,128)} async-done(((f32[2,512,512]{2,1,0:T(8,128)}), f32[2,16,512]{2,1,0:T(8,128)}) %reduce-scatter.16.cloned.1.call-update) | async-done | bytes 65552 | tf_op jit(solution)/shard_map/reduce_scatter | solution.py:463
  2371.7 139.7 %reduce-scatter.18.cloned.1.call-done = f32[16,2048]{1,0:T(8,128)} async-done(((f32[512,2048]{1,0:T(8,128)}), f32[16,2048]{1,0:T(8,128)}) %reduce-scatter.18.cloned.1.call-update) | async-done | bytes 131088 | tf_op jit(solution)/shard_map/reduce_scatter | solution.py:464
  2511.5 139.6 %reduce-scatter.20.cloned.1.call-done = f32[64,512]{1,0:T(8,128)} async-done(((f32[2048,512]{1,0:T(8,128)}), f32[64,512]{1,0:T(8,128)}) %reduce-scatter.20.cloned.1.call-update) | async-done | bytes 131088 | tf_op jit(solution)/shard_map/reduce_scatter | solution.py:465
  (1194 shorter events, 1134.7 us)
Async XLA Ops:
  7.2 219.0 %all-gather.15.cloned.1.call-start = ((), (), s32[]{:S(2)}) async-start(), calls=%async_computation.9 | async-start | bytes 1081344 | tf_op jit(solution)/shard_map/all_gather | solution.py:149
  7.9 230.6 %all-gather.11.cloned.1.call-start = ((), (), s32[]{:S(2)}) async-start(), calls=%async_computation.7 | async-start | bytes 1081344 | tf_op jit(solution)/shard_map/all_gather | solution.py:150
  8.7 255.3 %all-gather.13.cloned.1.call-start = ((), (), s32[]{:S(2)}) async-start(), calls=%async_computation.8 | async-start | bytes 1081344 | tf_op jit(solution)/shard_map/all_gather | solution.py:148
  9.4 416.7 %all-gather.17.cloned.1.call-start = ((), (), s32[]{:S(2)}) async-start(), calls=%async_computation.10 | async-start | bytes 1081344 | tf_op jit(solution)/shard_map/all_gather | solution.py:151
  10.0 645.6 %all-gather.19.cloned.1.call-start = ((), (), s32[]{:S(2)}) async-start(), calls=%async_computation.11 | async-start | bytes 2162688 | tf_op jit(solution)/shard_map/all_gather | solution.py:152
  10.6 652.8 %all-gather.21.cloned.1.call-start = ((), (), s32[]{:S(2)}) async-start(), calls=%async_computation.12 | async-start | bytes 2162688 | tf_op jit(solution)/shard_map/all_gather | solution.py:153
  11.1 1683.1 %reduce-scatter.24.cloned.1.call-start = ((), (), s32[]{:S(2)}) async-start(), calls=%async_computation.17 | async-start | bytes 270336
  230.0 41.5 %collective-permute-start.3 = (bf16[256,512]{1,0:T(8,128)(2,1)}, bf16[256,512]{1,0:T(8,128)(2,1)S(1)}, u32[]{:S(2)}, u32[]{:S(2)}) collective-permute-start(bf16[256,512]{1,0:T(8,128)(2,1)} %convolution_convert_fusion.34), channel_id=1, source_target_pairs={{0,1},{1,0},{2,3},{3,2},{4,5},{5,4},{6,7},{7,6},{8,9},{9,8},{10,11... | collective-permute-start | bytes 786440 | tf_op jit(solution)/shard_map/ppermute | solution.py:20
  234.1 39.1 %collective-permute-start.11 = (bf16[256,512]{1,0:T(8,128)(2,1)}, bf16[256,512]{1,0:T(8,128)(2,1)}, u32[]{:S(2)}, u32[]{:S(2)}) collective-permute-start(bf16[256,512]{1,0:T(8,128)(2,1)} %convolution_convert_fusion.30), channel_id=1, source_target_pairs={{0,1},{1,0},{2,3},{3,2},{4,5},{5,4},{6,7},{7,6},{8,9},{9,8},{10,11... | collective-permute-start | bytes 786440 | tf_op jit(solution)/shard_map/ppermute | solution.py:20
  238.3 35.0 %collective-permute-start.7 = (bf16[256,512]{1,0:T(8,128)(2,1)}, bf16[256,512]{1,0:T(8,128)(2,1)}, u32[]{:S(2)}, u32[]{:S(2)}) collective-permute-start(bf16[256,512]{1,0:T(8,128)(2,1)} %convolution_convert_fusion.32), channel_id=1, source_target_pairs={{0,1},{1,0},{2,3},{3,2},{4,5},{5,4},{6,7},{7,6},{8,9},{9,8},{10,11... | collective-permute-start | bytes 786440 | tf_op jit(solution)/shard_map/ppermute | solution.py:20
  251.4 36.0 %collective-permute-start.1 = (bf16[1024,512]{1,0:T(8,128)(2,1)}, bf16[1024,512]{1,0:T(8,128)(2,1)}, u32[]{:S(2)}, u32[]{:S(2)}) collective-permute-start(bf16[1024,512]{1,0:T(8,128)(2,1)} %convolution_convert_fusion.15), channel_id=1, source_target_pairs={{1,0},{2,1},{3,2},{4,3},{5,4},{6,5},{7,6},{8,7},{9,8},{10,9},{11,1... | collective-permute-start | bytes 3145736 | tf_op jit(solution)/shard_map/ppermute | solution.py:16
  255.6 37.2 %collective-permute-start.9 = (bf16[1024,512]{1,0:T(8,128)(2,1)}, bf16[1024,512]{1,0:T(8,128)(2,1)}, u32[]{:S(2)}, u32[]{:S(2)}) collective-permute-start(bf16[1024,512]{1,0:T(8,128)(2,1)} %convolution_convert_fusion.7), channel_id=1, source_target_pairs={{1,0},{2,1},{3,2},{4,3},{5,4},{6,5},{7,6},{8,7},{9,8},{10,9},{11,1... | collective-permute-start | bytes 3145736 | tf_op jit(solution)/shard_map/ppermute | solution.py:16
  276.8 26.2 collective-permute-start
  285.3 25.4 collective-permute-start.8
  287.4 30.2 %collective-permute-start.4 = (bf16[1024,512]{1,0:T(8,128)(2,1)}, bf16[1024,512]{1,0:T(8,128)(2,1)}, u32[]{:S(2)}, u32[]{:S(2)}) collective-permute-start(bf16[1024,512]{1,0:T(8,128)(2,1)} %convolution_convert_fusion.13), channel_id=1, source_target_pairs={{1,0},{2,1},{3,2},{4,3},{5,4},{6,5},{7,6},{8,7},{9,8},{10,9},{11,1... | collective-permute-start | bytes 3145736 | tf_op jit(solution)/shard_map/ppermute | solution.py:16
  1496.2 26.3 collective-permute-start.22
  1496.3 30.5 %collective-permute-start.18 = (bf16[256,512]{0,1:T(8,128)(2,1)}, bf16[256,512]{0,1:T(8,128)(2,1)}, u32[]{:S(2)}, u32[]{:S(2)}) collective-permute-start(bf16[256,512]{0,1:T(8,128)(2,1)} %bitcast.169), channel_id=1, source_target_pairs={{0,1},{1,0},{2,3},{3,2},{4,5},{5,4},{6,7},{7,6},{8,9},{9,8},{10,11... | collective-permute-start | bytes 786440 | tf_op jit(solution)/shard_map/ppermute | solution.py:20
  1497.7 313.1 %reduce-scatter.22.cloned.1.call-start = ((), (), s32[]{:S(2)}) async-start(), calls=%async_computation.16 | async-start | bytes 270336
  1498.8 443.6 %reduce-scatter.26.cloned.1.call-start = ((), (), s32[]{:S(2)}) async-start(), calls=%async_computation.18 | async-start | bytes 270336
  1499.9 574.1 %reduce-scatter.28.cloned.1.call-start = ((), (), s32[]{:S(2)}) async-start(), calls=%async_computation.19 | async-start | bytes 270336
  1511.6 721.0 %all-reduce.8.cloned.1.call-start = ((), (), s32[]{:S(2)}) async-start(), calls=%async_computation.20 | async-start | bytes 12582912
  1556.5 815.3 %reduce-scatter.16.cloned.1.call-start = ((), (), s32[]{:S(2)}) async-start(), calls=%async_computation.13 | async-start | bytes 2162688 | tf_op jit(solution)/shard_map/reduce_scatter | solution.py:463
  1566.9 944.5 %reduce-scatter.18.cloned.1.call-start = ((), (), s32[]{:S(2)}) async-start(), calls=%async_computation.14 | async-start | bytes 4325376 | tf_op jit(solution)/shard_map/reduce_scatter | solution.py:464
  1579.6 1071.5 %reduce-scatter.20.cloned.1.call-start = ((), (), s32[]{:S(2)}) async-start(), calls=%async_computation.15 | async-start | bytes 4325376 | tf_op jit(solution)/shard_map/reduce_scatter | solution.py:465
  (371 other events, 4609.7 us)
Sparse Core Ops, SparseCore 0:
  10.9 56.2 all-gather.14
  70.2 52.5 all-gather.10
  125.7 52.6 all-gather.12
  181.1 52.5 all-gather.16
  236.5 120.1 all-gather.18
  359.4 55.1 all-gather.20
  1497.9 181.2 reduce-scatter.23
  1681.5 129.3 reduce-scatter.21
  1813.1 129.3 reduce-scatter.25
  1944.6 129.3 reduce-scatter.27
  2079.9 152.5 all-reduce.7
  2235.4 136.3 reduce-scatter.15
  2374.6 136.8 reduce-scatter.17
  2514.2 136.8 reduce-scatter.19
where the time goes:
time: 2660 us
  waiting for transfers between devices  933 us (35%)
  matrix products  879 us (33%)
  other arithmetic  402 us (15%)
  blocking collectives  277 us (10%)
  local copies, waits for them, and re-layouts  109 us (4%)
  starting transfers between devices  37.5 us (1%)
    unnamed x19, waiting for transfers between devices  519 us
    convert_element_type x26, other arithmetic, to_low(): return values.astype(jnp.bfloat16)  219 us
    dot_general x12, matrix products, attend_backward(): jnp.einsum('qhd,khd->hqk', grad_blk, heads_v, preferred_element_type=jnp....  184 us
    reduce_scatter x1, waiting for transfers between devices, body(): lax.psum_scatter(grad_total[4], 'dp', scatter_dimension=0, tiled=True)  140 us
    reduce_scatter x1, waiting for transfers between devices, body(): lax.psum_scatter(grad_total[5], 'dp', scatter_dimension=0, tiled=True)  140 us
    reduce_scatter x1, waiting for transfers between devices, body(): lax.psum_scatter(grad_total[3], 'dp', scatter_dimension=1, tiled=True)  135 us
    dot_general x12, matrix products, attend_backward(): jnp.einsum('hqk,qhd->khd', to_low(prob_rows), grad_blk, preferred_element...  125 us
    unnamed x2, blocking collectives  125 us
  transfers between devices with their start and end apart: 38, of which 7 were waited for; matrix products, arithmetic and copies ran while one was open for 21% of the time, Pallas kernels for 0%

commit v1 on v0

v1 whole, which is shorter than its diff:
```python
import functools

import jax
import jax.numpy as jnp
from jax import lax
from jax.experimental import pallas as pl
from jax.experimental.pallas import tpu as pltpu
from jax.sharding import PartitionSpec as P

HEADS = 8
EPS = 1e-05
NEG = -1e30
LANES = 128
VMEM_LIMIT = 56 << 20


def nn(left, right):
    return lax.dot_general(
        left, right, (((1,), (0,)), ((), ())), preferred_element_type=jnp.float32
    )


def nt(left, right):
    return lax.dot_general(
        left, right, (((1,), (1,)), ((), ())), preferred_element_type=jnp.float32
    )


def tn(left, right):
    return lax.dot_general(
        left, right, (((0,), (0,)), ((), ())), preferred_element_type=jnp.float32
    )


def low(values):
    return values.astype(jnp.bfloat16)


def wide(values):
    return values.astype(jnp.float32)


def bit_count(axis):
    return (lax.axis_size(axis) - 1).bit_length()


def from_partner(x, axis, bit):
    return lax.ppermute(x, axis, [(i, i ^ 1 << bit) for i in range(lax.axis_size(axis))])


def prompt_to_continuation(x, axis):
    return lax.ppermute(x, axis, [(i + 1, i) for i in range(0, lax.axis_size(axis), 2)])


def continuation_to_prompt(x, axis):
    return lax.ppermute(x, axis, [(i, i + 1) for i in range(0, lax.axis_size(axis), 2)])


def tree_gather(x, axis):
    bits = bit_count(axis)
    me = lax.axis_index(axis)
    block = x.reshape((1,) * bits + x.shape)
    for bit in list(range(bits - 1, 0, -1)) + [0]:
        dim = bits - 1 - bit
        got = from_partner(block, axis, bit)
        block = jnp.where(
            (me >> bit) & 1 == 1,
            jnp.concatenate([got, block], dim),
            jnp.concatenate([block, got], dim),
        )
    return block.reshape((-1,) + x.shape[1:])


def tree_scatter(arrays, axis):
    bits = bit_count(axis)
    me = lax.axis_index(axis)
    size = lax.axis_size(axis)
    plain = list(range(bits))
    turned = plain[:1] + plain[1:3][::-1] + plain[3:]
    blocks = [
        a.reshape((2,) * bits + (a.shape[0] // size,) + a.shape[1:]) for a in arrays
    ]
    for step in range(bits):
        fresh = []
        for number, block in enumerate(blocks):
            bit = (plain, turned)[number % 2][step]
            dim = bits - 1 - bit
            first = lax.index_in_dim(block, 0, dim, keepdims=True)
            second = lax.index_in_dim(block, 1, dim, keepdims=True)
            upper = (me >> bit) & 1 == 1
            got = from_partner(low(jnp.where(upper, first, second)), axis, bit)
            fresh.append(jnp.where(upper, second, first) + wide(got))
        blocks = fresh
    return [b.reshape((a.shape[0] // size,) + a.shape[1:]) for a, b in zip(arrays, blocks)]


def self_forward_kernel(
    tq, tk, pairs, tiles, q_ref, kp_ref, vp_ref, kl_ref, vl_ref, lim_ref, o_ref, lse_ref, s_ref
):
    micro, tile = pl.program_id(0), pl.program_id(1)
    prefix_tiles = tiles[micro, tile, 0]
    local_first, local_end = tiles[micro, tile, 1], tiles[micro, tile, 2]
    reach, start = lim_ref[0, :, 0:1], lim_ref[0, :, 1:2]
    rows = tile * tq + lax.broadcasted_iota(jnp.int32, (tq, 1), 0)
    lane = lax.broadcasted_iota(jnp.int32, (tq, LANES), 1)
    column = lax.broadcasted_iota(jnp.int32, (tq, tk), 1)
    lse_all = jnp.zeros((tq, LANES), jnp.float32)
    heads = 2 * pairs
    prefix_rows = kp_ref.shape[1]
    half = LANES // 2
    total_pairs = q_ref.shape[2] // LANES

    def prefix_mask(j):
        return column < reach - j * tk

    def local_mask(j):
        return (column <= rows - j * tk) & (column >= start - j * tk)

    for group in range(total_pairs // pairs):
        queries = []
        for h in range(heads):
            p = group * pairs + h // 2
            q = q_ref[0, :, p * LANES : (p + 1) * LANES] * jnp.bfloat16(0.125)
            queries.append(jnp.where((lane >= half) == (h % 2 == 1), q, jnp.bfloat16(0)))

        def score(k_ref, offset, masker, j, tops):
            base = pl.multiple_of(j * tk, tk)
            seen = masker(j)
            out = []
            for h in range(heads):
                p = group * pairs + h // 2
                s = nt(queries[h], k_ref[0, pl.ds(base, tk), p * LANES : (p + 1) * LANES])
                s = jnp.where(seen, s, NEG)
                s_ref[h, :, pl.ds(pl.multiple_of(offset + base, tk), tk)] = s
                top = tops[h]
                for c in range(tk // LANES):
                    top = jnp.maximum(top, s[:, c * LANES : (c + 1) * LANES])
                out.append(top)
            return tuple(out)

        tops = tuple(jnp.full((tq, LANES), NEG, jnp.float32) for _ in range(heads))
        tops = lax.fori_loop(
            0, prefix_tiles, functools.partial(score, kp_ref, 0, prefix_mask), tops
        )
        tops = lax.fori_loop(
            local_first,
            local_end,
            functools.partial(score, kl_ref, prefix_rows, local_mask),
            tops,
        )
        tops = [jnp.max(t, axis=1, keepdims=True) for t in tops]

        def mix(v_ref, offset, j, carry):
            base = pl.multiple_of(j * tk, tk)
            out = []
            for h in range(heads):
                p = group * pairs + h // 2
                e = jnp.exp(
                    s_ref[h, :, pl.ds(pl.multiple_of(offset + base, tk), tk)] - tops[h]
                )
                total, mixed = carry[2 * h], carry[2 * h + 1]
                for c in range(tk // LANES):
                    total = total + e[:, c * LANES : (c + 1) * LANES]
                mixed = mixed + nn(
                    low(e), v_ref[0, pl.ds(base, tk), p * LANES : (p + 1) * LANES]
                )
                out += [total, mixed]
            return tuple(out)

        carry = tuple(jnp.zeros((tq, LANES), jnp.float32) for _ in range(2 * heads))
        carry = lax.fori_loop(0, prefix_tiles, functools.partial(mix, vp_ref, 0), carry)
        carry = lax.fori_loop(
            local_first, local_end, functools.partial(mix, vl_ref, prefix_rows), carry
        )
        for k in range(pairs):
            p = group * pairs + k
            outs = []
            for h in (2 * k, 2 * k + 1):
                total = jnp.sum(carry[2 * h], axis=1, keepdims=True)
                outs.append(carry[2 * h + 1] / total)
                lse_all = jnp.where(lane == 2 * p + h % 2, tops[h] + jnp.log(total), lse_all)
            o_ref[0, :, p * LANES : (p + 1) * LANES] = jnp.where(lane < half, outs[0], outs[1])
    lse_ref[0] = jnp.transpose(lse_all)[0 : lse_ref.shape[1], :]


def self_forward(qkv, far_kv, limits, tiles, tq=256, tk=256, pairs=4):
    micro, rows, width = qkv.shape
    width = width // 3
    whole = (1, rows, width)
    return pl.pallas_call(
        functools.partial(self_forward_kernel, tq, tk, pairs),
        out_shape=(
            jax.ShapeDtypeStruct((micro, rows, width), jnp.float32),
            jax.ShapeDtypeStruct((micro, HEADS, rows), jnp.float32),
        ),
        grid_spec=pltpu.PrefetchScalarGridSpec(
            num_scalar_prefetch=1,
            grid=(micro, rows // tq),
            in_specs=[
                pl.BlockSpec((1, tq, width), lambda m, i, s: (m, i, 0)),
                pl.BlockSpec(whole, lambda m, i, s: (m, 0, 0)),
                pl.BlockSpec(whole, lambda m, i, s: (m, 0, 1)),
                pl.BlockSpec(whole, lambda m, i, s: (m, 0, 1)),
                pl.BlockSpec(whole, lambda m, i, s: (m, 0, 2)),
                pl.BlockSpec((1, tq, 2), lambda m, i, s: (m, i, 0)),
            ],
            out_specs=[
                pl.BlockSpec((1, tq, width), lambda m, i, s: (m, i, 0)),
                pl.BlockSpec((1, HEADS, tq), lambda m, i, s: (m, 0, i)),
            ],
            scratch_shapes=[pltpu.VMEM((2 * pairs, tq, 2 * rows), jnp.float32)],
        ),
        compiler_params=pltpu.CompilerParams(vmem_limit_bytes=VMEM_LIMIT),
        name="self_forward",
    )(tiles, qkv, far_kv, far_kv, qkv, qkv, limits)


def self_backward_kernel(
    tq,
    tk,
    pairs,
    tiles,
    q_ref,
    kp_ref,
    vp_ref,
    kl_ref,
    vl_ref,
    do_ref,
    of_ref,
    lse_ref,
    lim_ref,
    dq_ref,
    dkp_ref,
    dvp_ref,
    dkl_ref,
    dvl_ref,
    sum_kp,
    sum_vp,
    sum_kl,
    sum_vl,
):
    micro = pl.program_id(0)
    row_count = q_ref.shape[1]
    half = LANES // 2
    for ref in (sum_kp, sum_vp, sum_kl, sum_vl):
        ref[...] = jnp.zeros_like(ref)
    lane = lax.broadcasted_iota(jnp.int32, (tq, LANES), 1)
    key_at = lax.broadcasted_iota(jnp.int32, (tk, tq), 0)
    pick_lane = lax.broadcasted_iota(jnp.int32, (8, LANES), 1)
    pick_row = lax.broadcasted_iota(jnp.int32, (8, LANES), 0)
    pick = wide(pick_lane // half == pick_row)
    for i in range(row_count // tq):
        here = slice(i * tq, (i + 1) * tq)
        prefix_tiles = tiles[micro, i, 0]
        local_first, local_end = tiles[micro, i, 1], tiles[micro, i, 2]
        reach, start = lim_ref[0, 0:1, here], lim_ref[0, 1:2, here]
        rows = i * tq + lax.broadcasted_iota(jnp.int32, (1, tq), 1)
        queries, grads, totals, deltas = [], [], [], []
        for k in range(pairs):
            cols = slice(k * LANES, (k + 1) * LANES)
            q = q_ref[0, here, cols] * jnp.bfloat16(0.125)
            do = do_ref[0, here, cols]
            sums = lax.dot_general(
                pick,
                wide(do) * of_ref[0, here, cols],
                (((1,), (1,)), ((), ())),
                preferred_element_type=jnp.float32,
                precision=lax.Precision.HIGHEST,
            )
            for h in range(2):
                mine = (lane >= half) == (h == 1)
                queries.append(jnp.where(mine, q, jnp.bfloat16(0)))
                grads.append(jnp.where(mine, do, jnp.bfloat16(0)))
                totals.append(lse_ref[0, 0, 2 * k + h : 2 * k + h + 1, here])
                deltas.append(sums[h : h + 1, :])

        def body(k_ref, v_ref, sum_k, sum_v, masker, j, dq):
            base = pl.multiple_of(j * tk, tk)
            seen = masker(j)
            out = []
            for k in range(pairs):
                cols = slice(k * LANES, (k + 1) * LANES)
                keys = k_ref[0, pl.ds(base, tk), cols]
                values = v_ref[0, pl.ds(base, tk), cols]
                dv, dk = 0.0, 0.0
                for h in (2 * k, 2 * k + 1):
                    s = jnp.where(seen, nt(keys, queries[h]), NEG)
                    p = jnp.exp(s - totals[h])
                    dp = nt(values, grads[h])
                    dv = dv + nn(low(p), grads[h])
                    ds = low(p * (dp - deltas[h]))
                    dk = dk + nn(ds, queries[h])
                    out.append(dq[h] + tn(ds, keys))
                sum_v[pl.ds(base, tk), cols] += dv
                sum_k[pl.ds(base, tk), cols] += dk
            return tuple(out)

        def prefix_mask(j):
            return key_at < reach - j * tk

        def local_mask(j):
            return (key_at <= rows - j * tk) & (key_at >= start - j * tk)

        dq = tuple(jnp.zeros((tq, LANES), jnp.float32) for _ in range(2 * pairs))
        dq = lax.fori_loop(
            0,
            prefix_tiles,
            functools.partial(body, kp_ref, vp_ref, sum_kp, sum_vp, prefix_mask),
            dq,
        )
        dq = lax.fori_loop(
            local_first,
            local_end,
            functools.partial(body, kl_ref, vl_ref, sum_kl, sum_vl, local_mask),
            dq,
        )
        for k in range(pairs):
            cols = slice(k * LANES, (k + 1) * LANES)
            dq_ref[0, here, cols] = low(jnp.where(lane < half, dq[2 * k], dq[2 * k + 1]) * 0.125)
    dkp_ref[0] = low(sum_kp[...])
    dvp_ref[0] = low(sum_vp[...])
    dkl_ref[0] = sum_kl[...]
    dvl_ref[0] = sum_vl[...]


def self_backward(qkv, far_kv, grad_out, out, lse, limits, tiles, tq=256, tk=256, pairs=2):
    micro, rows, width = qkv.shape
    width = width // 3
    cols = LANES * pairs
    parts = width // cols
    block = (1, rows, cols)
    f32 = jax.ShapeDtypeStruct((micro, rows, width), jnp.float32)
    bf16 = jax.ShapeDtypeStruct((micro, rows, width), jnp.bfloat16)
    return pl.pallas_call(
        functools.partial(self_backward_kernel, tq, tk, pairs),
        out_shape=(bf16, bf16, bf16, f32, f32),
        grid_spec=pltpu.PrefetchScalarGridSpec(
            num_scalar_prefetch=1,
            grid=(micro, parts),
            in_specs=[
                pl.BlockSpec(block, lambda m, i, s: (m, 0, i)),
                pl.BlockSpec(block, lambda m, i, s: (m, 0, i)),
                pl.BlockSpec(block, lambda m, i, s: (m, 0, parts + i)),
                pl.BlockSpec(block, lambda m, i, s: (m, 0, parts + i)),
                pl.BlockSpec(block, lambda m, i, s: (m, 0, 2 * parts + i)),
                pl.BlockSpec(block, lambda m, i, s: (m, 0, i)),
                pl.BlockSpec(block, lambda m, i, s: (m, 0, i)),
                pl.BlockSpec((1, 1, 2 * pairs, rows), lambda m, i, s: (m, i, 0, 0)),
                pl.BlockSpec((1, 2, rows), lambda m, i, s: (m, 0, 0)),
            ],
            out_specs=[pl.BlockSpec(block, lambda m, i, s: (m, 0, i))] * 5,
            scratch_shapes=[pltpu.VMEM((rows, cols), jnp.float32)] * 4,
        ),
        compiler_params=pltpu.CompilerParams(vmem_limit_bytes=VMEM_LIMIT),
        name="self_backward",
    )(
        tiles,
        qkv,
        far_kv,
        far_kv,
        qkv,
        qkv,
        grad_out,
        out,
        lse.reshape(micro, parts, 2 * pairs, rows),
        limits,
    )


def mask_limits(seg, off, is_prompt, tq=256, tk=256):
    micro, rows = seg.shape
    index = jnp.arange(off.shape[1], dtype=jnp.int32)
    own = seg[:, :, None] == index
    count = jnp.sum(own.astype(jnp.int32), axis=1)
    before = jnp.sum(jnp.where(index[:, None] > index[None, :], count[:, None, :], 0), axis=2)
    reach = jnp.sum(jnp.where(own, off[:, None, :], 0), axis=2)
    start = jnp.sum(jnp.where(own, before[:, None, :], 0), axis=2)
    reach = jnp.where(is_prompt, 0, reach)
    start = jnp.where(is_prompt, 0, start)
    tile_count = rows // tq
    most = jnp.max(reach.reshape(micro, tile_count, tq), axis=2)
    least = jnp.min(start.reshape(micro, tile_count, tq), axis=2)
    end = (jnp.arange(tile_count, dtype=jnp.int32) + 1) * tq
    tiles = jnp.stack(
        [
            (most + tk - 1) // tk,
            least // tk,
            jnp.broadcast_to((end + tk - 1) // tk, (micro, tile_count)),
        ],
        axis=2,
    )
    return jnp.stack([reach, start], axis=1), tiles


def smooth_gate(values):
    return jax.nn.gelu(values, approximate=True)


def norm_forward(values, gain, shift):
    mean = jnp.mean(values, axis=-1, keepdims=True)
    centred = values - mean
    inv = lax.rsqrt(jnp.mean(centred * centred, axis=-1, keepdims=True) + EPS)
    normed = centred * inv
    return normed * gain + shift, normed, inv


def norm_backward(grad, normed, inv, gain):
    scaled = grad * gain
    centred = scaled - jnp.mean(scaled, axis=-1, keepdims=True)
    grad_z = inv * (centred - normed * jnp.mean(scaled * normed, axis=-1, keepdims=True))
    rows = tuple(range(grad.ndim - 1))
    return grad_z, jnp.sum(grad * normed, axis=rows), jnp.sum(grad, axis=rows)


def heads_of(values):
    return values.reshape(values.shape[:-1] + (HEADS, values.shape[-1] // HEADS))


def total_tn(left, right):
    return tn(left.reshape(-1, left.shape[-1]), right.reshape(-1, right.shape[-1]))


def flat_nn(left, right):
    return nn(left.reshape(-1, left.shape[-1]), right).reshape(left.shape[:-1] + (right.shape[1],))


def flat_nt(left, right):
    return nt(left.reshape(-1, left.shape[-1]), right).reshape(left.shape[:-1] + (right.shape[0],))


def all_rows(values):
    return jnp.sum(wide(values), axis=(0, 1))


def middle(x, self_out, mem_kv, cot, weights):
    w_o0, w_q1, w_o1, w_in, w_out, ffn_bias, out_bias, omega, gain, shift = weights
    width = x.shape[-1]
    scale = (width // HEADS) ** -0.5
    rows = wide(x)
    self_low = low(self_out)
    h1, n1, i1 = norm_forward(
        rows * omega[0] + (flat_nn(self_low, w_o0) + out_bias[0]), gain[0], shift[0]
    )
    h1 = low(h1)
    cross_q = low(flat_nn(h1, w_q1))
    mem_k, mem_v = heads_of(mem_kv[..., :width]), heads_of(mem_kv[..., width:])
    scores = (
        jnp.einsum(
            "mqhd,mkhd->mhqk", heads_of(cross_q), mem_k, preferred_element_type=jnp.float32
        )
        * scale
    )
    prob = jax.nn.softmax(scores, axis=-1)
    cross = low(
        jnp.einsum("mhqk,mkhd->mqhd", low(prob), mem_v, preferred_element_type=jnp.float32)
    ).reshape(x.shape)
    h2, n2, i2 = norm_forward(
        wide(h1) * omega[1] + (flat_nn(cross, w_o1) + out_bias[1]), gain[1], shift[1]
    )
    h2 = low(h2)
    pre = flat_nn(h2, w_in) + ffn_bias
    act = low(smooth_gate(pre))
    final, n3, i3 = norm_forward(
        wide(h2) * omega[2] + (flat_nn(act, w_out) + out_bias[2]), gain[2], shift[2]
    )
    top = wide(cot)
    dz3, g_gain3, g_shift3 = norm_backward(top, n3, i3, gain[2])
    g_om3 = jnp.sum(dz3 * wide(h2), axis=(0, 1))
    df = low(dz3)
    dact = low(flat_nt(df, w_out))
    dpre = low(jax.vjp(smooth_gate, pre)[1](wide(dact))[0])
    dh2 = flat_nt(dpre, w_in) + dz3 * omega[2]
    dz2, g_gain2, g_shift2 = norm_backward(dh2, n2, i2, gain[1])
    g_om2 = jnp.sum(dz2 * wide(h1), axis=(0, 1))
    dc = low(dz2)
    dco = heads_of(low(flat_nt(dc, w_o1)))
    dprob = jnp.einsum("mqhd,mkhd->mhqk", dco, mem_v, preferred_element_type=jnp.float32)
    ds = low(prob * (dprob - jnp.sum(dprob * prob, axis=-1, keepdims=True)))
    dcq = low(
        jnp.einsum("mhqk,mkhd->mqhd", ds, mem_k, preferred_element_type=jnp.float32) * scale
    ).reshape(x.shape)
    dmk = (
        jnp.einsum(
            "mhqk,mqhd->mkhd", ds, heads_of(cross_q), preferred_element_type=jnp.float32
        )
        * scale
    ).reshape(mem_kv.shape[:2] + (width,))
    dmv = jnp.einsum(
        "mhqk,mqhd->mkhd", low(prob), dco, preferred_element_type=jnp.float32
    ).reshape(mem_kv.shape[:2] + (width,))
    dh1 = flat_nt(dcq, w_q1) + dz2 * omega[1]
    dz1, g_gain1, g_shift1 = norm_backward(dh1, n1, i1, gain[0])
    g_om1 = jnp.sum(dz1 * rows, axis=(0, 1))
    da = low(dz1)
    dso = low(flat_nt(da, w_o0))
    products = (
        total_tn(self_low, da),
        total_tn(h1, dcq),
        total_tn(cross, dc),
        total_tn(h2, dpre),
        total_tn(act, df),
    )
    small = (
        all_rows(dpre),
        jnp.stack([all_rows(da), all_rows(dc), all_rows(df)]),
        jnp.stack([g_om1, g_om2, g_om3]),
        jnp.stack([g_gain1, g_gain2, g_gain3]),
        jnp.stack([g_shift1, g_shift2, g_shift3]),
    )
    return low(final), dso, dz1 * omega[0], dmk, dmv, products, small


def body(
    layer_in,
    memory,
    seg_ids,
    offsets,
    cotangent,
    attn_q,
    attn_k,
    attn_v,
    attn_o,
    w_in,
    w_out,
    ffn_bias,
    out_bias,
    omega,
    ln_gain,
    ln_bias,
):
    axis = "dp"
    is_prompt = lax.axis_index(axis) % 2 == 1
    own_rows = attn_q.shape[1]
    width = attn_q.shape[2]
    hidden = w_in.shape[1]
    mem_rows = memory.shape[1]

    first = tree_gather(jnp.concatenate([attn_q[0], attn_k[0], attn_v[0]], axis=1), axis)
    far_x = prompt_to_continuation(layer_in, axis)
    mem_all = jnp.concatenate([memory, from_partner(memory, axis, 0)], axis=1)
    small = jnp.concatenate(
        [out_bias.T, omega.T, ln_gain.T, ln_bias.T, ffn_bias.reshape(own_rows, -1)], axis=1
    )
    small_cols = small.shape[1]
    rest = lax.all_gather(
        jnp.concatenate(
            [
                attn_o[0],
                attn_q[1],
                attn_o[1],
                attn_k[1],
                attn_v[1],
                w_in,
                w_out.reshape(own_rows, -1),
                jnp.pad(small, ((0, 0), (0, LANES - small_cols))),
            ],
            axis=1,
        ),
        axis,
        axis=0,
        tiled=True,
    )
    w_o0, w_q1, w_o1 = (rest[:, k * width : (k + 1) * width] for k in range(3))
    w_mem = rest[:, 3 * width : 5 * width]
    all_in = rest[:, 5 * width : 5 * width + hidden]
    all_out = rest[:, 5 * width + hidden : 5 * width + 2 * hidden].reshape(hidden, width)
    small = wide(rest[:, 5 * width + 2 * hidden :][:, :small_cols])
    biases, omegas, gains, shifts = (small[:, 3 * k : 3 * k + 3].T for k in range(4))
    all_ffn_bias = small[:, 12:].reshape(hidden)

    limits, tiles = mask_limits(seg_ids[:, 0], offsets[:, 0], is_prompt)
    qkv = low(flat_nn(layer_in, first))
    far_kv = low(flat_nn(far_x, first[:, width:]))
    self_out, lse = self_forward(qkv, far_kv, jnp.swapaxes(limits, 1, 2), tiles)
    mem_kv = low(flat_nn(mem_all, w_mem))
    final, dso, skip, dmk, dmv, products, small_sums = middle(
        layer_in,
        self_out,
        mem_kv,
        cotangent,
        (w_o0, w_q1, w_o1, all_in, all_out, all_ffn_bias, biases, omegas, gains, shifts),
    )
    got_dk = from_partner(low(dmk[:, mem_rows:]), axis, 0)
    got_dv = from_partner(low(dmv[:, mem_rows:]), axis, 0)
    mem_dk = low(dmk[:, :mem_rows] + wide(got_dk))
    mem_dv = low(dmv[:, :mem_rows] + wide(got_dv))
    memory_grad = low(
        flat_nt(mem_dk, w_mem[:, :width]) + flat_nt(mem_dv, w_mem[:, width:])
    )
    g_ffn, g_out, g_om, g_gain, g_shift = small_sums
    small_grad = jnp.concatenate(
        [g_out.T, g_om.T, g_gain.T, g_shift.T, g_ffn.reshape(width, -1)], axis=1
    )
    ready = tree_scatter(
        [
            products[4],
            products[3],
            products[0],
            products[1],
            products[2],
            total_tn(memory, mem_dk),
            total_tn(memory, mem_dv),
            small_grad,
        ],
        axis,
    )
    s_out, s_in, s_o0, s_q1, s_o1, s_k1, s_v1, s_small = ready

    dq, far_dk, far_dv, own_dk, own_dv = self_backward(
        qkv, far_kv, dso, self_out, lse, limits, tiles
    )
    dk = low(own_dk + wide(continuation_to_prompt(far_dk, axis)))
    dv = low(own_dv + wide(continuation_to_prompt(far_dv, axis)))
    s_q0, s_k0, s_v0 = tree_scatter(
        [total_tn(layer_in, dq), total_tn(layer_in, dk), total_tn(layer_in, dv)], axis
    )
    input_grad = low(
        flat_nt(dq, first[:, :width])
        + flat_nt(dk, first[:, width : 2 * width])
        + flat_nt(dv, first[:, 2 * width :])
        + skip
    )
    return (
        final,
        input_grad,
        memory_grad,
        jnp.stack([s_q0, s_q1]),
        jnp.stack([s_k0, s_k1]),
        jnp.stack([s_v0, s_v1]),
        jnp.stack([s_o0, s_o1]),
        s_in,
        s_out,
        s_small[:, 12:].reshape(-1),
        s_small[:, 0:3].T,
        s_small[:, 3:6].T,
        s_small[:, 6:9].T,
        s_small[:, 9:12].T,
    )


def solution(mesh):
    rows = P(None, "dp", None)
    small = P(None, "dp")
    return jax.shard_map(
        body,
        mesh=mesh,
        in_specs=(rows,) * 9 + (P("dp", None), P("dp", None), P("dp"), small, small, small, small),
        out_specs=(rows,) * 7 + (P("dp", None), P("dp", None), P("dp"), small, small, small, small),
        check_vma=False,
    )
```

time: 2660 us -> 1100 us (0.41)
  waiting for transfers between devices: 933 us -> 142 us
  matrix products: 879 us -> 305 us
  other arithmetic: 402 us -> 103 us
  Pallas kernels: 0 us -> 278 us
  blocking collectives: 277 us -> 0 us
  starting transfers between devices: 37.5 us -> 105 us
  local copies, waits for them, and re-layouts: 109 us -> 143 us
    dot_general x162 -> x33, matrix products: 879 us -> 282 us  [the longest x10 80.4 us: nt(): lax.dot_general(left, right, (((1,), (1,)), ((), ())), preferred_element_...]
    unnamed x19 -> x1, waiting for transfers between devices: 519 us -> 0.02 us
    reduce_scatter x3 -> x0, waiting for transfers between devices: 414 us -> none  [the longest x1 140 us: body(): lax.psum_scatter(grad_total[4], 'dp', scatter_dimension=0, tiled=True)]
    pallas_call x0 -> x2, Pallas kernels: none -> 278 us  [the longest x1 173 us: self_backward(): pl.pallas_call(functools.partial(self_backward_kernel, tq, tk, pairs), ou...]
    convert_element_type x33 -> x60, other arithmetic: 224 us -> 55.7 us  [the longest x59 54.8 us: low(): return values.astype(jnp.bfloat16)]
    all_gather x4 -> x0, blocking collectives: 153 us -> none  [the longest x1 40.6 us: fetch_forward(): lax.all_gather(shards[7], 'dp', axis=1, tiled=True)]
    ppermute x12 -> x63, waiting for transfers between devices: 0.03 us -> 142 us  [from_partner(): lax.ppermute(x, axis, [(i, i ^ 1 << bit) for i in range(lax.axis_size(axi...]
    unnamed x2 -> x0, blocking collectives: 125 us -> none
  transfers between devices with their start and end apart: 38 -> 67, of which waited for: 7 -> 42; matrix products, arithmetic and copies ran while one was open for 21% -> 19% of each run, Pallas kernels for 0% -> 25%
where the time goes in v1:
time: 1100 us; the launch traced here: 1090 us
  matrix products  305 us (28%)
  Pallas kernels  278 us (25%)
  local copies, waits for them, and re-layouts  143 us (13%)
  waiting for transfers between devices  142 us (13%)
  starting transfers between devices  105 us (10%)
  other arithmetic  103 us (9%)
  between operations  16.5 us (2%)
    pallas_call x1, Pallas kernels, self_backward(): pl.pallas_call(functools.partial(self_backward_kernel, tq, tk, pairs), ou...  173 us
    ppermute x63, waiting for transfers between devices, from_partner(): lax.ppermute(x, axis, [(i, i ^ 1 << bit) for i in range(lax.axis_size(axi...  142 us
    pallas_call x1, Pallas kernels, self_forward(): pl.pallas_call(functools.partial(self_forward_kernel, tq, tk, pairs), out...  105 us
    ppermute x63, starting transfers between devices, from_partner(): lax.ppermute(x, axis, [(i, i ^ 1 << bit) for i in range(lax.axis_size(axi...  101 us
    dot_general x10, matrix products, nt(): lax.dot_general(left, right, (((1,), (1,)), ((), ())), preferred_element_...  80.4 us
    dot_general x8, matrix products, nn(): lax.dot_general(left, right, (((1,), (0,)), ((), ())), preferred_element_...  66.1 us
    convert_element_type x59, other arithmetic, low(): return values.astype(jnp.bfloat16)  54.8 us
    unnamed x200, local copies, waits for them, and re-layouts  37.4 us
  transfers between devices with their start and end apart: 67, of which 42 were waited for; matrix products, arithmetic and copies ran while one was open for 19% of the time, Pallas kernels for 25%

profile of v1, /device:TPU:0, one launch (start us, length us, event | category | flops | bytes accessed | tf_op | source)
XLA Modules:
  0.0 1092.8 jit_solution(17568806483584393046)
XLA Ops:
  40.3 12.5 %collective-permute-done.3 = bf16[2,2,2,1,1,16,1536]{6,5,0,1,2,4,3:T(8,128)(2,1)S(1)} collective-permute-done((bf16[2,2,2,1,1,16,1536]{6,5,0,1,2,4,3:T(8,128)(2,1)S(1)}, bf16[2,2,2,1,1,16,1536]{6,5,0,1,2,4,3:T(8,128)(2,1)S(1)}, u32[]{:S(2)}, u32[]{:S(2)}) %collective-permute-start.3) | collective-permute-done | bytes 393248 | tf_op jit(solution)/shard_map/ppermute | solution.py:48
  57.7 10.0 fusion.19
  67.8 12.7 %copy.135 = bf16[3072,1536]{1,0:T(8,128)(2,1)} copy(bf16[3072,1536]{0,1:T(8,128)(2,1)} %fusion.19) | data formatting | bytes 18874368 | tf_op jit(solution)/shard_map/convert_element_type | solution.py:36
  87.7 8.7 copy.136
  96.4 104.8 %self_forward.1 = (f32[3,1024,512]{2,1,0:T(8,128)}, f32[3,8,1024]{2,1,0:T(8,128)}) custom-call(s32[3,4,3]{2,1,0:T(4,128)} %pad_add_fusion.1.tiles, bf16[3,1024,1536]{2,1,0:T(8,128)(2,1)} %bitcast.297, bf16[3,1024,1024]{2,1,0:T(8,128)(2,1)} %bitcast.303, bf16[3,1024,1024]{2,1,0:T(8,128)(2,1)} %bitcast.304, bf16[3,1024,1536]{2,1,0:T(8,128)(2,1)} %bitcast.298, ...), custom_call_target="tpu_custom_call" | custom-call | tf_op jit(solution)/shard_map/self_forward/pallas_call | solution.py:190
  248.3 23.9 %fusion.68 = (f32[3,8,1024]{2,1,0:T(8,128)S(1)}, f32[3,8,1024,512]{2,3,1,0:T(8,128)}) fusion(bf16[3,1024,8,64]{1,3,2,0:T(8,128)(2,1)} %bitcast.348, bf16[3,512,8,64]{1,3,2,0:T(8,128)(2,1)S(1)} %bitcast.330), kind=kOutput, calls=%fused_computation.326 | convolution fusion | flops 1648361984 | bytes 55148544 | tf_op jit(solution)/shard_map/sub | solution.py:453
  272.2 17.5 %fusion.35 = bf16[3,8,64,1024]{3,2,1,0:T(8,128)(2,1)S(1)} fusion(bf16[3,512,8,64]{1,3,2,0:T(8,128)(2,1)S(1)} %bitcast.358, f32[3,8,1024,512]{2,3,1,0:T(8,128)} %get-tuple-element.117, f32[3,8,1024]{2,1,0:T(8,128)S(1)} %get-tuple-element.116), kind=kOutput, calls=%fused_computation.83 | convolution fusion | flops 1637351424 | bytes 55148544 | tf_op jit(solution)/shard_map/mhqk,mkhd->mqhd/dot_general | solution.py:455
  297.1 21.6 %multiply_convert_fusion.1 = (bf16[3,1024,2048]{2,1,0:T(8,128)(2,1)}, f32[3,1024,2048]{2,1,0:T(8,128)}) fusion(f32[2048]{0:T(1024)S(1)} %add.368, bf16[3,1024,512]{2,1,0:T(8,128)(2,1)} %add_convert_fusion.4, bf16[512,6784]{1,0:T(8,128)(2,1)} %all-gather.2.cloned.1.call-done), kind=kOutput, calls=%fused_computation.21 | convolution fusion | flops 6505365504 | bytes 42999808 | tf_op jit(solution)/shard_map/dot_general | solution.py:18
  318.7 10.8 fusion.70
  343.7 28.1 %convert_reduce_fusion = (f32[2048]{0:T(1024)}, bf16[3,1024,2048]{2,1,0:T(8,128)(2,1)}) fusion(f32[3,1024,2048]{2,1,0:T(8,128)} %get-tuple-element.121, f32[2048]{0:T(1024)S(1)} %add.368, bf16[3,1024,512]{2,1,0:T(8,128)(2,1)} %get-tuple-element.94, bf16[2048,512,1]{1,0,2:T(8,128)(2,1)} %reshape.1174), kind=kOutput, calls=%fused_computation.20 | convolution fusion | flops 6599735296 | bytes 43008000 | tf_op jit(solution)/shard_map/dot_general | solution.py:24
  371.7 14.8 %multiply_reduce_fusion.2 = (f32[512]{0:T(512)}, f32[3,1024]{1,0:T(4,128)S(1)}, f32[3,1024]{1,0:T(4,128)S(1)}, f32[512]{0:T(512)}, f32[3,1024,512]{2,1,0:T(8,128)S(1)}) fusion(f32[3,1024,512]{2,1,0:T(8,128)S(1)} %get-tuple-element.119, f32[3,1024]{1,0:T(4,128)S(1)} %add_rsqrt_fusion.1, f32[3,1024]{1,0:T(4,128)S(1)} %broadcast_multiply_fusion.7, ...), kind=kOutput, calls=%fused_computation.52 | convolution fusion | flops 6472328192 | bytes 36808704 | tf_op jit(solution)/shard_map/dot_general | solution.py:24
  399.1 19.5 %fusion.15 = f32[3,8,64,512]{3,2,1,0:T(8,128)} fusion(bf16[3,1024,8,64]{1,3,2,0:T(8,128)(2,1)S(1)} %bitcast.389, f32[3,8,1024,512]{2,3,1,0:T(8,128)} %get-tuple-element.117, f32[3,8,1024]{2,1,0:T(8,128)S(1)} %get-tuple-element.116), kind=kOutput, calls=%fused_computation.24 | convolution fusion | flops 1635778560 | bytes 56721408 | tf_op jit(solution)/shard_map/mhqk,mqhd->mkhd/dot_general | solution.py:488
  418.6 33.2 %multiply_reduce_fusion = (f32[3,8,1024]{2,1,0:T(8,128)S(1)}, f32[3,8,1024,512]{2,3,1,0:T(8,128)}) fusion(f32[3,8,1024,512]{2,3,1,0:T(8,128)} %get-tuple-element.117, f32[3,8,1024]{2,1,0:T(8,128)S(1)} %get-tuple-element.116, bf16[3,1024,8,64]{1,3,2,0:T(8,128)(2,1)} %bitcast.390, bf16[3,512,8,64]{1,3,2,0:T(8,128)(2,1)S(1)} %bitcast.359), kind=kOutput, calls=%fused_computation.2 | convolution fusion | flops 1648336896 | bytes 105578496 | tf_op jit(solution)/shard_map/mqhd,mkhd->mhqk/dot_general | solution.py:477
  451.7 40.8 %multiply_convert_fusion = bf16[3,8,1024,512]{2,3,1,0:T(8,128)(2,1)} fusion(f32[3,8,1024,512]{2,3,1,0:T(8,128)} %get-tuple-element.126, f32[3,8,1024]{2,1,0:T(8,128)S(1)} %get-tuple-element.125, f32[3,8,1024,512]{2,3,1,0:T(8,128)} %get-tuple-element.117, f32[3,8,1024]{2,1,0:T(8,128)S(1)} %get-tuple-element.116), kind=kLoop, calls=%fused_computation.1 | loop fusion | flops 50331648 | bytes 126025728 | tf_op jit(solution)/shard_map/convert_element_type | solution.py:36
  492.6 14.2 %convolution_multiply_fusion = f32[3,8,64,512]{3,2,1,0:T(8,128)} fusion(bf16[3,1024,8,64]{1,3,2,0:T(8,128)(2,1)S(1)} %bitcast.349, bf16[3,8,1024,512]{2,3,1,0:T(8,128)(2,1)} %multiply_convert_fusion), kind=kOutput, calls=%fused_computation.90 | convolution fusion | flops 1611399168 | bytes 31457280 | tf_op jit(solution)/shard_map/mhqk,mqhd->mkhd/dot_general | solution.py:483
  506.7 14.9 %multiply_convert_fusion.2 = bf16[3,8,64,1024]{3,2,1,0:T(8,128)(2,1)} fusion(bf16[3,512,8,64]{1,3,2,0:T(8,128)(2,1)} %bitcast.329, bf16[3,8,1024,512]{2,3,1,0:T(8,128)(2,1)} %multiply_convert_fusion), kind=kOutput, calls=%fused_computation.63 | convolution fusion | flops 1613758464 | bytes 29884416 | tf_op jit(solution)/shard_map/mhqk,mkhd->mqhd/dot_general | solution.py:480
  536.9 9.6 fusion.75
  552.9 16.8 %copy.163 = bf16[2048,3072]{1,0:T(8,128)(2,1)} copy(bf16[2048,3072]{0,1:T(8,128)(2,1)} %bitcast.316) | data formatting | bytes 25165824 | tf_op jit(solution)/shard_map/dot_general | solution.py:30
  569.7 10.7 fusion.76
  609.5 172.7 %self_backward.1 = (bf16[3,1024,512]{2,1,0:T(8,128)(2,1)}, bf16[3,1024,512]{2,1,0:T(8,128)(2,1)}, bf16[3,1024,512]{2,1,0:T(8,128)(2,1)}, f32[3,1024,512]{2,1,0:T(8,128)}, f32[3,1024,512]{2,1,0:T(8,128)}) custom-call(s32[3,4,3]{2,1,0:T(4,128)} %pad_add_fusion.1.tiles, bf16[3,1024,1536]{2,1,0:T(8,128)(2,1)} %bitcast.300, bf16[3,1024,1024]{2,1,0:T(8,128)(2,1)} %bitcast.305, ...), custom_call_target="tpu_custom_call" | custom-call | tf_op jit(solution)/shard_map/self_backward/pallas_call | solution.py:334
  793.5 9.6 reshape.1194
  813.2 51.4 %collective-permute-start.62 = (bf16[2,2,1,2,1,16,16]{6,5,4,3,2,1,0:T(8,128)(2,1)S(1)}, bf16[2,2,1,2,1,16,16]{6,5,4,3,2,1,0:T(8,128)(2,1)S(1)}, u32[]{:S(2)}, u32[]{:S(2)}) collective-permute-start(bf16[2,2,1,2,1,16,16]{6,5,4,3,2,1,0:T(8,128)(2,1)S(1)} %select_convert_fusion.35), channel_id=1, source_target_pairs={{0,4},{1,5},{2,6},{3,7},{4,0},{5,1},{6,2},{7,3},{8,12},{9,13},{10,... | collective-permute-start | bytes 12296 | tf_op jit(solution)/shard_map/ppermute | solution.py:48
  988.9 8.7 collective-permute-done.27
  1053.1 9.7 add_convert_fusion
  (567 shorter events, 399.1 us)
Async XLA Ops:
  7.2 201.9 %all-gather.2.cloned.1.call-start = ((), (), s32[]{:S(2)}) async-start(), calls=%async_computation | async-start | bytes 7163904 | tf_op jit(solution)/shard_map/all_gather | solution.py:545
  18.7 7.7 collective-permute-start
  22.8 199.8 %collective-permute-start.6 = (bf16[3,256,512]{2,1,0:T(8,128)(2,1)}, bf16[3,256,512]{2,1,0:T(8,128)(2,1)}, u32[]{:S(2)}, u32[]{:S(2)}) collective-permute-start(bf16[3,256,512]{2,1,0:T(8,128)(2,1)} %param.17), channel_id=1, source_target_pairs={{0,1},{1,0},{2,3},{3,2},{4,5},{5,4},{6,7},{7,6},{8,9},{9,8},{10,11... | collective-permute-start | bytes 2359304 | tf_op jit(solution)/shard_map/ppermute | solution.py:48
  22.8 57.6 %collective-permute-start.5 = (bf16[3,1024,512]{2,1,0:T(8,128)(2,1)}, bf16[3,1024,512]{2,1,0:T(8,128)(2,1)}, u32[]{:S(2)}, u32[]{:S(2)}) collective-permute-start(bf16[3,1024,512]{2,1,0:T(8,128)(2,1)} %param.16), channel_id=1, source_target_pairs={{1,0},{3,2},{5,4},{7,6},{9,8},{11,10},{13,12},{15,14},{17,16},{19,... | collective-permute-start | bytes 9437192 | tf_op jit(solution)/shard_map/ppermute | solution.py:52
  32.1 6.8 collective-permute-start.2
  39.0 13.8 %collective-permute-start.3 = (bf16[2,2,2,1,1,16,1536]{6,5,0,1,2,4,3:T(8,128)(2,1)S(1)}, bf16[2,2,2,1,1,16,1536]{6,5,0,1,2,4,3:T(8,128)(2,1)S(1)}, u32[]{:S(2)}, u32[]{:S(2)}) collective-permute-start(bf16[2,2,2,1,1,16,1536]{6,5,0,1,2,4,3:T(8,128)(2,1)S(1)} %maximum_select_fusion.2), channel_id=1, source_target_pairs={{0,2},{1,3},{2,0},{3,1},{4,6},{5,7},{6,4},{7,5},{8,10},{9,11},{10,... | collective-permute-start | bytes 1179656 | tf_op jit(solution)/shard_map/ppermute | solution.py:48
  549.7 428.6 %collective-permute-start.51 = (bf16[2,2,2,2,1,16,2048]{6,5,4,3,2,1,0:T(8,128)(2,1)}, bf16[2,2,2,2,1,16,2048]{6,5,4,3,2,1,0:T(8,128)(2,1)}, u32[]{:S(2)}, u32[]{:S(2)}) collective-permute-start(bf16[2,2,2,2,1,16,2048]{6,5,4,3,2,1,0:T(8,128)(2,1)} %select_convert_fusion.1), channel_id=1, source_target_pairs={{0,1},{1,0},{2,3},{3,2},{4,5},{5,4},{6,7},{7,6},{8,9},{9,8},{10,11... | collective-permute-start | bytes 3145736 | tf_op jit(solution)/shard_map/ppermute | solution.py:48
  552.4 417.0 %collective-permute-start.10 = (bf16[3,256,512]{2,1,0:T(8,128)(2,1)}, bf16[3,256,512]{2,1,0:T(8,128)(2,1)}, u32[]{:S(2)}, u32[]{:S(2)}) collective-permute-start(bf16[3,256,512]{2,1,0:T(8,128)(2,1)} %copy.200), channel_id=1, source_target_pairs={{0,1},{1,0},{2,3},{3,2},{4,5},{5,4},{6,7},{7,6},{8,9},{9,8},{10,11... | collective-permute-start | bytes 2359304 | tf_op jit(solution)/shard_map/ppermute | solution.py:48
  583.6 397.8 %collective-permute-start.56 = (bf16[2,2,2,2,1,64,512]{6,5,4,3,2,1,0:T(8,128)(2,1)}, bf16[2,2,2,2,1,64,512]{6,5,4,3,2,1,0:T(8,128)(2,1)}, u32[]{:S(2)}, u32[]{:S(2)}) collective-permute-start(bf16[2,2,2,2,1,64,512]{6,5,4,3,2,1,0:T(8,128)(2,1)} %select_convert_fusion), channel_id=1, source_target_pairs={{0,1},{1,0},{2,3},{3,2},{4,5},{5,4},{6,7},{7,6},{8,9},{9,8},{10,11... | collective-permute-start | bytes 3145736 | tf_op jit(solution)/shard_map/ppermute | solution.py:48
  604.4 208.7 %collective-permute-start.61 = (bf16[2,2,2,2,1,16,16]{6,5,4,3,2,1,0:T(8,128)(2,1)S(1)}, bf16[2,2,2,2,1,16,16]{6,5,4,3,2,1,0:T(8,128)(2,1)S(1)}, u32[]{:S(2)}, u32[]{:S(2)}) collective-permute-start(bf16[2,2,2,2,1,16,16]{6,5,4,3,2,1,0:T(8,128)(2,1)S(1)} %select_convert_fusion.24), channel_id=1, source_target_pairs={{0,1},{1,0},{2,3},{3,2},{4,5},{5,4},{6,7},{7,6},{8,9},{9,8},{10,11... | collective-permute-start | bytes 24584 | tf_op jit(solution)/shard_map/ppermute | solution.py:48
  813.2 53.3 %collective-permute-start.62 = (bf16[2,2,1,2,1,16,16]{6,5,4,3,2,1,0:T(8,128)(2,1)S(1)}, bf16[2,2,1,2,1,16,16]{6,5,4,3,2,1,0:T(8,128)(2,1)S(1)}, u32[]{:S(2)}, u32[]{:S(2)}) collective-permute-start(bf16[2,2,1,2,1,16,16]{6,5,4,3,2,1,0:T(8,128)(2,1)S(1)} %select_convert_fusion.35), channel_id=1, source_target_pairs={{0,4},{1,5},{2,6},{3,7},{4,0},{5,1},{6,2},{7,3},{8,12},{9,13},{10,... | collective-permute-start | bytes 12296 | tf_op jit(solution)/shard_map/ppermute | solution.py:48
  871.4 17.2 %collective-permute-start.46 = (bf16[2,2,2,2,1,16,512]{6,5,4,3,2,1,0:T(8,128)(2,1)}, bf16[2,2,2,2,1,16,512]{6,5,4,3,2,1,0:T(8,128)(2,1)}, u32[]{:S(2)}, u32[]{:S(2)}) collective-permute-start(bf16[2,2,2,2,1,16,512]{6,5,4,3,2,1,0:T(8,128)(2,1)} %select_convert_fusion.6), channel_id=1, source_target_pairs={{0,1},{1,0},{2,3},{3,2},{4,5},{5,4},{6,7},{7,6},{8,9},{9,8},{10,11... | collective-permute-start | bytes 786440 | tf_op jit(solution)/shard_map/ppermute | solution.py:48
  874.1 11.1 %collective-permute-start.65 = (bf16[1,1,1,1,1,16,16]{6,5,4,3,2,1,0:T(8,128)(2,1)S(1)}, bf16[1,1,1,1,1,16,16]{6,5,4,3,2,1,0:T(8,128)(2,1)S(1)}, u32[]{:S(2)}, u32[]{:S(2)}) collective-permute-start(bf16[1,1,1,1,1,16,16]{6,5,4,3,2,1,0:T(8,128)(2,1)S(1)} %select_convert_fusion.54), channel_id=1, source_target_pairs={{0,16},{1,17},{2,18},{3,19},{4,20},{5,21},{6,22},{7,23},{8,24},{9,... | collective-permute-start | bytes 1544 | tf_op jit(solution)/shard_map/ppermute | solution.py:48
  890.5 82.3 %collective-permute-start.9 = (bf16[3,256,512]{2,1,0:T(8,128)(2,1)}, bf16[3,256,512]{2,1,0:T(8,128)(2,1)S(1)}, u32[]{:S(2)}, u32[]{:S(2)}) collective-permute-start(bf16[3,256,512]{2,1,0:T(8,128)(2,1)} %copy.198), channel_id=1, source_target_pairs={{0,1},{1,0},{2,3},{3,2},{4,5},{5,4},{6,7},{7,6},{8,9},{9,8},{10,11... | collective-permute-start | bytes 2359304 | tf_op jit(solution)/shard_map/ppermute | solution.py:48
  966.6 77.3 %collective-permute-start.7 = (bf16[3,1024,512]{2,1,0:T(8,128)(2,1)S(1)}, bf16[3,1024,512]{2,1,0:T(8,128)(2,1)S(1)}, u32[]{:S(2)}, u32[]{:S(2)}) collective-permute-start(bf16[3,1024,512]{2,1,0:T(8,128)(2,1)S(1)} %copy-done.77), channel_id=1, source_target_pairs={{0,1},{2,3},{4,5},{6,7},{8,9},{10,11},{12,13},{14,15},{16,17},{18,... | collective-permute-start | bytes 9437192 | tf_op jit(solution)/shard_map/ppermute | solution.py:56
  969.3 77.4 %collective-permute-start.8 = (bf16[3,1024,512]{2,1,0:T(8,128)(2,1)S(1)}, bf16[3,1024,512]{2,1,0:T(8,128)(2,1)S(1)}, u32[]{:S(2)}, u32[]{:S(2)}) collective-permute-start(bf16[3,1024,512]{2,1,0:T(8,128)(2,1)S(1)} %copy-done.76), channel_id=1, source_target_pairs={{0,1},{2,3},{4,5},{6,7},{8,9},{10,11},{12,13},{14,15},{16,17},{18,... | collective-permute-start | bytes 9437192 | tf_op jit(solution)/shard_map/ppermute | solution.py:56
  972.9 8.1 collective-permute-start.36
  981.0 43.0 %collective-permute-start.52 = (bf16[2,2,1,2,1,16,2048]{6,5,4,3,2,1,0:T(8,128)(2,1)S(1)}, bf16[2,2,1,2,1,16,2048]{6,5,4,3,2,1,0:T(8,128)(2,1)S(1)}, u32[]{:S(2)}, u32[]{:S(2)}) collective-permute-start(bf16[2,2,1,2,1,16,2048]{6,5,4,3,2,1,0:T(8,128)(2,1)S(1)} %select_convert_fusion.3), channel_id=1, source_target_pairs={{0,4},{1,5},{2,6},{3,7},{4,0},{5,1},{6,2},{7,3},{8,12},{9,13},{10,... | collective-permute-start | bytes 1572872 | tf_op jit(solution)/shard_map/ppermute | solution.py:48
  984.1 39.4 %collective-permute-start.57 = (bf16[2,2,2,1,1,64,512]{6,5,4,3,2,1,0:T(8,128)(2,1)S(1)}, bf16[2,2,2,1,1,64,512]{6,5,4,3,2,1,0:T(8,128)(2,1)S(1)}, u32[]{:S(2)}, u32[]{:S(2)}) collective-permute-start(bf16[2,2,2,1,1,64,512]{6,5,4,3,2,1,0:T(8,128)(2,1)S(1)} %select_convert_fusion.2), channel_id=1, source_target_pairs={{0,2},{1,3},{2,0},{3,1},{4,6},{5,7},{6,4},{7,5},{8,10},{9,11},{10,... | collective-permute-start | bytes 1572872 | tf_op jit(solution)/shard_map/ppermute | solution.py:48
  987.0 10.6 collective-permute-start.27
  1023.9 6.4 collective-permute-start.58
  1024.3 8.4 collective-permute-start.53
  1046.7 16.1 %collective-permute-start.21 = (bf16[2,2,2,2,1,16,512]{6,5,4,3,2,1,0:T(8,128)(2,1)}, bf16[2,2,2,2,1,16,512]{6,5,4,3,2,1,0:T(8,128)(2,1)}, u32[]{:S(2)}, u32[]{:S(2)}) collective-permute-start(bf16[2,2,2,2,1,16,512]{6,5,4,3,2,1,0:T(8,128)(2,1)} %select_convert_fusion.11), channel_id=1, source_target_pairs={{0,1},{1,0},{2,3},{3,2},{4,5},{5,4},{6,7},{7,6},{8,9},{9,8},{10,11... | collective-permute-start | bytes 786440 | tf_op jit(solution)/shard_map/ppermute | solution.py:48
  1050.4 14.0 %collective-permute-start.31 = (bf16[2,2,2,2,1,16,512]{6,5,4,3,2,1,0:T(8,128)(2,1)}, bf16[2,2,2,2,1,16,512]{6,5,4,3,2,1,0:T(8,128)(2,1)S(1)}, u32[]{:S(2)}, u32[]{:S(2)}) collective-permute-start(bf16[2,2,2,2,1,16,512]{6,5,4,3,2,1,0:T(8,128)(2,1)} %select_convert_fusion.9), channel_id=1, source_target_pairs={{0,1},{1,0},{2,3},{3,2},{4,5},{5,4},{6,7},{7,6},{8,9},{9,8},{10,11... | collective-permute-start | bytes 786440 | tf_op jit(solution)/shard_map/ppermute | solution.py:48
  (132 other events, 1627.1 us)
Sparse Core Ops, SparseCore 0:
  17.3 77.9 all-gather.1

commit v2 on v1

v2 whole, which is shorter than its diff:
```python
import functools

import jax
import jax.numpy as jnp
from jax import lax
from jax.experimental import pallas as pl
from jax.experimental.pallas import tpu as pltpu
from jax.sharding import PartitionSpec as P

HEADS = 8
EPS = 1e-05
NEG = -1e30
LANES = 128
VMEM_LIMIT = 56 << 20


def nn(left, right):
    return lax.dot_general(
        left, right, (((1,), (0,)), ((), ())), preferred_element_type=jnp.float32
    )


def nt(left, right):
    return lax.dot_general(
        left, right, (((1,), (1,)), ((), ())), preferred_element_type=jnp.float32
    )


def tn(left, right):
    return lax.dot_general(
        left, right, (((0,), (0,)), ((), ())), preferred_element_type=jnp.float32
    )


def low(values):
    return values.astype(jnp.bfloat16)


def wide(values):
    return values.astype(jnp.float32)


def bit_count(axis):
    return (lax.axis_size(axis) - 1).bit_length()


def from_partner(x, axis, bit):
    return lax.ppermute(x, axis, [(i, i ^ 1 << bit) for i in range(lax.axis_size(axis))])


def prompt_to_continuation(x, axis):
    return lax.ppermute(x, axis, [(i + 1, i) for i in range(0, lax.axis_size(axis), 2)])


def continuation_to_prompt(x, axis):
    return lax.ppermute(x, axis, [(i, i + 1) for i in range(0, lax.axis_size(axis), 2)])


def tree_gather(x, axis):
    bits = bit_count(axis)
    me = lax.axis_index(axis)
    block = x.reshape((1,) * bits + x.shape)
    for bit in list(range(bits - 1, 0, -1)) + [0]:
        dim = bits - 1 - bit
        got = from_partner(block, axis, bit)
        block = jnp.where(
            (me >> bit) & 1 == 1,
            jnp.concatenate([got, block], dim),
            jnp.concatenate([block, got], dim),
        )
    return block.reshape((-1,) + x.shape[1:])


class TreeScatter:
    def __init__(self, arrays, orders, axis):
        self.axis = axis
        self.bits = bit_count(axis)
        self.me = lax.axis_index(axis)
        self.blocks, self.orders, self.steps, self.shapes = [], [], [], []
        self.coming = {}
        self.join(arrays, orders)

    def join(self, arrays, orders):
        size = lax.axis_size(self.axis)
        plain = list(range(self.bits))
        turned = plain[:1] + plain[1:3][::-1] + plain[3:]
        for array, order in zip(arrays, orders):
            own = (array.shape[0] // size,) + array.shape[1:]
            self.blocks.append(array.reshape((2,) * self.bits + own))
            self.orders.append((plain, turned)[order])
            self.steps.append(0)
            self.shapes.append(own)

    def halves(self, number):
        bit = self.orders[number][self.steps[number]]
        dim = self.bits - 1 - bit
        mine = (self.me >> bit) & 1
        block = self.blocks[number]
        keep = lax.dynamic_index_in_dim(block, mine, dim, keepdims=True)
        away = lax.dynamic_index_in_dim(block, 1 - mine, dim, keepdims=True)
        return bit, keep, low(away)

    def send(self, after=None):
        live = [n for n in range(len(self.blocks)) if self.steps[n] < self.bits]
        parts = {n: self.halves(n) for n in live}
        aways = [parts[n][2] for n in live]
        if after is not None:
            after, aways = lax.optimization_barrier((after, aways))
        for n, away in zip(live, aways):
            bit, keep, _ = parts[n]
            self.coming[n] = (keep, from_partner(away, self.axis, bit))
        return after, live

    def receive(self, behind=None):
        for n, (keep, got) in self.coming.items():
            if behind is not None:
                got, _ = lax.optimization_barrier((got, behind))
            self.blocks[n] = wide(keep) + wide(got)
            self.steps[n] += 1
        self.coming = {}

    def finish(self):
        while any(step < self.bits for step in self.steps):
            self.send()
            self.receive()
        return [wide(b.reshape(own)) for b, own in zip(self.blocks, self.shapes)]


def tall_sum(values):
    return jnp.sum(values.reshape(-1, 8, values.shape[1]), axis=0)


def tall_max(values):
    return jnp.max(values.reshape(-1, 8, values.shape[1]), axis=0)


def alone(pair, number):
    half = pair.shape[0] // 2
    blank = jnp.zeros((half, pair.shape[1]), pair.dtype)
    if number == 0:
        return jnp.concatenate([pair[:half], blank], axis=0)
    return jnp.concatenate([blank, pair[half:]], axis=0)


def project_kernel(x_ref, far_ref, w_ref, qt_ref, kv_ref, kvt_ref, fkv_ref, fkvt_ref):
    width = x_ref.shape[2]
    for c in range(3):
        part = slice(c * width, (c + 1) * width)
        here = low(nn(x_ref[0], w_ref[:, part]))
        if c == 0:
            qt_ref[0] = jnp.transpose(here)
            continue
        into = slice((c - 1) * width, c * width)
        kv_ref[0, :, into] = here
        kvt_ref[0, into, :] = jnp.transpose(here)
        there = low(nn(far_ref[0], w_ref[:, part]))
        fkv_ref[0, :, into] = there
        fkvt_ref[0, into, :] = jnp.transpose(there)


def project(x, far, w, block=512):
    micro, rows, width = x.shape
    tall = lambda n: jax.ShapeDtypeStruct((micro, n, rows), jnp.bfloat16)
    long = jax.ShapeDtypeStruct((micro, rows, 2 * width), jnp.bfloat16)
    rows_in = pl.BlockSpec((1, block, width), lambda m, i: (m, i, 0))
    rows_out = pl.BlockSpec((1, block, 2 * width), lambda m, i: (m, i, 0))
    turned = lambda n: pl.BlockSpec((1, n, block), lambda m, i: (m, 0, i))
    return pl.pallas_call(
        project_kernel,
        out_shape=(tall(width), long, tall(2 * width), long, tall(2 * width)),
        grid=(micro, rows // block),
        in_specs=[
            rows_in,
            rows_in,
            pl.BlockSpec(w.shape, lambda m, i: (0, 0), pipeline_mode=pl.Buffered(1)),
        ],
        out_specs=[turned(width), rows_out, turned(2 * width), rows_out, turned(2 * width)],
        compiler_params=pltpu.CompilerParams(vmem_limit_bytes=VMEM_LIMIT),
        cost_estimate=pl.CostEstimate(
            flops=2 * 5 * micro * rows * width * width,
            bytes_accessed=22 * micro * rows * width,
            transcendentals=0,
        ),
        name="project",
    )(x, far, w)


def self_forward_kernel(
    tq, tk, pairs, tiles, qt_ref, kp_ref, kl_ref, vtp_ref, vtl_ref, lim_ref, ot_ref, lse_ref, s_ref
):
    micro, tile = pl.program_id(0), pl.program_id(1)
    prefix_rows = kp_ref.shape[1]
    prefix_tiles = tiles[micro, tile, 0]
    local_first, local_end = tiles[micro, tile, 1], tiles[micro, tile, 2]
    reach, start = lim_ref[0, 0:1, :], lim_ref[0, 1:2, :]
    rows = tile * tq + lax.broadcasted_iota(jnp.int32, (1, tq), 1)
    key_at = lax.broadcasted_iota(jnp.int32, (tk, tq), 0)
    heads = 2 * pairs
    size = LANES // 2

    def prefix_mask(j):
        return key_at < reach - j * tk

    def local_mask(j):
        return (key_at <= rows - j * tk) & (key_at >= start - j * tk)

    for group in range(HEADS // heads):
        queries = []
        for h in range(heads):
            p = group * pairs + h // 2
            pair = qt_ref[0, p * LANES : (p + 1) * LANES, :] * jnp.bfloat16(0.125)
            queries.append(alone(pair, h % 2))

        def score(k_ref, offset, masker, j, tops):
            base = pl.multiple_of(j * tk, tk)
            seen = masker(j)
            out = []
            for h in range(heads):
                p = group * pairs + h // 2
                s = nn(k_ref[0, pl.ds(base, tk), p * LANES : (p + 1) * LANES], queries[h])
                s = jnp.where(seen, s, NEG)
                s_ref[h, pl.ds(pl.multiple_of(offset + base, tk), tk), :] = s
                out.append(jnp.maximum(tops[h], tall_max(s)))
            return tuple(out)

        tops = tuple(jnp.full((8, tq), NEG, jnp.float32) for _ in range(heads))
        tops = lax.fori_loop(
            0, prefix_tiles, functools.partial(score, kp_ref, 0, prefix_mask), tops
        )
        tops = lax.fori_loop(
            local_first,
            local_end,
            functools.partial(score, kl_ref, prefix_rows, local_mask),
            tops,
        )
        tops = [jnp.max(t, axis=0, keepdims=True) for t in tops]

        def mix(vt_ref, offset, j, carry):
            base = pl.multiple_of(j * tk, tk)
            out = []
            for h in range(heads):
                head = group * heads + h
                e = jnp.exp(
                    s_ref[h, pl.ds(pl.multiple_of(offset + base, tk), tk), :] - tops[h]
                )
                total, mixed = carry[2 * h], carry[2 * h + 1]
                out.append(total + tall_sum(e))
                out.append(
                    mixed
                    + nn(vt_ref[0, head * size : (head + 1) * size, pl.ds(base, tk)], low(e))
                )
            return tuple(out)

        carry = (jnp.zeros((8, tq), jnp.float32), jnp.zeros((size, tq), jnp.float32)) * heads
        carry = lax.fori_loop(0, prefix_tiles, functools.partial(mix, vtp_ref, 0), carry)
        carry = lax.fori_loop(
            local_first, local_end, functools.partial(mix, vtl_ref, prefix_rows), carry
        )
        for h in range(heads):
            head = group * heads + h
            total = jnp.sum(carry[2 * h], axis=0, keepdims=True)
            ot_ref[0, head * size : (head + 1) * size, :] = carry[2 * h + 1] / total
            lse_ref[0, head : head + 1, :] = tops[h] + jnp.log(total)


def self_forward(qt, kv, kvt, far_kv, far_kvt, limits, tiles, tq=256, tk=256, pairs=4):
    micro, width, rows = qt.shape
    return pl.pallas_call(
        functools.partial(self_forward_kernel, tq, tk, pairs),
        out_shape=(
            jax.ShapeDtypeStruct((micro, width, rows), jnp.float32),
            jax.ShapeDtypeStruct((micro, HEADS, rows), jnp.float32),
        ),
        grid_spec=pltpu.PrefetchScalarGridSpec(
            num_scalar_prefetch=1,
            grid=(micro, rows // tq),
            in_specs=[
                pl.BlockSpec((1, width, tq), lambda m, i, s: (m, 0, i)),
                pl.BlockSpec((1, rows, width), lambda m, i, s: (m, 0, 0)),
                pl.BlockSpec((1, rows, width), lambda m, i, s: (m, 0, 0)),
                pl.BlockSpec((1, width, rows), lambda m, i, s: (m, 1, 0)),
                pl.BlockSpec((1, width, rows), lambda m, i, s: (m, 1, 0)),
                pl.BlockSpec((1, 2, tq), lambda m, i, s: (m, 0, i)),
            ],
            out_specs=[
                pl.BlockSpec((1, width, tq), lambda m, i, s: (m, 0, i)),
                pl.BlockSpec((1, HEADS, tq), lambda m, i, s: (m, 0, i)),
            ],
            scratch_shapes=[pltpu.VMEM((2 * pairs, 2 * rows, tq), jnp.float32)],
        ),
        compiler_params=pltpu.CompilerParams(vmem_limit_bytes=VMEM_LIMIT),
        cost_estimate=pl.CostEstimate(
            flops=4 * micro * rows * rows * width,
            bytes_accessed=16 * micro * rows * width,
            transcendentals=micro * rows * rows * HEADS,
        ),
        name="self_forward",
    )(tiles, qt, far_kv, kv, far_kvt, kvt, limits)


def self_backward_kernel(
    micro,
    tq,
    tk,
    pairs,
    tiles,
    qt_ref,
    kp_ref,
    vp_ref,
    kl_ref,
    vl_ref,
    ktp_ref,
    ktl_ref,
    dot_ref,
    lse_ref,
    delta_ref,
    lim_ref,
    x_ref,
    far_ref,
    dqt_ref,
    dkp_ref,
    dvp_ref,
    dkl_ref,
    dvl_ref,
    g_ref,
    sum_kp,
    sum_vp,
    sum_kl,
    sum_vl,
    sum_q,
):
    row_count = qt_ref.shape[2]
    size = LANES // 2
    for ref in (sum_kp, sum_vp, sum_kl, sum_vl):
        ref[...] = jnp.zeros_like(ref)
    key_at = lax.broadcasted_iota(jnp.int32, (tk, tq), 0)
    for i in range(row_count // tq):
        here = slice(i * tq, (i + 1) * tq)
        prefix_tiles = tiles[micro, i, 0]
        local_first, local_end = tiles[micro, i, 1], tiles[micro, i, 2]
        reach, start = lim_ref[0, 0:1, here], lim_ref[0, 1:2, here]
        rows = i * tq + lax.broadcasted_iota(jnp.int32, (1, tq), 1)
        queries, grads, totals, deltas = [], [], [], []
        for h in range(2 * pairs):
            part = slice(h // 2 * LANES, (h // 2 + 1) * LANES)
            queries.append(alone(qt_ref[0, part, here] * jnp.bfloat16(0.125), h % 2))
            grads.append(alone(dot_ref[0, part, here], h % 2))
            totals.append(lse_ref[0, 0, h : h + 1, here])
            deltas.append(delta_ref[0, 0, h : h + 1, here])
        sum_q[...] = jnp.zeros_like(sum_q)

        def body(k_ref, v_ref, kt_ref, sum_k, sum_v, masker, j, _):
            base = pl.multiple_of(j * tk, tk)
            seen = masker(j)
            for k in range(pairs):
                cols = slice(k * LANES, (k + 1) * LANES)
                keys = k_ref[0, pl.ds(base, tk), cols]
                values = v_ref[0, pl.ds(base, tk), cols]
                for h in (2 * k, 2 * k + 1):
                    s = jnp.where(seen, nn(keys, queries[h]), NEG)
                    p = jnp.exp(s - totals[h])
                    dp = nn(values, grads[h])
                    sum_v[pl.ds(base, tk), cols] += nt(low(p), grads[h])
                    ds = low(p * (dp - deltas[h]))
                    sum_k[pl.ds(base, tk), cols] += nt(ds, queries[h])
                    part = slice(h * size, (h + 1) * size)
                    sum_q[part, :] += nn(kt_ref[0, part, pl.ds(base, tk)], ds)
            return 0

        def prefix_mask(j):
            return key_at < reach - j * tk

        def local_mask(j):
            return (key_at <= rows - j * tk) & (key_at >= start - j * tk)

        lax.fori_loop(
            0,
            prefix_tiles,
            functools.partial(body, kp_ref, vp_ref, ktp_ref, sum_kp, sum_vp, prefix_mask),
            0,
        )
        lax.fori_loop(
            local_first,
            local_end,
            functools.partial(body, kl_ref, vl_ref, ktl_ref, sum_kl, sum_vl, local_mask),
            0,
        )
        dqt_ref[0, :, here] = low(sum_q[...] * 0.125)
    dkp_ref[0] = low(sum_kp[...])
    dvp_ref[0] = low(sum_vp[...])
    dkl_ref[0] = low(sum_kl[...])
    dvl_ref[0] = low(sum_vl[...])
    width = x_ref.shape[2]
    own, far = jnp.transpose(x_ref[0]), jnp.transpose(far_ref[0])
    g_ref[:, :width] = nt(own, dqt_ref[0])
    g_ref[:, width : 2 * width] = nn(own, dkl_ref[0]) + nn(far, dkp_ref[0])
    g_ref[:, 2 * width :] = nn(own, dvl_ref[0]) + nn(far, dvp_ref[0])


def self_backward(
    number, qt, kv, kvt, far_kv, far_kvt, grad_out, lse, delta, limits, tiles, x, far_x
):
    tq, tk, pairs = 256, 256, HEADS // 2
    micro, width, rows = qt.shape
    tall = pl.BlockSpec((1, width, rows), lambda i, s: (number, 0, 0))
    long = lambda place: pl.BlockSpec((1, rows, width), lambda i, s: (number, 0, place))
    line = pl.BlockSpec((1, 1, HEADS, rows), lambda i, s: (number, 0, 0, 0))
    tall_out = pl.BlockSpec((1, width, rows), lambda i, s: (0, 0, 0))
    long_out = pl.BlockSpec((1, rows, width), lambda i, s: (0, 0, 0))
    bf16 = jax.ShapeDtypeStruct((1, rows, width), jnp.bfloat16)
    return pl.pallas_call(
        functools.partial(self_backward_kernel, number, tq, tk, pairs),
        out_shape=(
            jax.ShapeDtypeStruct((1, width, rows), jnp.bfloat16),
            bf16,
            bf16,
            bf16,
            bf16,
            jax.ShapeDtypeStruct((width, 3 * width), jnp.float32),
        ),
        grid_spec=pltpu.PrefetchScalarGridSpec(
            num_scalar_prefetch=1,
            grid=(1,),
            in_specs=[
                tall,
                long(0),
                long(1),
                long(0),
                long(1),
                tall,
                tall,
                tall,
                line,
                line,
                pl.BlockSpec((1, 2, rows), lambda i, s: (number, 0, 0)),
                long(0),
                long(0),
            ],
            out_specs=[tall_out]
            + [long_out] * 4
            + [pl.BlockSpec((width, 3 * width), lambda i, s: (0, 0))],
            scratch_shapes=[pltpu.VMEM((rows, width), jnp.float32)] * 4
            + [pltpu.VMEM((width, tq), jnp.float32)],
        ),
        compiler_params=pltpu.CompilerParams(vmem_limit_bytes=60 << 20),
        cost_estimate=pl.CostEstimate(
            flops=10 * rows * rows * width,
            bytes_accessed=40 * rows * width,
            transcendentals=rows * rows * HEADS,
        ),
        name="self_backward",
    )(
        tiles,
        qt,
        far_kv,
        far_kv,
        kv,
        kv,
        far_kvt,
        kvt,
        grad_out,
        lse[:, None],
        delta[:, None],
        limits,
        x,
        far_x,
    )


def mask_limits(seg, off, is_prompt, tq=256, tk=256):
    micro, rows = seg.shape
    index = jnp.arange(off.shape[1], dtype=jnp.int32)
    own = seg[:, :, None] == index
    count = jnp.sum(own.astype(jnp.int32), axis=1)
    before = jnp.sum(jnp.where(index[:, None] > index[None, :], count[:, None, :], 0), axis=2)
    reach = jnp.sum(jnp.where(own, off[:, None, :], 0), axis=2)
    start = jnp.sum(jnp.where(own, before[:, None, :], 0), axis=2)
    reach = jnp.where(is_prompt, 0, reach)
    start = jnp.where(is_prompt, 0, start)
    tile_count = rows // tq
    most = jnp.max(reach.reshape(micro, tile_count, tq), axis=2)
    least = jnp.min(start.reshape(micro, tile_count, tq), axis=2)
    end = (jnp.arange(tile_count, dtype=jnp.int32) + 1) * tq
    tiles = jnp.stack(
        [
            (most + tk - 1) // tk,
            least // tk,
            jnp.broadcast_to((end + tk - 1) // tk, (micro, tile_count)),
        ],
        axis=2,
    )
    return jnp.stack([reach, start], axis=1), tiles


GELU_C = 0.7978845608028654
GELU_A = 0.044715


def spread(column, values):
    return jnp.concatenate([wide(column)] * (values.shape[1] // LANES), axis=1)


def lanes_of(values):
    total = values[:, :LANES]
    for c in range(1, values.shape[1] // LANES):
        total = total + values[:, c * LANES : (c + 1) * LANES]
    return total


def norm_tall(z):
    count = z.shape[0]
    mean = jnp.sum(tall_sum(z), axis=0, keepdims=True) / count
    centred = z - mean
    inv = lax.rsqrt(jnp.sum(tall_sum(centred * centred), axis=0, keepdims=True) / count + EPS)
    return centred * inv, inv


def norm_tall_backward(scaled, normed, inv):
    count = scaled.shape[0]
    mean = jnp.sum(tall_sum(scaled), axis=0, keepdims=True) / count
    slope = jnp.sum(tall_sum(scaled * normed), axis=0, keepdims=True) / count
    return inv * (scaled - mean - normed * slope)


def middle_kernel(
    x_ref,
    cot_ref,
    ot_ref,
    mem_ref,
    far_mem_ref,
    win_ref,
    wout_ref,
    wo0_ref,
    wq1_ref,
    wo1_ref,
    wk1_ref,
    wv1_ref,
    small_ref,
    out_ref,
    dso_ref,
    delta_ref,
    skip_ref,
    own_dmk_ref,
    own_dmv_ref,
    far_dmk_ref,
    far_dmv_ref,
    ga_ref,
    gb_ref,
    mk_ref,
    mv_ref,
    mkt_ref,
    mvt_ref,
    wint_ref,
    woutt_ref,
    wo0t_ref,
    wq1t_ref,
    wo1t_ref,
    par_ref,
    fb_ref,
    dmk_ref,
    dmv_ref,
    gpar_ref,
    gfb_ref,
    p_ref,
    act_ref,
    slope_ref,
    mixed_ref,
    dcq_ref,
):
    micro, tile = pl.program_id(0), pl.program_id(1)
    width = x_ref.shape[2]
    hidden = win_ref.shape[1]
    mem_rows = mk_ref.shape[0]
    own_mem = mem_ref.shape[1]
    chunk = width
    half_mem = 256
    size = LANES // 2
    par_count = par_ref.shape[0]
    mem_at = width + hidden

    @pl.when((micro == 0) & (tile == 0))
    def _():
        for ref in (ga_ref, gb_ref, gpar_ref, gfb_ref):
            ref[...] = jnp.zeros_like(ref)
        for here, there in ((wo0_ref, wo0t_ref), (wq1_ref, wq1t_ref), (wo1_ref, wo1t_ref)):
            there[...] = jnp.transpose(here[...])
        for c in range(hidden // chunk):
            part = slice(c * chunk, (c + 1) * chunk)
            wint_ref[part, :] = jnp.transpose(win_ref[:, part])
            woutt_ref[:, part] = jnp.transpose(wout_ref[:, part])
            column = small_ref[:, par_count + c : par_count + c + 1]
            fb_ref[part, :] = low(jnp.broadcast_to(wide(column), (chunk, LANES)))
        for n in range(par_count):
            column = small_ref[:, n : n + 1]
            par_ref[n] = low(jnp.broadcast_to(wide(column), (width, LANES)))

    @pl.when(tile == 0)
    def _():
        dmk_ref[...] = jnp.zeros_like(dmk_ref)
        dmv_ref[...] = jnp.zeros_like(dmv_ref)
        for number, ref in enumerate((mem_ref, far_mem_ref)):
            part = slice(number * own_mem, (number + 1) * own_mem)
            for w_ref, m_ref, mt_ref in ((wk1_ref, mk_ref, mkt_ref), (wv1_ref, mv_ref, mvt_ref)):
                got = low(nn(ref[0], w_ref[...]))
                m_ref[part, :] = got
                mt_ref[:, part] = jnp.transpose(got)

    def par(kind, number, like):
        return spread(par_ref[3 * kind + number], like)

    def note(kind, number, values):
        gpar_ref[3 * kind + number] += lanes_of(values)

    x = wide(jnp.transpose(x_ref[0]))
    self_out = ot_ref[0]
    self_low = low(self_out)
    z = x * par(1, 0, x) + (nn(wo0t_ref[...], self_low) + par(0, 0, x))
    n1, inv1 = norm_tall(z)
    h1 = low(n1 * par(2, 0, x) + par(3, 0, x))
    cq = low(nn(wq1t_ref[...], h1)) * jnp.bfloat16(0.125)
    tops, shares = [], []
    for head in range(HEADS):
        pair = slice(head // 2 * LANES, (head // 2 + 1) * LANES)
        query = alone(cq[pair, :], head % 2)
        top = None
        for c in range(mem_rows // half_mem):
            keys = slice(c * half_mem, (c + 1) * half_mem)
            s = nn(mk_ref[keys, pair], query)
            p_ref[head, keys, :] = s
            here = tall_max(s)
            top = here if top is None else jnp.maximum(top, here)
        tops.append(jnp.max(top, axis=0, keepdims=True))
    for head in range(HEADS):
        part = slice(head * size, (head + 1) * size)
        total, mixed = 0.0, 0.0
        for c in range(mem_rows // half_mem):
            keys = slice(c * half_mem, (c + 1) * half_mem)
            e = jnp.exp(p_ref[head, keys, :] - tops[head])
            p_ref[head, keys, :] = e
            total = total + tall_sum(e)
            mixed = mixed + nn(mvt_ref[part, keys], low(e))
        share = 1.0 / jnp.sum(total, axis=0, keepdims=True)
        shares.append(share)
        mixed_ref[part, :] = mixed * share
    cross = low(mixed_ref[...])
    z = wide(h1) * par(1, 1, x) + (nn(wo1t_ref[...], cross) + par(0, 1, x))
    n2, inv2 = norm_tall(z)
    h2 = low(n2 * par(2, 1, x) + par(3, 1, x))
    branch = 0.0
    for c in range(hidden // chunk):
        part = slice(c * chunk, (c + 1) * chunk)
        pre = nn(wint_ref[part, :], h2)
        pre = pre + spread(fb_ref[part, :], pre)
        square = pre * pre
        gate = 0.5 * jnp.tanh(pre * (square * (GELU_C * GELU_A) + GELU_C)) + 0.5
        act = low(pre * gate)
        act_ref[part, :] = act
        slope_ref[part, :] = gate + (pre * (gate * (1.0 - gate))) * (
            square * (6.0 * GELU_C * GELU_A) + 2.0 * GELU_C
        )
        branch = branch + nn(woutt_ref[:, part], act)
    z = wide(h2) * par(1, 2, x) + (branch + par(0, 2, x))
    n3, inv3 = norm_tall(z)
    out_ref[0] = jnp.transpose(low(n3 * par(2, 2, x) + par(3, 2, x)))

    top = wide(jnp.transpose(cot_ref[0]))
    note(2, 2, top * n3)
    note(3, 2, top)
    dz = norm_tall_backward(top * par(2, 2, x), n3, inv3)
    note(1, 2, dz * wide(h2))
    df = low(dz)
    note(0, 2, wide(df))
    dh = dz * par(1, 2, x)
    for c in range(hidden // chunk):
        part = slice(c * chunk, (c + 1) * chunk)
        dact = low(nn(wout_ref[:, part], df))
        dpre = low(wide(dact) * slope_ref[part, :])
        gfb_ref[part, :] += lanes_of(wide(dpre))
        at = width + c * chunk
        gb_ref[:, at : at + chunk] += nt(act_ref[part, :], df)
        ga_ref[:, part] += nt(h2, dpre)
        dh = dh + nn(win_ref[:, part], dpre)
    note(2, 1, dh * n2)
    note(3, 1, dh)
    dz = norm_tall_backward(dh * par(2, 1, x), n2, inv2)
    note(1, 1, dz * wide(h1))
    dc = low(dz)
    note(0, 1, wide(dc))
    gb_ref[:, :width] += nt(cross, dc)
    dco = low(nn(wo1_ref[...], dc))
    for k in range(HEADS // 2):
        pair = slice(k * LANES, (k + 1) * LANES)
        queries = [alone(cq[pair, :], number) for number in range(2)]
        grads = [alone(dco[pair, :], number) for number in range(2)]
        weighed = wide(dco[pair, :]) * mixed_ref[pair, :]
        dq = [0.0, 0.0]
        for c in range(mem_rows // half_mem):
            keys = slice(c * half_mem, (c + 1) * half_mem)
            for number in range(2):
                head = 2 * k + number
                part = slice(head * size, (head + 1) * size)
                delta = jnp.sum(
                    tall_sum(weighed[number * size : (number + 1) * size]), axis=0, keepdims=True
                )
                p = p_ref[head, keys, :] * shares[head]
                ds = low(p * (nn(mv_ref[keys, pair], grads[number]) - delta))
                dq[number] = dq[number] + nn(mkt_ref[part, keys], ds)
                dmk_ref[keys, pair] += nt(ds, queries[number])
                dmv_ref[keys, pair] += nt(low(p), grads[number])
        for number in range(2):
            head = 2 * k + number
            dcq_ref[head * size : (head + 1) * size, :] = low(dq[number] * 0.125)
    dcq = dcq_ref[...]
    ga_ref[:, hidden + width : hidden + 2 * width] += nt(h1, dcq)
    dh = nn(wq1_ref[...], dcq) + dz * par(1, 1, x)
    note(2, 0, dh * n1)
    note(3, 0, dh)
    dz = norm_tall_backward(dh * par(2, 0, x), n1, inv1)
    note(1, 0, dz * x)
    da = low(dz)
    note(0, 0, wide(da))
    ga_ref[:, hidden : hidden + width] += nt(self_low, da)
    dso = low(nn(wo0_ref[...], da))
    dso_ref[0] = dso
    share = wide(dso) * self_out
    delta_ref[0] = jnp.concatenate(
        [
            jnp.sum(tall_sum(share[h * size : (h + 1) * size]), axis=0, keepdims=True)
            for h in range(HEADS)
        ],
        axis=0,
    )
    skip_ref[0] = jnp.transpose(dz * par(1, 0, x))

    @pl.when(tile == pl.num_programs(1) - 1)
    def _():
        turned = [jnp.transpose(mem_ref[0]), jnp.transpose(far_mem_ref[0])]
        for ref, own, far, at in (
            (dmk_ref, own_dmk_ref, far_dmk_ref, mem_at),
            (dmv_ref, own_dmv_ref, far_dmv_ref, mem_at + width),
        ):
            own_low, far_low = low(ref[:own_mem, :]), low(ref[own_mem:, :])
            own[0] = ref[:own_mem, :]
            far[0] = far_low
            gb_ref[:, at : at + width] += nn(turned[0], own_low) + nn(turned[1], far_low)

    @pl.when((micro == pl.num_programs(0) - 1) & (tile == pl.num_programs(1) - 1))
    def _():
        lane = lax.broadcasted_iota(jnp.int32, (width, LANES), 1)
        small = jnp.zeros((width, LANES), jnp.float32)
        for n in range(par_count):
            small = jnp.where(lane == n, jnp.sum(gpar_ref[n], axis=1, keepdims=True), small)
        for c in range(hidden // chunk):
            column = jnp.sum(gfb_ref[c * chunk : (c + 1) * chunk, :], axis=1, keepdims=True)
            small = jnp.where(lane == par_count + c, column, small)
        gb_ref[:, mem_at + 2 * width :] = small


def middle(x, cot, self_out, memory, far_memory, rest, hidden, block=256):
    micro, rows, width = x.shape
    own_mem = memory.shape[1]
    mem_rows = 2 * own_mem
    f32, bf16 = jnp.float32, jnp.bfloat16
    row_block = pl.BlockSpec((1, block, width), lambda m, i: (m, i, 0))
    tall_block = pl.BlockSpec((1, width, block), lambda m, i: (m, 0, i))
    mem_block = pl.BlockSpec((1, own_mem, width), lambda m, i: (m, 0, 0))

    def fixed(columns, place):
        return pl.BlockSpec(
            (width, columns), lambda m, i: (0, place), pipeline_mode=pl.Buffered(1)
        )

    base = 2 * hidden // width
    columns = [hidden + 2 * width, 3 * width + hidden + LANES]
    mem_out = lambda kind: jax.ShapeDtypeStruct((micro, own_mem, width), kind)
    return pl.pallas_call(
        middle_kernel,
        out_shape=[
            jax.ShapeDtypeStruct((micro, rows, width), bf16),
            jax.ShapeDtypeStruct((micro, width, rows), bf16),
            jax.ShapeDtypeStruct((micro, HEADS, rows), f32),
            jax.ShapeDtypeStruct((micro, rows, width), f32),
            mem_out(f32),
            mem_out(f32),
            mem_out(bf16),
            mem_out(bf16),
        ]
        + [jax.ShapeDtypeStruct((width, n), f32) for n in columns],
        grid=(micro, rows // block),
        in_specs=[row_block, row_block, tall_block, mem_block, mem_block]
        + [fixed(hidden, 0), fixed(hidden, 1)]
        + [fixed(width, base + n) for n in range(5)]
        + [fixed(LANES, (base + 5) * width // LANES)],
        out_specs=[
            row_block,
            tall_block,
            pl.BlockSpec((1, HEADS, block), lambda m, i: (m, 0, i)),
            row_block,
        ]
        + [mem_block] * 4
        + [fixed(n, 0) for n in columns],
        scratch_shapes=[
            pltpu.VMEM((mem_rows, width), bf16),
            pltpu.VMEM((mem_rows, width), bf16),
            pltpu.VMEM((width, mem_rows), bf16),
            pltpu.VMEM((width, mem_rows), bf16),
            pltpu.VMEM((hidden, width), bf16),
            pltpu.VMEM((width, hidden), bf16),
            pltpu.VMEM((width, width), bf16),
            pltpu.VMEM((width, width), bf16),
            pltpu.VMEM((width, width), bf16),
            pltpu.VMEM((12, width, LANES), bf16),
            pltpu.VMEM((hidden, LANES), bf16),
            pltpu.VMEM((mem_rows, width), f32),
            pltpu.VMEM((mem_rows, width), f32),
            pltpu.VMEM((12, width, LANES), f32),
            pltpu.VMEM((hidden, LANES), f32),
            pltpu.VMEM((HEADS, mem_rows, block), f32),
            pltpu.VMEM((hidden, block), bf16),
            pltpu.VMEM((hidden, block), f32),
            pltpu.VMEM((width, block), f32),
            pltpu.VMEM((width, block), bf16),
        ],
        compiler_params=pltpu.CompilerParams(vmem_limit_bytes=60 << 20),
        cost_estimate=pl.CostEstimate(
            flops=6 * micro * rows * width * (3 * width + 2 * hidden + 4 * mem_rows),
            bytes_accessed=20 * micro * rows * width + 30 * width * (width + hidden),
            transcendentals=micro * rows * (HEADS * mem_rows + hidden),
        ),
        name="middle",
    )(x, cot, self_out, memory, far_memory, *[rest] * 8)


def input_grad_kernel(
    dqt_ref, dk_ref, dv_ref, far_dk_ref, far_dv_ref, w_ref, skip_ref, *rest
):
    out_ref = rest[-1]
    width = dk_ref.shape[2]
    dk = low(wide(dk_ref[0]) + wide(far_dk_ref[0]))
    dv = low(wide(dv_ref[0]) + wide(far_dv_ref[0]))
    out_ref[0] = low(
        nt(jnp.transpose(dqt_ref[0]), w_ref[:, :width])
        + nt(dk, w_ref[:, width : 2 * width])
        + nt(dv, w_ref[:, 2 * width :])
        + skip_ref[0]
    )


def input_gradient(number, dqt, dk, dv, far_dk, far_dv, w, skip, so_far, block=512):
    micro, rows, width = skip.shape
    row_block = pl.BlockSpec((1, block, width), lambda i: (0, i, 0))
    place = pl.BlockSpec((1, block, width), lambda i: (number, i, 0))
    before = [] if so_far is None else [so_far]
    return pl.pallas_call(
        input_grad_kernel,
        out_shape=jax.ShapeDtypeStruct((micro, rows, width), jnp.bfloat16),
        grid=(rows // block,),
        in_specs=[pl.BlockSpec((1, width, block), lambda i: (0, 0, i))]
        + [row_block] * 4
        + [
            pl.BlockSpec(w.shape, lambda i: (0, 0), pipeline_mode=pl.Buffered(1)),
            place,
        ]
        + [pl.BlockSpec(memory_space=pl.ANY)] * len(before),
        out_specs=place,
        input_output_aliases={7: 0} if before else {},
        compiler_params=pltpu.CompilerParams(vmem_limit_bytes=VMEM_LIMIT),
        cost_estimate=pl.CostEstimate(
            flops=6 * rows * width * width,
            bytes_accessed=16 * rows * width + 6 * width * width,
            transcendentals=0,
        ),
        name="input_gradient",
    )(dqt, dk, dv, far_dk, far_dv, w, skip, *before)


def total_tn(left, right):
    return tn(left.reshape(-1, left.shape[-1]), right.reshape(-1, right.shape[-1]))


def flat_nn(left, right):
    return nn(left.reshape(-1, left.shape[-1]), right).reshape(left.shape[:-1] + (right.shape[1],))


def flat_nt(left, right):
    return nt(left.reshape(-1, left.shape[-1]), right).reshape(left.shape[:-1] + (right.shape[0],))


def body(
    layer_in,
    memory,
    seg_ids,
    offsets,
    cotangent,
    attn_q,
    attn_k,
    attn_v,
    attn_o,
    w_in,
    w_out,
    ffn_bias,
    out_bias,
    omega,
    ln_gain,
    ln_bias,
):
    axis = "dp"
    is_prompt = lax.axis_index(axis) % 2 == 1
    own_rows = attn_q.shape[1]
    width = attn_q.shape[2]
    hidden = w_in.shape[1]
    mem_rows = memory.shape[1]

    packed = jnp.concatenate([attn_q[0], attn_k[0], attn_v[0]], axis=1)
    packed, w_in, w_out, small_parts, layer_in, memory = lax.optimization_barrier(
        (packed, w_in, w_out, (out_bias, omega, ln_gain, ln_bias, ffn_bias), layer_in, memory)
    )
    first = tree_gather(packed, axis)
    far_x = prompt_to_continuation(layer_in, axis)
    far_memory = from_partner(memory, axis, 0)
    parts = hidden // width
    small = jnp.concatenate(
        [p.T for p in small_parts[:4]] + [small_parts[4].reshape(own_rows, -1)], axis=1
    )
    small_cols = small.shape[1]
    rest = lax.all_gather(
        jnp.concatenate(
            [
                jnp.swapaxes(w_in.reshape(own_rows, width, parts), 1, 2).reshape(own_rows, -1),
                w_out.reshape(own_rows, -1),
                attn_o[0],
                attn_q[1],
                attn_o[1],
                attn_k[1],
                attn_v[1],
                jnp.pad(small, ((0, 0), (0, LANES - small_cols))),
            ],
            axis=1,
        ),
        axis,
        axis=0,
        tiled=True,
    )
    limits, tiles = mask_limits(seg_ids[:, 0], offsets[:, 0], is_prompt)
    qt, kv, kvt, far_kv, far_kvt = project(layer_in, far_x, first)
    self_out, lse = self_forward(qt, kv, kvt, far_kv, far_kvt, limits, tiles)
    (
        final,
        dso,
        delta,
        skip,
        own_mk,
        own_mv,
        far_mk,
        far_mv,
        g_a,
        g_b,
    ) = middle(layer_in, cotangent, self_out, memory, far_memory, rest, hidden)

    ready = TreeScatter([g_a, g_b], [0, 1], axis)
    back, far = [], []
    for number in range(layer_in.shape[0]):
        dso, _ = ready.send(dso)
        back.append(
            self_backward(
                number,
                qt,
                kv,
                kvt,
                far_kv,
                far_kvt,
                dso,
                lse,
                delta,
                limits,
                tiles,
                layer_in,
                far_x,
            )
        )
        ready.receive(back[number][0])
        far.append(continuation_to_prompt(back[number][1:3], axis))
    mem_dk = low(own_mk + wide(from_partner(far_mk, axis, 0)))
    mem_dv = low(own_mv + wide(from_partner(far_mv, axis, 0)))
    at = 2 * hidden + 3 * width
    memory_grad = low(
        flat_nt(mem_dk, rest[:, at : at + width])
        + flat_nt(mem_dv, rest[:, at + width : at + 2 * width])
    )
    late = TreeScatter([sum(b[5] for b in back)], [0], axis)
    input_grad = None
    for number, (b, f) in enumerate(zip(back, far)):
        input_grad = input_gradient(
            number, b[0], b[3], b[4], f[0], f[1], first, skip, input_grad
        )
    s_a, s_b = ready.finish()
    (s_c,) = late.finish()
    s_q0, s_k0, s_v0 = (s_c[:, k * width : (k + 1) * width] for k in range(3))
    s_in = jnp.swapaxes(s_a[:, :hidden].reshape(own_rows, parts, width), 1, 2)
    s_in = s_in.reshape(own_rows, hidden)
    s_o0, s_q1 = s_a[:, hidden : hidden + width], s_a[:, hidden + width :]
    s_o1 = s_b[:, :width]
    s_out = s_b[:, width : width + hidden].reshape(w_out.shape)
    s_k1, s_v1 = (s_b[:, hidden + k * width :][:, :width] for k in (1, 2))
    s_small = s_b[:, hidden + 3 * width :][:, :small_cols]
    return (
        final,
        input_grad,
        memory_grad,
        jnp.stack([s_q0, s_q1]),
        jnp.stack([s_k0, s_k1]),
        jnp.stack([s_v0, s_v1]),
        jnp.stack([s_o0, s_o1]),
        s_in,
        s_out,
        s_small[:, 12:].reshape(-1),
        s_small[:, 0:3].T,
        s_small[:, 3:6].T,
        s_small[:, 6:9].T,
        s_small[:, 9:12].T,
    )


def solution(mesh):
    rows = P(None, "dp", None)
    small = P(None, "dp")
    return jax.shard_map(
        body,
        mesh=mesh,
        in_specs=(rows,) * 9 + (P("dp", None), P("dp", None), P("dp"), small, small, small, small),
        out_specs=(rows,) * 7 + (P("dp", None), P("dp", None), P("dp"), small, small, small, small),
        check_vma=False,
    )
```

time: 1100 us -> 588 us (0.53)
  matrix products: 305 us -> 4.82 us
  Pallas kernels: 278 us -> 403 us
  local copies, waits for them, and re-layouts: 143 us -> 38.4 us
  waiting for transfers between devices: 142 us -> 39.7 us
  other arithmetic: 103 us -> 25.9 us
  starting transfers between devices: 105 us -> 57.2 us
    dot_general x23 -> x0, matrix products: 201 us -> none  [the longest x8 66.1 us: nn(): lax.dot_general(left, right, (((1,), (0,)), ((), ())), preferred_element_...]
    pallas_call x1 -> x8, Pallas kernels: 173 us -> 340 us  [the longest x1 163 us: middle(): pl.pallas_call(middle_kernel, out_shape=[jax.ShapeDtypeStruct((micro, row...]
    ppermute x63 -> x23, waiting for transfers between devices: 142 us -> 39.6 us  [from_partner(): lax.ppermute(x, axis, [(i, i ^ 1 << bit) for i in range(lax.axis_size(axi...]
    dot_general x10 -> x2, matrix products: 80.4 us -> 4.82 us  [nt(): lax.dot_general(left, right, (((1,), (1,)), ((), ())), preferred_element_...]
    ppermute x63 -> x23, starting transfers between devices: 101 us -> 42.9 us  [from_partner(): lax.ppermute(x, axis, [(i, i ^ 1 << bit) for i in range(lax.axis_size(axi...]
    convert_element_type x60 -> x0, other arithmetic: 55.7 us -> none  [the longest x59 54.8 us: low(): return values.astype(jnp.bfloat16)]
    pallas_call x1, Pallas kernels: 105 us -> 63.3 us  [self_forward(): pl.pallas_call(functools.partial(self_forward_kernel, tq, tk, pairs), out...]
    dot_general x4 -> x0, local copies, waits for them, and re-layouts: 28 us -> none  [tn(): lax.dot_general(left, right, (((0,), (0,)), ((), ())), preferred_element_...]
  transfers between devices with their start and end apart: 67 -> 31, of which waited for: 42 -> 11; matrix products, arithmetic and copies ran while one was open for 19% -> 8% of each run, Pallas kernels for 25% -> 41%
where the time goes in v2:
time: 588 us; the launch traced here: 584 us
  Pallas kernels  403 us (69%)
  starting transfers between devices  57.2 us (10%)
  waiting for transfers between devices  39.7 us (7%)
  local copies, waits for them, and re-layouts  38.4 us (7%)
  other arithmetic  25.9 us (4%)
  between operations  15 us (3%)
    pallas_call x1, Pallas kernels, middle(): pl.pallas_call(middle_kernel, out_shape=[jax.ShapeDtypeStruct((micro, row...  163 us
    pallas_call x3, Pallas kernels, self_backward(): pl.pallas_call(functools.partial(self_backward_kernel, number, tq, tk, pa...  144 us
    pallas_call x1, Pallas kernels, self_forward(): pl.pallas_call(functools.partial(self_forward_kernel, tq, tk, pairs), out...  63.3 us
    ppermute x23, starting transfers between devices, from_partner(): lax.ppermute(x, axis, [(i, i ^ 1 << bit) for i in range(lax.axis_size(axi...  42.9 us
    ppermute x23, waiting for transfers between devices, from_partner(): lax.ppermute(x, axis, [(i, i ^ 1 << bit) for i in range(lax.axis_size(axi...  39.6 us
    pallas_call x3, Pallas kernels, input_gradient(): pl.pallas_call(input_grad_kernel, out_shape=jax.ShapeDtypeStruct((micro,...  17.3 us
    pallas_call x1, Pallas kernels, project(): pl.pallas_call(project_kernel, out_shape=(tall(width), long, tall(2 * wid...  15 us
    unnamed x57, local copies, waits for them, and re-layouts  14.1 us
  transfers between devices with their start and end apart: 31, of which 11 were waited for; matrix products, arithmetic and copies ran while one was open for 8% of the time, Pallas kernels for 41%

profile of v2, /device:TPU:0, one launch (start us, length us, event | category | flops | bytes accessed | tf_op | source)
XLA Modules:
  0.0 584.2 jit_solution(12082305524171029500)
XLA Ops:
  15.9 4.1 collective-permute-start.1
  24.1 3.9 collective-permute-done.2
  29.6 6.2 %collective-permute-done.3 = bf16[2,2,1,1,1,16,1536]{6,5,0,1,2,4,3:T(8,128)(2,1)S(1)} collective-permute-done((bf16[2,2,1,1,1,16,1536]{6,5,0,1,2,4,3:T(8,128)(2,1)S(1)}, bf16[2,2,1,1,1,16,1536]{6,5,0,1,2,4,3:T(8,128)(2,1)S(1)}, u32[]{:S(2)}, u32[]{:S(2)}) %collective-permute-start.3) | collective-permute-done | bytes 196640 | tf_op jit(solution)/shard_map/ppermute | solution.py:48
  37.5 10.2 %collective-permute-done.4 = bf16[2,2,2,1,1,16,1536]{6,5,0,1,2,4,3:T(8,128)(2,1)S(1)} collective-permute-done((bf16[2,2,2,1,1,16,1536]{6,5,0,1,2,4,3:T(8,128)(2,1)S(1)}, bf16[2,2,2,1,1,16,1536]{6,5,0,1,2,4,3:T(8,128)(2,1)S(1)}, u32[]{:S(2)}, u32[]{:S(2)}) %collective-permute-start.4) | collective-permute-done | bytes 393248 | tf_op jit(solution)/shard_map/ppermute | solution.py:48
  56.3 15.0 %project.1 = (bf16[3,512,1024]{2,1,0:T(8,128)(2,1)}, bf16[3,1024,1024]{2,1,0:T(8,128)(2,1)}, bf16[3,1024,1024]{2,1,0:T(8,128)(2,1)}, bf16[3,1024,1024]{2,1,0:T(8,128)(2,1)}, bf16[3,1024,1024]{2,1,0:T(8,128)(2,1)}) custom-call(bf16[3,1024,512]{2,1,0:T(8,128)(2,1)} %x_ref.4, bf16[3,1024,512]{2,1,0:T(8,128)(2,1)} %copy-done, bf16[512,1536]{1,0:T(8,128)(2,1)} %bitcast.96), custom_call_target="tpu_custom_call" | custom-call | flops 8053063680 | bytes 34603008 | tf_op jit(solution)/shard_map/project/pallas_call | solution.py:168
  71.3 63.3 %self_forward.1 = (f32[3,512,1024]{2,1,0:T(8,128)}, f32[3,8,1024]{2,1,0:T(8,128)}) custom-call(s32[3,4,3]{2,1,0:T(4,128)} %pad_add_fusion.1.tiles, bf16[3,512,1024]{2,1,0:T(8,128)(2,1)} %get-tuple-element.76.qt_ref, bf16[3,1024,1024]{2,1,0:T(8,128)(2,1)} %get-tuple-element.77.kp_ref.vp_ref, bf16[3,1024,1024]{2,1,0:T(8,128)(2,1)} %get-tuple-element.78.kl_ref.vl_ref, ...), custom_call_target="tpu_custom_call" | custom-call | flops 6442450944 | bytes 25165824 | tf_op jit(solution)/shard_map/self_forward/pallas_call | solution.py:268
  134.7 163.4 %middle.1 = (bf16[3,1024,512]{2,1,0:T(8,128)(2,1)}, bf16[3,512,1024]{2,1,0:T(8,128)(2,1)}, f32[3,8,1024]{2,1,0:T(8,128)}, f32[3,1024,512]{2,1,0:T(8,128)}, f32[3...) custom-call(bf16[3,1024,512]{2,1,0:T(8,128)(2,1)} %x_ref.4, ...), custom_call_target="tpu_custom_call" | custom-call | flops 72477573120 | bytes 70778880 | tf_op jit(solution)/shard_map/middle/pallas_call | solution.py:776
  298.0 3.3 dynamic-slice_convert_fusion.1
  304.7 51.2 %self_backward.3 = (bf16[1,512,1024]{2,1,0:T(8,128)(2,1)}, bf16[1,1024,512]{2,1,0:T(8,128)(2,1)}, bf16[1,1024,512]{2,1,0:T(8,128)(2,1)}, bf16[1,1024,512]{2,1,0:...) custom-call(s32[3,4,3]{2,1,0:T(4,128)} %pad_add_fusion.1.tiles, ...), custom_call_target="tpu_custom_call" | custom-call | flops 5368709120 | bytes 20971520 | tf_op jit(solution)/shard_map/self_backward/pallas_call | solution.py:411
  360.7 3.0 convert_add_fusion.1
  373.4 5.7 input_gradient.3.rest_0_
  379.2 11.5 %collective-permute-start.10 = (bf16[2,2,1,2,1,16,3712]{6,5,4,3,2,1,0:T(8,128)(2,1)}, bf16[2,2,1,2,1,16,3712]{6,5,4,3,2,1,0:T(8,128)(2,1)}, u32[]{:S(2)}, u32[]{:S(2)}) collective-permute-start(bf16[2,2,1,2,1,16,3712]{6,5,4,3,2,1,0:T(8,128)(2,1)} %dynamic-slice_convert_fusion.2), channel_id=1, source_target_pairs={{0,4},{1,5},{2,6},{3,7},{4,0},{5,1},{6,2},{7,3},{8,12},{9,13},{10,... | collective-permute-start | bytes 2850824 | tf_op jit(solution)/shard_map/ppermute | solution.py:48
  390.7 45.3 %self_backward.4 = (bf16[1,512,1024]{2,1,0:T(8,128)(2,1)}, bf16[1,1024,512]{2,1,0:T(8,128)(2,1)}, bf16[1,1024,512]{2,1,0:T(8,128)(2,1)}, bf16[1,1024,512]{2,1,0:...) custom-call(s32[3,4,3]{2,1,0:T(4,128)} %pad_add_fusion.1.tiles, ...), custom_call_target="tpu_custom_call" | custom-call | flops 5368709120 | bytes 20971520 | tf_op jit(solution)/shard_map/self_backward/pallas_call | solution.py:411
  446.4 9.8 %collective-permute-start.24 = (bf16[2,2,1,1,1,16,3072]{6,5,4,3,2,1,0:T(8,128)(2,1)}, bf16[2,2,1,1,1,16,3072]{6,5,4,3,2,1,0:T(8,128)(2,1)S(1)}, u32[]{:S(2)}, u32[]{:S(2)}) collective-permute-start(bf16[2,2,1,1,1,16,3072]{6,5,4,3,2,1,0:T(8,128)(2,1)} %dynamic-slice_convert_fusion.7), channel_id=1, source_target_pairs={{0,4},{1,5},{2,6},{3,7},{4,0},{5,1},{6,2},{7,3},{8,12},{9,13},{10,... | collective-permute-start | bytes 1179656 | tf_op jit(solution)/shard_map/ppermute | solution.py:48
  456.2 47.7 %self_backward.5 = (bf16[1,512,1024]{2,1,0:T(8,128)(2,1)}, bf16[1,1024,512]{2,1,0:T(8,128)(2,1)}, bf16[1,1024,512]{2,1,0:T(8,128)(2,1)}, bf16[1,1024,512]{2,1,0:...) custom-call(s32[3,4,3]{2,1,0:T(4,128)} %pad_add_fusion.1.tiles, ...), custom_call_target="tpu_custom_call" | custom-call | flops 5368709120 | bytes 20971520 | tf_op jit(solution)/shard_map/self_backward/pallas_call | solution.py:411
  503.8 4.8 add_add_fusion
  509.6 3.4 collective-permute-start.11
  515.3 5.8 input_gradient.4.rest_0_
  523.8 3.2 collective-permute-done.25
  528.6 5.2 collective-permute-done.26
  552.1 6.0 %collective-permute-start.21 = (bf16[2,2,1,1,1,16,1536]{6,5,4,3,2,1,0:T(8,128)(2,1)S(1)}, bf16[2,2,1,1,1,16,1536]{6,5,4,3,2,1,0:T(8,128)(2,1)S(1)}, u32[]{:S(2)}, u32[]{:S(2)}) collective-permute-start(bf16[2,2,1,1,1,16,1536]{6,5,4,3,2,1,0:T(8,128)(2,1)S(1)} %dynamic-slice_convert_fusion.10), channel_id=1, source_target_pairs={{0,4},{1,5},{2,6},{3,7},{4,0},{5,1},{6,2},{7,3},{8,12},{9,13},{10,... | collective-permute-start | bytes 589832 | tf_op jit(solution)/shard_map/ppermute | solution.py:48
  558.0 3.6 collective-permute-done.21
  563.0 3.4 collective-permute-done.22
  569.5 5.7 input_gradient.5
  (197 shorter events, 84.3 us)
Async XLA Ops:
  7.2 127.4 %all-gather.2.cloned.1.call-start = ((), (), s32[]{:S(2)}) async-start(), calls=%async_computation | async-start | bytes 7163904 | tf_op jit(solution)/shard_map/all_gather | solution.py:926
  20.0 114.7 %collective-permute-start.6 = (bf16[3,256,512]{2,1,0:T(8,128)(2,1)}, bf16[3,256,512]{2,1,0:T(8,128)(2,1)}, u32[]{:S(2)}, u32[]{:S(2)}) collective-permute-start(bf16[3,256,512]{2,1,0:T(8,128)(2,1)} %mem_ref), channel_id=1, source_target_pairs={{0,1},{1,0},{2,3},{3,2},{4,5},{5,4},{6,7},{7,6},{8,9},{9,8},{10,11... | collective-permute-start | bytes 2359304 | tf_op jit(solution)/shard_map/ppermute | solution.py:48
  20.0 34.7 %collective-permute-start = (bf16[3,1024,512]{2,1,0:T(8,128)(2,1)}, bf16[3,1024,512]{2,1,0:T(8,128)(2,1)S(1)}, u32[]{:S(2)}, u32[]{:S(2)}) collective-permute-start(bf16[3,1024,512]{2,1,0:T(8,128)(2,1)} %x_ref.4), channel_id=1, source_target_pairs={{1,0},{3,2},{5,4},{7,6},{9,8},{11,10},{13,12},{15,14},{17,16},{19,... | collective-permute-start | bytes 9437192 | tf_op jit(solution)/shard_map/ppermute | solution.py:52
  28.0 7.8 %collective-permute-start.3 = (bf16[2,2,1,1,1,16,1536]{6,5,0,1,2,4,3:T(8,128)(2,1)S(1)}, bf16[2,2,1,1,1,16,1536]{6,5,0,1,2,4,3:T(8,128)(2,1)S(1)}, u32[]{:S(2)}, u32[]{:S(2)}) collective-permute-start(bf16[2,2,1,1,1,16,1536]{6,5,0,1,2,4,3:T(8,128)(2,1)S(1)} %maximum_select_fusion.4), channel_id=1, source_target_pairs={{0,4},{1,5},{2,6},{3,7},{4,0},{5,1},{6,2},{7,3},{8,12},{9,13},{10,... | collective-permute-start | bytes 589832 | tf_op jit(solution)/shard_map/ppermute | solution.py:48
  35.9 11.7 %collective-permute-start.4 = (bf16[2,2,2,1,1,16,1536]{6,5,0,1,2,4,3:T(8,128)(2,1)S(1)}, bf16[2,2,2,1,1,16,1536]{6,5,0,1,2,4,3:T(8,128)(2,1)S(1)}, u32[]{:S(2)}, u32[]{:S(2)}) collective-permute-start(bf16[2,2,2,1,1,16,1536]{6,5,0,1,2,4,3:T(8,128)(2,1)S(1)} %maximum_select_fusion.2), channel_id=1, source_target_pairs={{0,2},{1,3},{2,0},{3,1},{4,6},{5,7},{6,4},{7,5},{8,10},{9,11},{10,... | collective-permute-start | bytes 1179656 | tf_op jit(solution)/shard_map/ppermute | solution.py:48
  303.6 57.1 %collective-permute-start.7 = (bf16[2,2,2,2,1,16,3072]{6,5,4,3,2,1,0:T(8,128)(2,1)}, bf16[2,2,2,2,1,16,3072]{6,5,4,3,2,1,0:T(8,128)(2,1)}, u32[]{:S(2)}, u32[]{:S(2)}) collective-permute-start(bf16[2,2,2,2,1,16,3072]{6,5,4,3,2,1,0:T(8,128)(2,1)} %dynamic-slice_convert_fusion.1), channel_id=1, source_target_pairs={{0,1},{1,0},{2,3},{3,2},{4,5},{5,4},{6,7},{7,6},{8,9},{9,8},{10,11... | collective-permute-start | bytes 4718600 | tf_op jit(solution)/shard_map/ppermute | solution.py:48
  303.7 53.6 %collective-permute-start.18 = (bf16[3,256,512]{2,1,0:T(8,128)(2,1)}, bf16[3,256,512]{2,1,0:T(8,128)(2,1)}, u32[]{:S(2)}, u32[]{:S(2)}) collective-permute-start(bf16[3,256,512]{2,1,0:T(8,128)(2,1)} %get-tuple-element.126), channel_id=1, source_target_pairs={{0,1},{1,0},{2,3},{3,2},{4,5},{5,4},{6,7},{7,6},{8,9},{9,8},{10,11... | collective-permute-start | bytes 2359304 | tf_op jit(solution)/shard_map/ppermute | solution.py:48
  304.2 64.4 %collective-permute-start.17 = (bf16[3,256,512]{2,1,0:T(8,128)(2,1)}, bf16[3,256,512]{2,1,0:T(8,128)(2,1)}, u32[]{:S(2)}, u32[]{:S(2)}) collective-permute-start(bf16[3,256,512]{2,1,0:T(8,128)(2,1)} %get-tuple-element.124), channel_id=1, source_target_pairs={{0,1},{1,0},{2,3},{3,2},{4,5},{5,4},{6,7},{7,6},{8,9},{9,8},{10,11... | collective-permute-start | bytes 2359304 | tf_op jit(solution)/shard_map/ppermute | solution.py:48
  304.3 61.3 %collective-permute-start.8 = (bf16[2,2,2,2,1,16,3712]{6,5,4,3,2,1,0:T(8,128)(2,1)S(1)}, bf16[2,2,2,2,1,16,3712]{6,5,4,3,2,1,0:T(8,128)(2,1)}, u32[]{:S(2)}, u32[]{:S(2)}) collective-permute-start(bf16[2,2,2,2,1,16,3712]{6,5,4,3,2,1,0:T(8,128)(2,1)S(1)} %dynamic-slice_convert_fusion), channel_id=1, source_target_pairs={{0,1},{1,0},{2,3},{3,2},{4,5},{5,4},{6,7},{7,6},{8,9},{9,8},{10,11... | collective-permute-start | bytes 5701640 | tf_op jit(solution)/shard_map/ppermute | solution.py:48
  355.9 16.2 %collective-permute-start.15 = (bf16[1,1024,512]{2,1,0:T(8,128)(2,1)}, bf16[1,1024,512]{2,1,0:T(8,128)(2,1)S(1)}, u32[]{:S(2)}, u32[]{:S(2)}) collective-permute-start(bf16[1,1024,512]{2,1,0:T(8,128)(2,1)} %get-tuple-element.121), channel_id=1, source_target_pairs={{0,1},{2,3},{4,5},{6,7},{8,9},{10,11},{12,13},{14,15},{16,17},{18,... | collective-permute-start | bytes 3145736 | tf_op jit(solution)/shard_map/ppermute | solution.py:56
  357.3 14.8 %collective-permute-start.16 = (bf16[1,1024,512]{2,1,0:T(8,128)(2,1)}, bf16[1,1024,512]{2,1,0:T(8,128)(2,1)S(1)}, u32[]{:S(2)}, u32[]{:S(2)}) collective-permute-start(bf16[1,1024,512]{2,1,0:T(8,128)(2,1)} %get-tuple-element.122), channel_id=1, source_target_pairs={{0,1},{2,3},{4,5},{6,7},{8,9},{10,11},{12,13},{14,15},{16,17},{18,... | collective-permute-start | bytes 3145736 | tf_op jit(solution)/shard_map/ppermute | solution.py:56
  368.6 72.0 %collective-permute-start.9 = (bf16[2,2,2,1,1,16,3072]{6,5,4,3,2,1,0:T(8,128)(2,1)}, bf16[2,2,2,1,1,16,3072]{6,5,4,3,2,1,0:T(8,128)(2,1)}, u32[]{:S(2)}, u32[]{:S(2)}) collective-permute-start(bf16[2,2,2,1,1,16,3072]{6,5,4,3,2,1,0:T(8,128)(2,1)} %dynamic-slice_convert_fusion.4), channel_id=1, source_target_pairs={{0,2},{1,3},{2,0},{3,1},{4,6},{5,7},{6,4},{7,5},{8,10},{9,11},{10,... | collective-permute-start | bytes 2359304 | tf_op jit(solution)/shard_map/ppermute | solution.py:48
  379.2 64.6 %collective-permute-start.10 = (bf16[2,2,1,2,1,16,3712]{6,5,4,3,2,1,0:T(8,128)(2,1)}, bf16[2,2,1,2,1,16,3712]{6,5,4,3,2,1,0:T(8,128)(2,1)}, u32[]{:S(2)}, u32[]{:S(2)}) collective-permute-start(bf16[2,2,1,2,1,16,3712]{6,5,4,3,2,1,0:T(8,128)(2,1)} %dynamic-slice_convert_fusion.2), channel_id=1, source_target_pairs={{0,4},{1,5},{2,6},{3,7},{4,0},{5,1},{6,2},{7,3},{8,12},{9,13},{10,... | collective-permute-start | bytes 2850824 | tf_op jit(solution)/shard_map/ppermute | solution.py:48
  436.0 73.5 %collective-permute-start.13 = (bf16[1,1024,512]{2,1,0:T(8,128)(2,1)}, bf16[1,1024,512]{2,1,0:T(8,128)(2,1)}, u32[]{:S(2)}, u32[]{:S(2)}) collective-permute-start(bf16[1,1024,512]{2,1,0:T(8,128)(2,1)} %get-tuple-element.117), channel_id=1, source_target_pairs={{0,1},{2,3},{4,5},{6,7},{8,9},{10,11},{12,13},{14,15},{16,17},{18,... | collective-permute-start | bytes 3145736 | tf_op jit(solution)/shard_map/ppermute | solution.py:56
  438.3 74.7 %collective-permute-start.14 = (bf16[1,1024,512]{2,1,0:T(8,128)(2,1)}, bf16[1,1024,512]{2,1,0:T(8,128)(2,1)}, u32[]{:S(2)}, u32[]{:S(2)}) collective-permute-start(bf16[1,1024,512]{2,1,0:T(8,128)(2,1)} %get-tuple-element.118), channel_id=1, source_target_pairs={{0,1},{2,3},{4,5},{6,7},{8,9},{10,11},{12,13},{14,15},{16,17},{18,... | collective-permute-start | bytes 3145736 | tf_op jit(solution)/shard_map/ppermute | solution.py:56
  446.4 74.8 %collective-permute-start.24 = (bf16[2,2,1,1,1,16,3072]{6,5,4,3,2,1,0:T(8,128)(2,1)}, bf16[2,2,1,1,1,16,3072]{6,5,4,3,2,1,0:T(8,128)(2,1)S(1)}, u32[]{:S(2)}, u32[]{:S(2)}) collective-permute-start(bf16[2,2,1,1,1,16,3072]{6,5,4,3,2,1,0:T(8,128)(2,1)} %dynamic-slice_convert_fusion.7), channel_id=1, source_target_pairs={{0,4},{1,5},{2,6},{3,7},{4,0},{5,1},{6,2},{7,3},{8,12},{9,13},{10,... | collective-permute-start | bytes 1179656 | tf_op jit(solution)/shard_map/ppermute | solution.py:48
  456.2 65.2 %collective-permute-start.27 = (bf16[2,2,1,1,1,16,3712]{6,5,4,3,2,1,0:T(8,128)(2,1)S(1)}, bf16[2,2,1,1,1,16,3712]{6,5,4,3,2,1,0:T(8,128)(2,1)}, u32[]{:S(2)}, u32[]{:S(2)}) collective-permute-start(bf16[2,2,1,1,1,16,3712]{6,5,4,3,2,1,0:T(8,128)(2,1)S(1)} %dynamic-slice_convert_fusion.5), channel_id=1, source_target_pairs={{0,2},{1,3},{2,0},{3,1},{4,6},{5,7},{6,4},{7,5},{8,10},{9,11},{10,... | collective-permute-start | bytes 1425416 | tf_op jit(solution)/shard_map/ppermute | solution.py:48
  509.6 30.8 %collective-permute-start.19 = (bf16[2,2,2,2,1,16,1536]{6,5,4,3,2,1,0:T(8,128)(2,1)}, bf16[2,2,2,2,1,16,1536]{6,5,4,3,2,1,0:T(8,128)(2,1)}, u32[]{:S(2)}, u32[]{:S(2)}) collective-permute-start(bf16[2,2,2,2,1,16,1536]{6,5,4,3,2,1,0:T(8,128)(2,1)} %dynamic-slice_convert_fusion.3), channel_id=1, source_target_pairs={{0,1},{1,0},{2,3},{3,2},{4,5},{5,4},{6,7},{7,6},{8,9},{9,8},{10,11... | collective-permute-start | bytes 2359304 | tf_op jit(solution)/shard_map/ppermute | solution.py:48
  509.6 59.9 %collective-permute-start.11 = (bf16[1,1024,512]{2,1,0:T(8,128)(2,1)}, bf16[1,1024,512]{2,1,0:T(8,128)(2,1)}, u32[]{:S(2)}, u32[]{:S(2)}) collective-permute-start(bf16[1,1024,512]{2,1,0:T(8,128)(2,1)} %get-tuple-element.112), channel_id=1, source_target_pairs={{0,1},{2,3},{4,5},{6,7},{8,9},{10,11},{12,13},{14,15},{16,17},{18,... | collective-permute-start | bytes 3145736 | tf_op jit(solution)/shard_map/ppermute | solution.py:56
  513.0 56.4 %collective-permute-start.12 = (bf16[1,1024,512]{2,1,0:T(8,128)(2,1)}, bf16[1,1024,512]{2,1,0:T(8,128)(2,1)}, u32[]{:S(2)}, u32[]{:S(2)}) collective-permute-start(bf16[1,1024,512]{2,1,0:T(8,128)(2,1)} %get-tuple-element.113), channel_id=1, source_target_pairs={{0,1},{2,3},{4,5},{6,7},{8,9},{10,11},{12,13},{14,15},{16,17},{18,... | collective-permute-start | bytes 3145736 | tf_op jit(solution)/shard_map/ppermute | solution.py:56
  527.9 11.1 %collective-permute-start.28 = (bf16[2,1,1,1,1,16,3712]{6,5,4,3,2,1,0:T(8,128)(2,1)}, bf16[2,1,1,1,1,16,3712]{6,5,4,3,2,1,0:T(8,128)(2,1)}, u32[]{:S(2)}, u32[]{:S(2)}) collective-permute-start(bf16[2,1,1,1,1,16,3712]{6,5,4,3,2,1,0:T(8,128)(2,1)} %dynamic-slice_convert_fusion.8), channel_id=1, source_target_pairs={{0,8},{1,9},{2,10},{3,11},{4,12},{5,13},{6,14},{7,15},{8,0},{9,1},... | collective-permute-start | bytes 712712 | tf_op jit(solution)/shard_map/ppermute | solution.py:48
  542.9 7.8 %collective-permute-start.20 = (bf16[2,2,2,1,1,16,1536]{6,5,4,3,2,1,0:T(8,128)(2,1)S(1)}, bf16[2,2,2,1,1,16,1536]{6,5,4,3,2,1,0:T(8,128)(2,1)S(1)}, u32[]{:S(2)}, u32[]{:S(2)}) collective-permute-start(bf16[2,2,2,1,1,16,1536]{6,5,4,3,2,1,0:T(8,128)(2,1)S(1)} %dynamic-slice_convert_fusion.6), channel_id=1, source_target_pairs={{0,2},{1,3},{2,0},{3,1},{4,6},{5,7},{6,4},{7,5},{8,10},{9,11},{10,... | collective-permute-start | bytes 1179656 | tf_op jit(solution)/shard_map/ppermute | solution.py:48
  552.1 9.6 %collective-permute-start.21 = (bf16[2,2,1,1,1,16,1536]{6,5,4,3,2,1,0:T(8,128)(2,1)S(1)}, bf16[2,2,1,1,1,16,1536]{6,5,4,3,2,1,0:T(8,128)(2,1)S(1)}, u32[]{:S(2)}, u32[]{:S(2)}) collective-permute-start(bf16[2,2,1,1,1,16,1536]{6,5,4,3,2,1,0:T(8,128)(2,1)S(1)} %dynamic-slice_convert_fusion.10), channel_id=1, source_target_pairs={{0,4},{1,5},{2,6},{3,7},{4,0},{5,1},{6,2},{7,3},{8,12},{9,13},{10,... | collective-permute-start | bytes 589832 | tf_op jit(solution)/shard_map/ppermute | solution.py:48
  566.5 8.7 %collective-permute-start.23 = (bf16[1,1,1,1,1,16,1536]{6,5,4,3,2,1,0:T(8,128)(2,1)S(1)}, bf16[1,1,1,1,1,16,1536]{6,5,4,3,2,1,0:T(8,128)(2,1)S(1)}, u32[]{:S(2)}, u32[]{:S(2)}) collective-permute-start(bf16[1,1,1,1,1,16,1536]{6,5,4,3,2,1,0:T(8,128)(2,1)S(1)} %dynamic-slice_convert_fusion.14), channel_id=1, source_target_pairs={{0,16},{1,17},{2,18},{3,19},{4,20},{5,21},{6,22},{7,23},{8,24},{9,... | collective-permute-start | bytes 147464 | tf_op jit(solution)/shard_map/ppermute | solution.py:48
  (28 other events, 185.9 us)
Sparse Core Ops, SparseCore 0:
  16.0 74.9 all-gather.1

commit v3 on v2

--- a/solution.py
+++ b/solution.py
@@ -40,8 +40,9 @@
     return values.astype(jnp.float32)
 
 
-def bit_count(axis):
-    return (lax.axis_size(axis) - 1).bit_length()
+def stages_of(axis):
+    bits = (lax.axis_size(axis) - 1).bit_length()
+    return [(0, 1)] + [(bit, min(2, bits - bit)) for bit in range(1, bits, 2)]
 
 
 def from_partner(x, axis, bit):
@@ -56,74 +57,62 @@
     return lax.ppermute(x, axis, [(i, i + 1) for i in range(0, lax.axis_size(axis), 2)])
 
 
+def shifted(x, axis, offset):
+    return lax.ppermute(x, axis, [(i, i ^ offset) for i in range(lax.axis_size(axis))])
+
+
 def tree_gather(x, axis):
-    bits = bit_count(axis)
+    stages = stages_of(axis)
     me = lax.axis_index(axis)
-    block = x.reshape((1,) * bits + x.shape)
-    for bit in list(range(bits - 1, 0, -1)) + [0]:
-        dim = bits - 1 - bit
-        got = from_partner(block, axis, bit)
-        block = jnp.where(
-            (me >> bit) & 1 == 1,
-            jnp.concatenate([got, block], dim),
-            jnp.concatenate([block, got], dim),
-        )
+    block = x.reshape((1,) * len(stages) + x.shape)
+    for number in reversed(range(len(stages))):
+        bit, count = stages[number]
+        dim = len(stages) - 1 - number
+        place = (me >> bit) & ((1 << count) - 1)
+        parts = [block] + [shifted(block, axis, k << bit) for k in range(1, 1 << count)]
+        out = []
+        for spot in range(1 << count):
+            piece = parts[spot]
+            for mine in range(1, 1 << count):
+                piece = jnp.where(place == mine, parts[spot ^ mine], piece)
+            out.append(piece)
+        block = jnp.concatenate(out, dim)
     return block.reshape((-1,) + x.shape[1:])
 
 
 class TreeScatter:
-    def __init__(self, arrays, orders, axis):
+    def __init__(self, array, axis):
         self.axis = axis
-        self.bits = bit_count(axis)
+        self.stages = stages_of(axis)
         self.me = lax.axis_index(axis)
-        self.blocks, self.orders, self.steps, self.shapes = [], [], [], []
-        self.coming = {}
-        self.join(arrays, orders)
-
-    def join(self, arrays, orders):
-        size = lax.axis_size(self.axis)
-        plain = list(range(self.bits))
-        turned = plain[:1] + plain[1:3][::-1] + plain[3:]
-        for array, order in zip(arrays, orders):
-            own = (array.shape[0] // size,) + array.shape[1:]
-            self.blocks.append(array.reshape((2,) * self.bits + own))
-            self.orders.append((plain, turned)[order])
-            self.steps.append(0)
-            self.shapes.append(own)
-
-    def halves(self, number):
-        bit = self.orders[number][self.steps[number]]
-        dim = self.bits - 1 - bit
-        mine = (self.me >> bit) & 1
-        block = self.blocks[number]
-        keep = lax.dynamic_index_in_dim(block, mine, dim, keepdims=True)
-        away = lax.dynamic_index_in_dim(block, 1 - mine, dim, keepdims=True)
-        return bit, keep, low(away)
+        self.own = (array.shape[0] // lax.axis_size(axis),) + array.shape[1:]
+        sizes = tuple(1 << count for _, count in reversed(self.stages))
+        self.block = array.reshape(sizes + self.own)
+        self.number = 0
 
     def send(self, after=None):
-        live = [n for n in range(len(self.blocks)) if self.steps[n] < self.bits]
-        parts = {n: self.halves(n) for n in live}
-        aways = [parts[n][2] for n in live]
+        bit, count = self.stages[self.number]
+        dim = len(self.stages) - 1 - self.number
+        place = (self.me >> bit) & ((1 << count) - 1)
+        pick = lambda k: lax.dynamic_index_in_dim(self.block, place ^ k, dim, keepdims=True)
+        aways = [low(pick(k)) for k in range(1, 1 << count)]
         if after is not None:
             after, aways = lax.optimization_barrier((after, aways))
-        for n, away in zip(live, aways):
-            bit, keep, _ = parts[n]
-            self.coming[n] = (keep, from_partner(away, self.axis, bit))
-        return after, live
+        self.keep = pick(0)
+        self.got = [shifted(a, self.axis, k << bit) for k, a in enumerate(aways, 1)]
+        return after
 
     def receive(self, behind=None):
-        for n, (keep, got) in self.coming.items():
-            if behind is not None:
-                got, _ = lax.optimization_barrier((got, behind))
-            self.blocks[n] = wide(keep) + wide(got)
-            self.steps[n] += 1
-        self.coming = {}
+        if behind is not None:
+            self.got, _ = lax.optimization_barrier((self.got, behind))
+        self.block = sum([wide(g) for g in self.got], self.keep)
+        self.number += 1
 
     def finish(self):
-        while any(step < self.bits for step in self.steps):
+        while self.number < len(self.stages):
             self.send()
             self.receive()
-        return [wide(b.reshape(own)) for b, own in zip(self.blocks, self.shapes)]
+        return self.block.reshape(self.own)
 
 
 def tall_sum(values):
@@ -186,7 +175,7 @@
 
 
 def self_forward_kernel(
-    tq, tk, pairs, tiles, qt_ref, kp_ref, kl_ref, vtp_ref, vtl_ref, lim_ref, ot_ref, lse_ref, s_ref
+    tq, tk, pairs, tiles, qt_ref, kp_ref, kl_ref, vtp_ref, vtl_ref, lim_ref, ot_ref, lse_ref, s_ref, e_ref
 ):
     micro, tile = pl.program_id(0), pl.program_id(1)
     prefix_rows = kp_ref.shape[1]
@@ -204,6 +193,7 @@
     def local_mask(j):
         return (key_at <= rows - j * tk) & (key_at >= start - j * tk)
 
+    ot_ref[0] = jnp.zeros((ot_ref.shape[1], tq), jnp.float32)
     for group in range(HEADS // heads):
         queries = []
         for h in range(heads):
@@ -239,27 +229,27 @@
             base = pl.multiple_of(j * tk, tk)
             out = []
             for h in range(heads):
-                head = group * heads + h
                 e = jnp.exp(
                     s_ref[h, pl.ds(pl.multiple_of(offset + base, tk), tk), :] - tops[h]
                 )
-                total, mixed = carry[2 * h], carry[2 * h + 1]
-                out.append(total + tall_sum(e))
-                out.append(
-                    mixed
-                    + nn(vt_ref[0, head * size : (head + 1) * size, pl.ds(base, tk)], low(e))
-                )
+                out.append(carry[h] + tall_sum(e))
+                e_ref[h] = low(e)
+            for h in range(heads):
+                head = group * heads + h
+                part = slice(head * size, (head + 1) * size)
+                ot_ref[0, part, :] += nn(vt_ref[0, part, pl.ds(base, tk)], e_ref[h])
             return tuple(out)
 
-        carry = (jnp.zeros((8, tq), jnp.float32), jnp.zeros((size, tq), jnp.float32)) * heads
+        carry = (jnp.zeros((8, tq), jnp.float32),) * heads
         carry = lax.fori_loop(0, prefix_tiles, functools.partial(mix, vtp_ref, 0), carry)
         carry = lax.fori_loop(
             local_first, local_end, functools.partial(mix, vtl_ref, prefix_rows), carry
         )
         for h in range(heads):
             head = group * heads + h
-            total = jnp.sum(carry[2 * h], axis=0, keepdims=True)
-            ot_ref[0, head * size : (head + 1) * size, :] = carry[2 * h + 1] / total
+            total = jnp.sum(carry[h], axis=0, keepdims=True)
+            part = slice(head * size, (head + 1) * size)
+            ot_ref[0, part, :] = ot_ref[0, part, :] / total
             lse_ref[0, head : head + 1, :] = tops[h] + jnp.log(total)
 
 
@@ -286,7 +276,10 @@
                 pl.BlockSpec((1, width, tq), lambda m, i, s: (m, 0, i)),
                 pl.BlockSpec((1, HEADS, tq), lambda m, i, s: (m, 0, i)),
             ],
-            scratch_shapes=[pltpu.VMEM((2 * pairs, 2 * rows, tq), jnp.float32)],
+            scratch_shapes=[
+                pltpu.VMEM((2 * pairs, 2 * rows, tq), jnp.float32),
+                pltpu.VMEM((2 * pairs, tk, tq), jnp.bfloat16),
+            ],
         ),
         compiler_params=pltpu.CompilerParams(vmem_limit_bytes=VMEM_LIMIT),
         cost_estimate=pl.CostEstimate(
@@ -299,7 +292,6 @@
 
 
 def self_backward_kernel(
-    micro,
     tq,
     tk,
     pairs,
@@ -328,9 +320,19 @@
     sum_kl,
     sum_vl,
     sum_q,
+    s_ref,
+    dp_ref,
+    p_ref,
+    ds_ref,
 ):
+    micro = pl.program_id(0)
     row_count = qt_ref.shape[2]
     size = LANES // 2
+
+    @pl.when(micro == 0)
+    def _():
+        g_ref[...] = jnp.zeros_like(g_ref)
+
     for ref in (sum_kp, sum_vp, sum_kl, sum_vl):
         ref[...] = jnp.zeros_like(ref)
     key_at = lax.broadcasted_iota(jnp.int32, (tk, tq), 0)
@@ -352,19 +354,20 @@
         def body(k_ref, v_ref, kt_ref, sum_k, sum_v, masker, j, _):
             base = pl.multiple_of(j * tk, tk)
             seen = masker(j)
-            for k in range(pairs):
-                cols = slice(k * LANES, (k + 1) * LANES)
-                keys = k_ref[0, pl.ds(base, tk), cols]
-                values = v_ref[0, pl.ds(base, tk), cols]
-                for h in (2 * k, 2 * k + 1):
-                    s = jnp.where(seen, nn(keys, queries[h]), NEG)
-                    p = jnp.exp(s - totals[h])
-                    dp = nn(values, grads[h])
-                    sum_v[pl.ds(base, tk), cols] += nt(low(p), grads[h])
-                    ds = low(p * (dp - deltas[h]))
-                    sum_k[pl.ds(base, tk), cols] += nt(ds, queries[h])
-                    part = slice(h * size, (h + 1) * size)
-                    sum_q[part, :] += nn(kt_ref[0, part, pl.ds(base, tk)], ds)
+            heads = 2 * pairs
+            cols = [slice(h // 2 * LANES, (h // 2 + 1) * LANES) for h in range(heads)]
+            for h in range(heads):
+                s_ref[h] = nn(k_ref[0, pl.ds(base, tk), cols[h]], queries[h])
+                dp_ref[h] = nn(v_ref[0, pl.ds(base, tk), cols[h]], grads[h])
+            for h in range(heads):
+                p = jnp.exp(jnp.where(seen, s_ref[h], NEG) - totals[h])
+                p_ref[h] = low(p)
+                ds_ref[h] = low(p * (dp_ref[h] - deltas[h]))
+            for h in range(heads):
+                part = slice(h * size, (h + 1) * size)
+                sum_v[pl.ds(base, tk), cols[h]] += nt(p_ref[h], grads[h])
+                sum_k[pl.ds(base, tk), cols[h]] += nt(ds_ref[h], queries[h])
+                sum_q[part, :] += nn(kt_ref[0, part, pl.ds(base, tk)], ds_ref[h])
             return 0
 
         def prefix_mask(j):
@@ -392,26 +395,22 @@
     dvl_ref[0] = low(sum_vl[...])
     width = x_ref.shape[2]
     own, far = jnp.transpose(x_ref[0]), jnp.transpose(far_ref[0])
-    g_ref[:, :width] = nt(own, dqt_ref[0])
-    g_ref[:, width : 2 * width] = nn(own, dkl_ref[0]) + nn(far, dkp_ref[0])
-    g_ref[:, 2 * width :] = nn(own, dvl_ref[0]) + nn(far, dvp_ref[0])
-
-
-def self_backward(
-    number, qt, kv, kvt, far_kv, far_kvt, grad_out, lse, delta, limits, tiles, x, far_x
-):
+    g_ref[:, :width] += nt(own, dqt_ref[0])
+    g_ref[:, width : 2 * width] += nn(own, dkl_ref[0]) + nn(far, dkp_ref[0])
+    g_ref[:, 2 * width :] += nn(own, dvl_ref[0]) + nn(far, dvp_ref[0])
+
+
+def self_backward(qt, kv, kvt, far_kv, far_kvt, grad_out, lse, delta, limits, tiles, x, far_x):
     tq, tk, pairs = 256, 256, HEADS // 2
     micro, width, rows = qt.shape
-    tall = pl.BlockSpec((1, width, rows), lambda i, s: (number, 0, 0))
-    long = lambda place: pl.BlockSpec((1, rows, width), lambda i, s: (number, 0, place))
-    line = pl.BlockSpec((1, 1, HEADS, rows), lambda i, s: (number, 0, 0, 0))
-    tall_out = pl.BlockSpec((1, width, rows), lambda i, s: (0, 0, 0))
-    long_out = pl.BlockSpec((1, rows, width), lambda i, s: (0, 0, 0))
-    bf16 = jax.ShapeDtypeStruct((1, rows, width), jnp.bfloat16)
+    tall = pl.BlockSpec((1, width, rows), lambda m, s: (m, 0, 0))
+    long = lambda place: pl.BlockSpec((1, rows, width), lambda m, s: (m, 0, place))
+    line = pl.BlockSpec((1, 1, HEADS, rows), lambda m, s: (m, 0, 0, 0))
+    bf16 = jax.ShapeDtypeStruct((micro, rows, width), jnp.bfloat16)
     return pl.pallas_call(
-        functools.partial(self_backward_kernel, number, tq, tk, pairs),
+        functools.partial(self_backward_kernel, tq, tk, pairs),
         out_shape=(
-            jax.ShapeDtypeStruct((1, width, rows), jnp.bfloat16),
+            jax.ShapeDtypeStruct((micro, width, rows), jnp.bfloat16),
             bf16,
             bf16,
             bf16,
@@ -420,7 +419,7 @@
         ),
         grid_spec=pltpu.PrefetchScalarGridSpec(
             num_scalar_prefetch=1,
-            grid=(1,),
+            grid=(micro,),
             in_specs=[
                 tall,
                 long(0),
@@ -432,21 +431,27 @@
                 tall,
                 line,
                 line,
-                pl.BlockSpec((1, 2, rows), lambda i, s: (number, 0, 0)),
+                pl.BlockSpec((1, 2, rows), lambda m, s: (m, 0, 0)),
                 long(0),
                 long(0),
             ],
-            out_specs=[tall_out]
-            + [long_out] * 4
-            + [pl.BlockSpec((width, 3 * width), lambda i, s: (0, 0))],
+            out_specs=[tall]
+            + [long(0)] * 4
+            + [
+                pl.BlockSpec(
+                    (width, 3 * width), lambda m, s: (0, 0), pipeline_mode=pl.Buffered(1)
+                )
+            ],
             scratch_shapes=[pltpu.VMEM((rows, width), jnp.float32)] * 4
-            + [pltpu.VMEM((width, tq), jnp.float32)],
+            + [pltpu.VMEM((width, tq), jnp.float32)]
+            + [pltpu.VMEM((HEADS, tk, tq), t) for t in (jnp.float32, jnp.float32)]
+            + [pltpu.VMEM((HEADS, tk, tq), t) for t in (jnp.bfloat16, jnp.bfloat16)],
         ),
         compiler_params=pltpu.CompilerParams(vmem_limit_bytes=60 << 20),
         cost_estimate=pl.CostEstimate(
-            flops=10 * rows * rows * width,
-            bytes_accessed=40 * rows * width,
-            transcendentals=rows * rows * HEADS,
+            flops=10 * micro * rows * rows * width,
+            bytes_accessed=40 * micro * rows * width,
+            transcendentals=micro * rows * rows * HEADS,
         ),
         name="self_backward",
     )(
@@ -544,8 +549,7 @@
     own_dmv_ref,
     far_dmk_ref,
     far_dmv_ref,
-    ga_ref,
-    gb_ref,
+    g_out_ref,
     mk_ref,
     mv_ref,
     mkt_ref,
@@ -565,7 +569,9 @@
     act_ref,
     slope_ref,
     mixed_ref,
-    dcq_ref,
+    work_ref,
+    g_ref,
+    sems,
 ):
     micro, tile = pl.program_id(0), pl.program_id(1)
     width = x_ref.shape[2]
@@ -576,11 +582,13 @@
     half_mem = 256
     size = LANES // 2
     par_count = par_ref.shape[0]
-    mem_at = width + hidden
+    block = x_ref.shape[1]
+    base = 2 * hidden
+    mem_at = base + 3 * width
 
     @pl.when((micro == 0) & (tile == 0))
     def _():
-        for ref in (ga_ref, gb_ref, gpar_ref, gfb_ref):
+        for ref in (g_ref, gpar_ref, gfb_ref):
             ref[...] = jnp.zeros_like(ref)
         for here, there in ((wo0_ref, wo0t_ref), (wq1_ref, wq1t_ref), (wo1_ref, wo1t_ref)):
             there[...] = jnp.transpose(here[...])
@@ -646,19 +654,20 @@
     z = wide(h1) * par(1, 1, x) + (nn(wo1t_ref[...], cross) + par(0, 1, x))
     n2, inv2 = norm_tall(z)
     h2 = low(n2 * par(2, 1, x) + par(3, 1, x))
-    branch = 0.0
     for c in range(hidden // chunk):
         part = slice(c * chunk, (c + 1) * chunk)
-        pre = nn(wint_ref[part, :], h2)
+        slope_ref[part, :] = nn(wint_ref[part, :], h2)
+    for c in range(hidden // chunk):
+        part = slice(c * chunk, (c + 1) * chunk)
+        pre = slope_ref[part, :]
         pre = pre + spread(fb_ref[part, :], pre)
         square = pre * pre
         gate = 0.5 * jnp.tanh(pre * (square * (GELU_C * GELU_A) + GELU_C)) + 0.5
-        act = low(pre * gate)
-        act_ref[part, :] = act
+        act_ref[part, :] = low(pre * gate)
         slope_ref[part, :] = gate + (pre * (gate * (1.0 - gate))) * (
             square * (6.0 * GELU_C * GELU_A) + 2.0 * GELU_C
         )
-        branch = branch + nn(woutt_ref[:, part], act)
+    branch = nn(woutt_ref[...], act_ref[...])
     z = wide(h2) * par(1, 2, x) + (branch + par(0, 2, x))
     n3, inv3 = norm_tall(z)
     out_ref[0] = jnp.transpose(low(n3 * par(2, 2, x) + par(3, 2, x)))
@@ -670,48 +679,53 @@
     note(1, 2, dz * wide(h2))
     df = low(dz)
     note(0, 2, wide(df))
-    dh = dz * par(1, 2, x)
     for c in range(hidden // chunk):
         part = slice(c * chunk, (c + 1) * chunk)
-        dact = low(nn(wout_ref[:, part], df))
-        dpre = low(wide(dact) * slope_ref[part, :])
+        work_ref[part, :] = low(nn(wout_ref[:, part], df))
+    for c in range(hidden // chunk):
+        part = slice(c * chunk, (c + 1) * chunk)
+        dpre = low(wide(work_ref[part, :]) * slope_ref[part, :])
         gfb_ref[part, :] += lanes_of(wide(dpre))
-        at = width + c * chunk
-        gb_ref[:, at : at + chunk] += nt(act_ref[part, :], df)
-        ga_ref[:, part] += nt(h2, dpre)
-        dh = dh + nn(win_ref[:, part], dpre)
+        work_ref[part, :] = dpre
+    dh = dz * par(1, 2, x) + nn(win_ref[...], work_ref[...])
+    for c in range(hidden // chunk):
+        part = slice(c * chunk, (c + 1) * chunk)
+        at = hidden + c * chunk
+        g_ref[:, at : at + chunk] += nt(act_ref[part, :], df)
+        g_ref[:, part] += nt(h2, work_ref[part, :])
     note(2, 1, dh * n2)
     note(3, 1, dh)
     dz = norm_tall_backward(dh * par(2, 1, x), n2, inv2)
     note(1, 1, dz * wide(h1))
     dc = low(dz)
     note(0, 1, wide(dc))
-    gb_ref[:, :width] += nt(cross, dc)
+    g_ref[:, base + 2 * width : base + 3 * width] += nt(cross, dc)
     dco = low(nn(wo1_ref[...], dc))
-    for k in range(HEADS // 2):
-        pair = slice(k * LANES, (k + 1) * LANES)
-        queries = [alone(cq[pair, :], number) for number in range(2)]
-        grads = [alone(dco[pair, :], number) for number in range(2)]
-        weighed = wide(dco[pair, :]) * mixed_ref[pair, :]
-        dq = [0.0, 0.0]
-        for c in range(mem_rows // half_mem):
-            keys = slice(c * half_mem, (c + 1) * half_mem)
-            for number in range(2):
-                head = 2 * k + number
-                part = slice(head * size, (head + 1) * size)
-                delta = jnp.sum(
-                    tall_sum(weighed[number * size : (number + 1) * size]), axis=0, keepdims=True
-                )
-                p = p_ref[head, keys, :] * shares[head]
-                ds = low(p * (nn(mv_ref[keys, pair], grads[number]) - delta))
-                dq[number] = dq[number] + nn(mkt_ref[part, keys], ds)
-                dmk_ref[keys, pair] += nt(ds, queries[number])
-                dmv_ref[keys, pair] += nt(low(p), grads[number])
-        for number in range(2):
-            head = 2 * k + number
-            dcq_ref[head * size : (head + 1) * size, :] = low(dq[number] * 0.125)
-    dcq = dcq_ref[...]
-    ga_ref[:, hidden + width : hidden + 2 * width] += nt(h1, dcq)
+    queries = [alone(cq[h // 2 * LANES : (h // 2 + 1) * LANES], h % 2) for h in range(HEADS)]
+    grads = [alone(dco[h // 2 * LANES : (h // 2 + 1) * LANES], h % 2) for h in range(HEADS)]
+    weighed = wide(dco) * mixed_ref[...]
+    deltas = [
+        jnp.sum(tall_sum(weighed[h * size : (h + 1) * size]), axis=0, keepdims=True)
+        for h in range(HEADS)
+    ]
+    mixed_ref[...] = jnp.zeros_like(mixed_ref)
+    for c in range(mem_rows // half_mem):
+        keys = slice(c * half_mem, (c + 1) * half_mem)
+        spot = [slice(h * half_mem, (h + 1) * half_mem) for h in range(HEADS)]
+        cols = [slice(h // 2 * LANES, (h // 2 + 1) * LANES) for h in range(HEADS)]
+        for h in range(HEADS):
+            slope_ref[spot[h], :] = nn(mv_ref[keys, cols[h]], grads[h])
+        for h in range(HEADS):
+            p = p_ref[h, keys, :] * shares[h]
+            act_ref[spot[h], :] = low(p)
+            work_ref[spot[h], :] = low(p * (slope_ref[spot[h], :] - deltas[h]))
+        for h in range(HEADS):
+            part = slice(h * size, (h + 1) * size)
+            dmv_ref[keys, cols[h]] += nt(act_ref[spot[h], :], grads[h])
+            dmk_ref[keys, cols[h]] += nt(work_ref[spot[h], :], queries[h])
+            mixed_ref[part, :] += nn(mkt_ref[part, keys], work_ref[spot[h], :])
+    dcq = low(mixed_ref[...] * 0.125)
+    g_ref[:, base + width : base + 2 * width] += nt(h1, dcq)
     dh = nn(wq1_ref[...], dcq) + dz * par(1, 1, x)
     note(2, 0, dh * n1)
     note(3, 0, dh)
@@ -719,7 +733,7 @@
     note(1, 0, dz * x)
     da = low(dz)
     note(0, 0, wide(da))
-    ga_ref[:, hidden : hidden + width] += nt(self_low, da)
+    g_ref[:, base : base + width] += nt(self_low, da)
     dso = low(nn(wo0_ref[...], da))
     dso_ref[0] = dso
     share = wide(dso) * self_out
@@ -742,7 +756,7 @@
             own_low, far_low = low(ref[:own_mem, :]), low(ref[own_mem:, :])
             own[0] = ref[:own_mem, :]
             far[0] = far_low
-            gb_ref[:, at : at + width] += nn(turned[0], own_low) + nn(turned[1], far_low)
+            g_ref[:, at : at + width] += nn(turned[0], own_low) + nn(turned[1], far_low)
 
     @pl.when((micro == pl.num_programs(0) - 1) & (tile == pl.num_programs(1) - 1))
     def _():
@@ -753,7 +767,23 @@
         for c in range(hidden // chunk):
             column = jnp.sum(gfb_ref[c * chunk : (c + 1) * chunk, :], axis=1, keepdims=True)
             small = jnp.where(lane == par_count + c, column, small)
-        gb_ref[:, mem_at + 2 * width :] = small
+        g_ref[:, mem_at + 2 * width :] = small
+        slots, step = hidden // width, block
+        copies = []
+        for number, at in enumerate(range(0, g_ref.shape[1], step)):
+            cols = min(step, g_ref.shape[1] - at)
+            slot = number % slots
+            if number >= slots:
+                copies[number - slots].wait()
+            spot = slice(slot * width, (slot + 1) * width)
+            act_ref[spot, :cols] = low(g_ref[:, at : at + cols])
+            copy = pltpu.make_async_copy(
+                act_ref.at[spot, :cols], g_out_ref.at[:, at : at + cols], sems.at[slot]
+            )
+            copy.start()
+            copies.append(copy)
+        for copy in copies[-slots:]:
+            copy.wait()
 
 
 def middle(x, cot, self_out, memory, far_memory, rest, hidden, block=256):
@@ -771,7 +801,7 @@
         )
 
     base = 2 * hidden // width
-    columns = [hidden + 2 * width, 3 * width + hidden + LANES]
+    columns = 2 * hidden + 5 * width + LANES
     mem_out = lambda kind: jax.ShapeDtypeStruct((micro, own_mem, width), kind)
     return pl.pallas_call(
         middle_kernel,
@@ -785,7 +815,7 @@
             mem_out(bf16),
             mem_out(bf16),
         ]
-        + [jax.ShapeDtypeStruct((width, n), f32) for n in columns],
+        + [jax.ShapeDtypeStruct((width, columns), bf16)],
         grid=(micro, rows // block),
         in_specs=[row_block, row_block, tall_block, mem_block, mem_block]
         + [fixed(hidden, 0), fixed(hidden, 1)]
@@ -798,7 +828,7 @@
             row_block,
         ]
         + [mem_block] * 4
-        + [fixed(n, 0) for n in columns],
+        + [pl.BlockSpec(memory_space=pl.ANY)],
         scratch_shapes=[
             pltpu.VMEM((mem_rows, width), bf16),
             pltpu.VMEM((mem_rows, width), bf16),
@@ -819,9 +849,11 @@
             pltpu.VMEM((hidden, block), bf16),
             pltpu.VMEM((hidden, block), f32),
             pltpu.VMEM((width, block), f32),
-            pltpu.VMEM((width, block), bf16),
+            pltpu.VMEM((hidden, block), bf16),
+            pltpu.VMEM((width, columns), f32),
+            pltpu.SemaphoreType.DMA((hidden // width,)),
         ],
-        compiler_params=pltpu.CompilerParams(vmem_limit_bytes=60 << 20),
+        compiler_params=pltpu.CompilerParams(vmem_limit_bytes=61 << 20),
         cost_estimate=pl.CostEstimate(
             flops=6 * micro * rows * width * (3 * width + 2 * hidden + 4 * mem_rows),
             bytes_accessed=20 * micro * rows * width + 30 * width * (width + hidden),
@@ -832,9 +864,9 @@
 
 
 def input_grad_kernel(
-    dqt_ref, dk_ref, dv_ref, far_dk_ref, far_dv_ref, w_ref, skip_ref, *rest
+    dqt_ref, dk_ref, dv_ref, far_dk_ref, far_dv_ref, w_ref, skip_ref, *others
 ):
-    out_ref = rest[-1]
+    out_ref = others[-1]
     width = dk_ref.shape[2]
     dk = low(wide(dk_ref[0]) + wide(far_dk_ref[0]))
     dv = low(wide(dv_ref[0]) + wide(far_dv_ref[0]))
@@ -846,28 +878,27 @@
     )
 
 
-def input_gradient(number, dqt, dk, dv, far_dk, far_dv, w, skip, so_far, block=512):
+def input_gradient(first, count, dqt, dk, dv, far_dk, far_dv, w, skip, so_far=None, block=512):
     micro, rows, width = skip.shape
-    row_block = pl.BlockSpec((1, block, width), lambda i: (0, i, 0))
-    place = pl.BlockSpec((1, block, width), lambda i: (number, i, 0))
+    row_block = pl.BlockSpec((1, block, width), lambda m, i: (first + m, i, 0))
     before = [] if so_far is None else [so_far]
     return pl.pallas_call(
         input_grad_kernel,
         out_shape=jax.ShapeDtypeStruct((micro, rows, width), jnp.bfloat16),
-        grid=(rows // block,),
-        in_specs=[pl.BlockSpec((1, width, block), lambda i: (0, 0, i))]
+        grid=(count, rows // block),
+        in_specs=[pl.BlockSpec((1, width, block), lambda m, i: (first + m, 0, i))]
         + [row_block] * 4
         + [
-            pl.BlockSpec(w.shape, lambda i: (0, 0), pipeline_mode=pl.Buffered(1)),
-            place,
+            pl.BlockSpec(w.shape, lambda m, i: (0, 0), pipeline_mode=pl.Buffered(1)),
+            row_block,
         ]
         + [pl.BlockSpec(memory_space=pl.ANY)] * len(before),
-        out_specs=place,
+        out_specs=row_block,
         input_output_aliases={7: 0} if before else {},
         compiler_params=pltpu.CompilerParams(vmem_limit_bytes=VMEM_LIMIT),
         cost_estimate=pl.CostEstimate(
-            flops=6 * rows * width * width,
-            bytes_accessed=16 * rows * width + 6 * width * width,
+            flops=6 * count * rows * width * width,
+            bytes_accessed=16 * count * rows * width + 6 * width * width,
             transcendentals=0,
         ),
         name="input_gradient",
@@ -953,56 +984,43 @@
         own_mv,
         far_mk,
         far_mv,
-        g_a,
-        g_b,
+        g_main,
     ) = middle(layer_in, cotangent, self_out, memory, far_memory, rest, hidden)
 
-    ready = TreeScatter([g_a, g_b], [0, 1], axis)
-    back, far = [], []
-    for number in range(layer_in.shape[0]):
-        dso, _ = ready.send(dso)
-        back.append(
-            self_backward(
-                number,
-                qt,
-                kv,
-                kvt,
-                far_kv,
-                far_kvt,
-                dso,
-                lse,
-                delta,
-                limits,
-                tiles,
-                layer_in,
-                far_x,
-            )
-        )
-        ready.receive(back[number][0])
-        far.append(continuation_to_prompt(back[number][1:3], axis))
-    mem_dk = low(own_mk + wide(from_partner(far_mk, axis, 0)))
-    mem_dv = low(own_mv + wide(from_partner(far_mv, axis, 0)))
+    summed = lax.psum_scatter(g_main, axis, scatter_dimension=0, tiled=True)
+    dqt, far_dk, far_dv, dk, dv, g_late = self_backward(
+        qt, kv, kvt, far_kv, far_kvt, dso, lse, delta, limits, tiles, layer_in, far_x
+    )
+    far_dk, far_dv = continuation_to_prompt((far_dk, far_dv), axis)
+    late = TreeScatter(g_late, axis)
+    far_mk, far_mv = from_partner((far_mk, far_mv), axis, 0)
+    far_mk = late.send(far_mk)
+    mem_dk = low(own_mk + wide(far_mk))
+    mem_dv = low(own_mv + wide(far_mv))
     at = 2 * hidden + 3 * width
     memory_grad = low(
         flat_nt(mem_dk, rest[:, at : at + width])
         + flat_nt(mem_dv, rest[:, at + width : at + 2 * width])
     )
-    late = TreeScatter([sum(b[5] for b in back)], [0], axis)
+    late.receive(memory_grad)
     input_grad = None
-    for number, (b, f) in enumerate(zip(back, far)):
+    micro = layer_in.shape[0]
+    for begin, count in ((0, micro - 1), (micro - 1, 1)):
+        skip = late.send(skip)
         input_grad = input_gradient(
-            number, b[0], b[3], b[4], f[0], f[1], first, skip, input_grad
+            begin, count, dqt, dk, dv, far_dk, far_dv, first, skip, input_grad
         )
-    s_a, s_b = ready.finish()
-    (s_c,) = late.finish()
+        late.receive(input_grad)
+    s_c = late.finish()
+    summed = wide(summed)
     s_q0, s_k0, s_v0 = (s_c[:, k * width : (k + 1) * width] for k in range(3))
-    s_in = jnp.swapaxes(s_a[:, :hidden].reshape(own_rows, parts, width), 1, 2)
+    s_in = jnp.swapaxes(summed[:, :hidden].reshape(own_rows, parts, width), 1, 2)
     s_in = s_in.reshape(own_rows, hidden)
-    s_o0, s_q1 = s_a[:, hidden : hidden + width], s_a[:, hidden + width :]
-    s_o1 = s_b[:, :width]
-    s_out = s_b[:, width : width + hidden].reshape(w_out.shape)
-    s_k1, s_v1 = (s_b[:, hidden + k * width :][:, :width] for k in (1, 2))
-    s_small = s_b[:, hidden + 3 * width :][:, :small_cols]
+    s_out = summed[:, hidden : 2 * hidden].reshape(w_out.shape)
+    s_o0, s_q1, s_o1, s_k1, s_v1 = (
+        summed[:, 2 * hidden + k * width :][:, :width] for k in range(5)
+    )
+    s_small = summed[:, 2 * hidden + 5 * width :][:, :small_cols]
     return (
         final,
         input_grad,

time: 588 us -> 477 us (0.81)
  Pallas kernels: 403 us -> 358 us
  waiting for transfers between devices: 39.7 us -> 17.8 us
  other arithmetic: 25.9 us -> 8.8 us
  local copies, waits for them, and re-layouts: 38.4 us -> 25.8 us
  starting transfers between devices: 57.2 us -> 48 us
    pallas_call x3 -> x1, Pallas kernels: 144 us -> 94.8 us  [self_backward(): pl.pallas_call(functools.partial(self_backward_kernel, tq, tk, pairs), ou...]
    ppermute x23 -> x3, starting transfers between devices: 42.9 us -> 3.29 us  [from_partner(): lax.ppermute(x, axis, [(i, i ^ 1 << bit) for i in range(lax.axis_size(axi...]
    ppermute x0 -> x14, starting transfers between devices: none -> 38.9 us  [shifted(): lax.ppermute(x, axis, [(i, i ^ offset) for i in range(lax.axis_size(axis))])]
    ppermute x23 -> x3, waiting for transfers between devices: 39.6 us -> 6.1 us  [from_partner(): lax.ppermute(x, axis, [(i, i ^ 1 << bit) for i in range(lax.axis_size(axi...]
    add x13 -> x2, other arithmetic: 17.9 us -> 1.43 us  [receive(): self.block = sum([wide(g) for g in self.got], self.keep)]
    pallas_call x1, Pallas kernels: 163 us -> 176 us  [middle(): pl.pallas_call(middle_kernel, out_shape=[jax.ShapeDtypeStruct((micro, row...]
    ppermute x0 -> x14, waiting for transfers between devices: none -> 11.7 us  [shifted(): lax.ppermute(x, axis, [(i, i ^ offset) for i in range(lax.axis_size(axis))])]
    ppermute x6 -> x2, starting transfers between devices: 13 us -> 4.48 us  [continuation_to_prompt(): lax.ppermute(x, axis, [(i, i + 1) for i in range(0, lax.axis_size(axis),...]
  transfers between devices with their start and end apart: 31 -> 22, of which waited for: 11 -> 7; matrix products, arithmetic and copies ran while one was open for 8% -> 3% of each run, Pallas kernels for 41% -> 38%
where the time goes in v3:
time: 477 us; the launch traced here: 478 us
  Pallas kernels  358 us (75%)
  starting transfers between devices  48 us (10%)
  local copies, waits for them, and re-layouts  25.8 us (5%)
  waiting for transfers between devices  17.8 us (4%)
  between operations  14.7 us (3%)
  other arithmetic  8.8 us (2%)
  matrix products  5.3 us (1%)
    pallas_call x1, Pallas kernels, middle(): pl.pallas_call(middle_kernel, out_shape=[jax.ShapeDtypeStruct((micro, row...  176 us
    pallas_call x1, Pallas kernels, self_backward(): pl.pallas_call(functools.partial(self_backward_kernel, tq, tk, pairs), ou...  94.8 us
    pallas_call x1, Pallas kernels, self_forward(): pl.pallas_call(functools.partial(self_forward_kernel, tq, tk, pairs), out...  57.1 us
    ppermute x14, starting transfers between devices, shifted(): lax.ppermute(x, axis, [(i, i ^ offset) for i in range(lax.axis_size(axis))])  38.9 us
    pallas_call x2, Pallas kernels, input_gradient(): pl.pallas_call(input_grad_kernel, out_shape=jax.ShapeDtypeStruct((micro,...  15.2 us
    pallas_call x1, Pallas kernels, project(): pl.pallas_call(project_kernel, out_shape=(tall(width), long, tall(2 * wid...  14.4 us
    unnamed x25, local copies, waits for them, and re-layouts  11.7 us
    ppermute x14, waiting for transfers between devices, shifted(): lax.ppermute(x, axis, [(i, i ^ offset) for i in range(lax.axis_size(axis))])  11.7 us
  transfers between devices with their start and end apart: 22, of which 7 were waited for; matrix products, arithmetic and copies ran while one was open for 3% of the time, Pallas kernels for 38%

profile of v3, /device:TPU:0, one launch (start us, length us, event | category | flops | bytes accessed | tf_op | source)
XLA Modules:
  0.0 478.1 jit_solution(14023886634350014217)
XLA Ops:
  19.4 5.1 %collective-permute-start.1 = (bf16[1,1,1,16,1536]{4,3,2,1,0:T(8,128)(2,1)S(1)}, bf16[1,1,1,16,1536]{4,3,2,1,0:T(8,128)(2,1)S(1)}, u32[]{:S(2)}, u32[]{:S(2)}) collective-permute-start(bf16[1,1,1,16,1536]{4,3,2,1,0:T(8,128)(2,1)S(1)} %bitcast.88), channel_id=1, source_target_pairs={{0,24},{1,25},{2,26},{3,27},{4,28},{5,29},{6,30},{7,31},{8,16},{9,... | collective-permute-start | bytes 147464 | tf_op jit(solution)/shard_map/ppermute | solution.py:61
  26.4 2.8 collective-permute-start.8
  31.2 2.7 collective-permute-start.4
  34.9 5.5 %collective-permute-done.4 = bf16[4,1,1,16,1536]{4,3,2,1,0:T(8,128)(2,1)S(1)} collective-permute-done((bf16[4,1,1,16,1536]{4,3,2,1,0:T(8,128)(2,1)S(1)}, bf16[4,1,1,16,1536]{4,3,2,1,0:T(8,128)(2,1)S(1)}, u32[]{:S(2)}, u32[]{:S(2)}) %collective-permute-start.4) | collective-permute-done | bytes 196640 | tf_op jit(solution)/shard_map/ppermute | solution.py:61
  40.4 3.5 collective-permute-done.5
  48.0 14.4 %project.1 = (bf16[3,512,1024]{2,1,0:T(8,128)(2,1)}, bf16[3,1024,1024]{2,1,0:T(8,128)(2,1)}, bf16[3,1024,1024]{2,1,0:T(8,128)(2,1)}, bf16[3,1024,1024]{2,1,0:T(8,128)(2,1)}, bf16[3,1024,1024]{2,1,0:T(8,128)(2,1)}) custom-call(bf16[3,1024,512]{2,1,0:T(8,128)(2,1)} %x_ref.2, bf16[3,1024,512]{2,1,0:T(8,128)(2,1)} %collective-permute-done.far_ref, ...), custom_call_target="tpu_custom_call" | custom-call | flops 8053063680 | bytes 34603008 | tf_op jit(solution)/shard_map/project/pallas_call | solution.py:157
  62.4 57.1 %self_forward.1 = (f32[3,512,1024]{2,1,0:T(8,128)}, f32[3,8,1024]{2,1,0:T(8,128)}) custom-call(s32[3,4,3]{2,1,0:T(4,128)} %pad_add_fusion.1.tiles, bf16[3,512,1024]{2,1,0:T(8,128)(2,1)} %get-tuple-element.65.qt_ref, bf16[3,1024,1024]{2,1,0:T(8,128)(2,1)} %get-tuple-element.66.kp_ref.vp_ref, bf16[3,1024,1024]{2,1,0:T(8,128)(2,1)} %get-tuple-element.67.kl_ref.vl_ref, ...), custom_call_target="tpu_custom_call" | custom-call | flops 6442450944 | bytes 25165824 | tf_op jit(solution)/shard_map/self_forward/pallas_call | solution.py:258
  120.4 176.1 %middle.1 = (bf16[3,1024,512]{2,1,0:T(8,128)(2,1)}, bf16[3,512,1024]{2,1,0:T(8,128)(2,1)}, f32[3,8,1024]{2,1,0:T(8,128)}, f32[3,1024,512]{2,1,0:T(8,128)}, f32[3...) custom-call(bf16[3,1024,512]{2,1,0:T(8,128)(2,1)} %x_ref.2, ...), custom_call_target="tpu_custom_call" | custom-call | flops 72477573120 | bytes 70778880 | tf_op jit(solution)/shard_map/middle/pallas_call | solution.py:806
  296.5 94.8 %self_backward.1 = (bf16[3,512,1024]{2,1,0:T(8,128)(2,1)}, bf16[3,1024,512]{2,1,0:T(8,128)(2,1)}, bf16[3,1024,512]{2,1,0:T(8,128)(2,1)}, bf16[3,1024,512]{2,1,0:...) custom-call(s32[3,4,3]{2,1,0:T(4,128)} %pad_add_fusion.1.tiles, ...), custom_call_target="tpu_custom_call" | custom-call | flops 16106127360 | bytes 62914560 | tf_op jit(solution)/shard_map/self_backward/pallas_call | solution.py:410
  391.4 1.5 collective-permute-start.10
  392.9 3.0 collective-permute-start.9
  396.4 2.4 dynamic-slice_convert_fusion
  398.8 5.3 %collective-permute-done.11 = bf16[3,256,512]{2,1,0:T(8,128)(2,1)} collective-permute-done((bf16[3,256,512]{2,1,0:T(8,128)(2,1)}, bf16[3,256,512]{2,1,0:T(8,128)(2,1)}, u32[]{:S(2)}, u32[]{:S(2)}) %collective-permute-start.11) | collective-permute-done | bytes 786464 | tf_op jit(solution)/shard_map/ppermute | solution.py:49
  405.2 2.4 fusion
  407.6 3.0 add_convert_fusion
  410.6 1.3 convert_add_fusion
  412.0 16.8 %collective-permute-start.14 = (bf16[4,1,1,16,1536]{4,3,2,1,0:T(8,128)(2,1)S(1)}, bf16[4,1,1,16,1536]{4,3,2,1,0:T(8,128)(2,1)S(1)}, u32[]{:S(2)}, u32[]{:S(2)}) collective-permute-start(bf16[4,1,1,16,1536]{4,3,2,1,0:T(8,128)(2,1)S(1)} %get-tuple-element.98), channel_id=1, source_target_pairs={{0,2},{1,3},{2,0},{3,1},{4,6},{5,7},{6,4},{7,5},{8,10},{9,11},{10,... | collective-permute-start | bytes 589832 | tf_op jit(solution)/shard_map/ppermute | solution.py:61
  428.8 2.4 collective-permute-start.15
  431.3 1.4 collective-permute-start.16
  432.7 1.6 copy-done
  434.3 9.5 %input_gradient.2.others_0_ = bf16[3,1024,512]{2,1,0:T(8,128)(2,1)} custom-call(bf16[3,512,1024]{2,1,0:T(8,128)(2,1)} %get-tuple-element.83.dqt_ref, bf16[3,1024,512]{2,1,0:T(8,128)(2,1)} %get-tuple-element.84.dk_ref, bf16[3,1024,512]{2,1,0:T(8,128)(2,1)} %get-tuple-element.85.dv_ref, bf16[3,1024,512]{2,1,0:T(8,128)(2,1)} %collective-permute-done.9.far_dk_ref, ...), custom_call_target="tpu_custom_call" | custom-call | flops 3221225472 | bytes 18350080 | tf_op jit(solution)/shard_map/input_gradient/pallas_call | solution.py:885
  443.8 2.1 collective-permute-done.16
  446.1 8.4 %collective-permute-start.18 = (bf16[1,1,1,16,1536]{4,3,2,1,0:T(8,128)(2,1)S(1)}, bf16[1,1,1,16,1536]{4,3,2,1,0:T(8,128)(2,1)S(1)}, u32[]{:S(2)}, u32[]{:S(2)}) collective-permute-start(bf16[1,1,1,16,1536]{4,3,2,1,0:T(8,128)(2,1)S(1)} %get-tuple-element.106), channel_id=1, source_target_pairs={{0,16},{1,17},{2,18},{3,19},{4,20},{5,21},{6,22},{7,23},{8,24},{9,... | collective-permute-start | bytes 147464 | tf_op jit(solution)/shard_map/ppermute | solution.py:61
  454.5 5.7 %input_gradient.3 = bf16[3,1024,512]{2,1,0:T(8,128)(2,1)} custom-call(bf16[3,512,1024]{2,1,0:T(8,128)(2,1)} %get-tuple-element.83.dqt_ref, bf16[3,1024,512]{2,1,0:T(8,128)(2,1)} %get-tuple-element.84.dk_ref, bf16[3,1024,512]{2,1,0:T(8,128)(2,1)} %get-tuple-element.85.dv_ref, ...), custom_call_target="tpu_custom_call", output_to_operand_aliasing={{}: (7, {})} | custom-call | flops 1610612736 | bytes 9961472 | tf_op jit(solution)/shard_map/input_gradient/pallas_call | solution.py:885
  (115 shorter events, 34.6 us)
Async XLA Ops:
  7.2 112.4 %all-gather.2.cloned.1.call-start = ((), (), s32[]{:S(2)}) async-start(), calls=%async_computation.1 | async-start | bytes 7163904 | tf_op jit(solution)/shard_map/all_gather | solution.py:957
  19.3 441.1 %reduce-scatter.2.cloned.1.call-start = ((), (), s32[]{:S(2)}) async-start(), calls=%async_computation.2 | async-start | bytes 7163904 | tf_op jit(solution)/shard_map/reduce_scatter | solution.py:990
  19.4 11.7 %collective-permute-start.1 = (bf16[1,1,1,16,1536]{4,3,2,1,0:T(8,128)(2,1)S(1)}, bf16[1,1,1,16,1536]{4,3,2,1,0:T(8,128)(2,1)S(1)}, u32[]{:S(2)}, u32[]{:S(2)}) collective-permute-start(bf16[1,1,1,16,1536]{4,3,2,1,0:T(8,128)(2,1)S(1)} %bitcast.88), channel_id=1, source_target_pairs={{0,24},{1,25},{2,26},{3,27},{4,28},{5,29},{6,30},{7,31},{8,16},{9,... | collective-permute-start | bytes 147464 | tf_op jit(solution)/shard_map/ppermute | solution.py:61
  24.5 6.6 %collective-permute-start.2 = (bf16[1,1,1,16,1536]{4,3,2,1,0:T(8,128)(2,1)S(1)}, bf16[1,1,1,16,1536]{4,3,2,1,0:T(8,128)(2,1)S(1)}, u32[]{:S(2)}, u32[]{:S(2)}) collective-permute-start(bf16[1,1,1,16,1536]{4,3,2,1,0:T(8,128)(2,1)S(1)} %bitcast.89), channel_id=1, source_target_pairs={{0,16},{1,17},{2,18},{3,19},{4,20},{5,21},{6,22},{7,23},{8,24},{9,... | collective-permute-start | bytes 147464 | tf_op jit(solution)/shard_map/ppermute | solution.py:61
  24.5 6.6 %collective-permute-start.3 = (bf16[1,1,1,16,1536]{4,3,2,1,0:T(8,128)(2,1)S(1)}, bf16[1,1,1,16,1536]{4,3,2,1,0:T(8,128)(2,1)S(1)}, u32[]{:S(2)}, u32[]{:S(2)}) collective-permute-start(bf16[1,1,1,16,1536]{4,3,2,1,0:T(8,128)(2,1)S(1)} %bitcast.90), channel_id=1, source_target_pairs={{0,8},{1,9},{2,10},{3,11},{4,12},{5,13},{6,14},{7,15},{8,0},{9,1},... | collective-permute-start | bytes 147464 | tf_op jit(solution)/shard_map/ppermute | solution.py:61
  25.1 22.9 %collective-permute-start = (bf16[3,1024,512]{2,1,0:T(8,128)(2,1)}, bf16[3,1024,512]{2,1,0:T(8,128)(2,1)}, u32[]{:S(2)}, u32[]{:S(2)}) collective-permute-start(bf16[3,1024,512]{2,1,0:T(8,128)(2,1)} %x_ref.2), channel_id=1, source_target_pairs={{1,0},{3,2},{5,4},{7,6},{9,8},{11,10},{13,12},{15,14},{17,16},{19,... | collective-permute-start | bytes 9437192 | tf_op jit(solution)/shard_map/ppermute | solution.py:53
  26.4 93.1 %collective-permute-start.8 = (bf16[3,256,512]{2,1,0:T(8,128)(2,1)}, bf16[3,256,512]{2,1,0:T(8,128)(2,1)S(1)}, u32[]{:S(2)}, u32[]{:S(2)}) collective-permute-start(bf16[3,256,512]{2,1,0:T(8,128)(2,1)} %mem_ref), channel_id=1, source_target_pairs={{0,1},{1,0},{2,3},{3,2},{4,5},{5,4},{6,7},{7,6},{8,9},{9,8},{10,11... | collective-permute-start | bytes 2359304 | tf_op jit(solution)/shard_map/ppermute | solution.py:49
  31.2 9.2 %collective-permute-start.4 = (bf16[4,1,1,16,1536]{4,3,2,1,0:T(8,128)(2,1)S(1)}, bf16[4,1,1,16,1536]{4,3,2,1,0:T(8,128)(2,1)S(1)}, u32[]{:S(2)}, u32[]{:S(2)}) collective-permute-start(bf16[4,1,1,16,1536]{4,3,2,1,0:T(8,128)(2,1)S(1)} %pad_maximum_fusion.2), channel_id=1, source_target_pairs={{0,6},{1,7},{2,4},{3,5},{4,2},{5,3},{6,0},{7,1},{8,14},{9,15},{10,... | collective-permute-start | bytes 589832 | tf_op jit(solution)/shard_map/ppermute | solution.py:61
  33.8 10.1 %collective-permute-start.5 = (bf16[4,1,1,16,1536]{4,3,2,1,0:T(8,128)(2,1)S(1)}, bf16[4,1,1,16,1536]{4,3,2,1,0:T(8,128)(2,1)S(1)}, u32[]{:S(2)}, u32[]{:S(2)}) collective-permute-start(bf16[4,1,1,16,1536]{4,3,2,1,0:T(8,128)(2,1)S(1)} %pad_maximum_fusion.2), channel_id=1, source_target_pairs={{0,4},{1,5},{2,6},{3,7},{4,0},{5,1},{6,2},{7,3},{8,12},{9,13},{10,... | collective-permute-start | bytes 589832 | tf_op jit(solution)/shard_map/ppermute | solution.py:61
  34.3 9.6 %collective-permute-start.6 = (bf16[4,1,1,16,1536]{4,3,2,1,0:T(8,128)(2,1)S(1)}, bf16[4,1,1,16,1536]{4,3,2,1,0:T(8,128)(2,1)S(1)}, u32[]{:S(2)}, u32[]{:S(2)}) collective-permute-start(bf16[4,1,1,16,1536]{4,3,2,1,0:T(8,128)(2,1)S(1)} %pad_maximum_fusion.2), channel_id=1, source_target_pairs={{0,2},{1,3},{2,0},{3,1},{4,6},{5,7},{6,4},{7,5},{8,10},{9,11},{10,... | collective-permute-start | bytes 589832 | tf_op jit(solution)/shard_map/ppermute | solution.py:61
  44.2 2.4 collective-permute-start.7
  391.4 41.3 %collective-permute-start.10 = (bf16[3,1024,512]{2,1,0:T(8,128)(2,1)}, bf16[3,1024,512]{2,1,0:T(8,128)(2,1)S(1)}, u32[]{:S(2)}, u32[]{:S(2)}) collective-permute-start(bf16[3,1024,512]{2,1,0:T(8,128)(2,1)} %get-tuple-element.87), channel_id=1, source_target_pairs={{0,1},{2,3},{4,5},{6,7},{8,9},{10,11},{12,13},{14,15},{16,17},{18,... | collective-permute-start | bytes 9437192 | tf_op jit(solution)/shard_map/ppermute | solution.py:57
  392.9 39.8 %collective-permute-start.9 = (bf16[3,1024,512]{2,1,0:T(8,128)(2,1)}, bf16[3,1024,512]{2,1,0:T(8,128)(2,1)}, u32[]{:S(2)}, u32[]{:S(2)}) collective-permute-start(bf16[3,1024,512]{2,1,0:T(8,128)(2,1)} %get-tuple-element.86), channel_id=1, source_target_pairs={{0,1},{2,3},{4,5},{6,7},{8,9},{10,11},{12,13},{14,15},{16,17},{18,... | collective-permute-start | bytes 9437192 | tf_op jit(solution)/shard_map/ppermute | solution.py:57
  395.9 8.2 %collective-permute-start.11 = (bf16[3,256,512]{2,1,0:T(8,128)(2,1)}, bf16[3,256,512]{2,1,0:T(8,128)(2,1)}, u32[]{:S(2)}, u32[]{:S(2)}) collective-permute-start(bf16[3,256,512]{2,1,0:T(8,128)(2,1)} %get-tuple-element.90), channel_id=1, source_target_pairs={{0,1},{1,0},{2,3},{3,2},{4,5},{5,4},{6,7},{7,6},{8,9},{9,8},{10,11... | collective-permute-start | bytes 2359304 | tf_op jit(solution)/shard_map/ppermute | solution.py:49
  395.9 9.4 %collective-permute-start.13 = (bf16[3,256,512]{2,1,0:T(8,128)(2,1)}, bf16[3,256,512]{2,1,0:T(8,128)(2,1)}, u32[]{:S(2)}, u32[]{:S(2)}) collective-permute-start(bf16[3,256,512]{2,1,0:T(8,128)(2,1)} %get-tuple-element.95), channel_id=1, source_target_pairs={{0,1},{1,0},{2,3},{3,2},{4,5},{5,4},{6,7},{7,6},{8,9},{9,8},{10,11... | collective-permute-start | bytes 2359304 | tf_op jit(solution)/shard_map/ppermute | solution.py:49
  404.1 6.5 %collective-permute-start.12 = (bf16[4,4,1,16,1536]{4,3,2,1,0:T(8,128)(2,1)}, bf16[4,4,1,16,1536]{4,3,2,1,0:T(8,128)(2,1)}, u32[]{:S(2)}, u32[]{:S(2)}) collective-permute-start(bf16[4,4,1,16,1536]{4,3,2,1,0:T(8,128)(2,1)} %dynamic-slice_convert_fusion), channel_id=1, source_target_pairs={{0,1},{1,0},{2,3},{3,2},{4,5},{5,4},{6,7},{7,6},{8,9},{9,8},{10,11... | collective-permute-start | bytes 2359304 | tf_op jit(solution)/shard_map/ppermute | solution.py:61
  404.4 3.2 copy-start.2
  407.6 3.0 copy-start.1
  412.0 31.8 %collective-permute-start.14 = (bf16[4,1,1,16,1536]{4,3,2,1,0:T(8,128)(2,1)S(1)}, bf16[4,1,1,16,1536]{4,3,2,1,0:T(8,128)(2,1)S(1)}, u32[]{:S(2)}, u32[]{:S(2)}) collective-permute-start(bf16[4,1,1,16,1536]{4,3,2,1,0:T(8,128)(2,1)S(1)} %get-tuple-element.98), channel_id=1, source_target_pairs={{0,2},{1,3},{2,0},{3,1},{4,6},{5,7},{6,4},{7,5},{8,10},{9,11},{10,... | collective-permute-start | bytes 589832 | tf_op jit(solution)/shard_map/ppermute | solution.py:61
  428.8 14.9 %collective-permute-start.15 = (bf16[4,1,1,16,1536]{4,3,2,1,0:T(8,128)(2,1)S(1)}, bf16[4,1,1,16,1536]{4,3,2,1,0:T(8,128)(2,1)S(1)}, u32[]{:S(2)}, u32[]{:S(2)}) collective-permute-start(bf16[4,1,1,16,1536]{4,3,2,1,0:T(8,128)(2,1)S(1)} %get-tuple-element.99), channel_id=1, source_target_pairs={{0,4},{1,5},{2,6},{3,7},{4,0},{5,1},{6,2},{7,3},{8,12},{9,13},{10,... | collective-permute-start | bytes 589832 | tf_op jit(solution)/shard_map/ppermute | solution.py:61
  431.3 14.6 %collective-permute-start.16 = (bf16[4,1,1,16,1536]{4,3,2,1,0:T(8,128)(2,1)S(1)}, bf16[4,1,1,16,1536]{4,3,2,1,0:T(8,128)(2,1)S(1)}, u32[]{:S(2)}, u32[]{:S(2)}) collective-permute-start(bf16[4,1,1,16,1536]{4,3,2,1,0:T(8,128)(2,1)S(1)} %get-tuple-element.100), channel_id=1, source_target_pairs={{0,6},{1,7},{2,4},{3,5},{4,2},{5,3},{6,0},{7,1},{8,14},{9,15},{10,... | collective-permute-start | bytes 589832 | tf_op jit(solution)/shard_map/ppermute | solution.py:61
  446.0 14.2 %collective-permute-start.17 = (bf16[1,1,1,16,1536]{4,3,2,1,0:T(8,128)(2,1)S(1)}, bf16[1,1,1,16,1536]{4,3,2,1,0:T(8,128)(2,1)S(1)}, u32[]{:S(2)}, u32[]{:S(2)}) collective-permute-start(bf16[1,1,1,16,1536]{4,3,2,1,0:T(8,128)(2,1)S(1)} %get-tuple-element.105), channel_id=1, source_target_pairs={{0,8},{1,9},{2,10},{3,11},{4,12},{5,13},{6,14},{7,15},{8,0},{9,1},... | collective-permute-start | bytes 147464 | tf_op jit(solution)/shard_map/ppermute | solution.py:61
  446.1 14.1 %collective-permute-start.18 = (bf16[1,1,1,16,1536]{4,3,2,1,0:T(8,128)(2,1)S(1)}, bf16[1,1,1,16,1536]{4,3,2,1,0:T(8,128)(2,1)S(1)}, u32[]{:S(2)}, u32[]{:S(2)}) collective-permute-start(bf16[1,1,1,16,1536]{4,3,2,1,0:T(8,128)(2,1)S(1)} %get-tuple-element.106), channel_id=1, source_target_pairs={{0,16},{1,17},{2,18},{3,19},{4,20},{5,21},{6,22},{7,23},{8,24},{9,... | collective-permute-start | bytes 147464 | tf_op jit(solution)/shard_map/ppermute | solution.py:61
  454.5 5.9 %collective-permute-start.19 = (bf16[1,1,1,16,1536]{4,3,2,1,0:T(8,128)(2,1)S(1)}, bf16[1,1,1,16,1536]{4,3,2,1,0:T(8,128)(2,1)S(1)}, u32[]{:S(2)}, u32[]{:S(2)}) collective-permute-start(bf16[1,1,1,16,1536]{4,3,2,1,0:T(8,128)(2,1)S(1)} %get-tuple-element.107), channel_id=1, source_target_pairs={{0,24},{1,25},{2,26},{3,27},{4,28},{5,29},{6,30},{7,31},{8,16},{9,... | collective-permute-start | bytes 147464 | tf_op jit(solution)/shard_map/ppermute | solution.py:61
  (3 other events, 3.2 us)
Sparse Core Ops, SparseCore 0:
  19.4 77.6 all-gather.1
  296.7 155.7 reduce-scatter.1

commit v4 on v3

--- a/solution.py
+++ b/solution.py
@@ -309,9 +309,9 @@
     lim_ref,
     x_ref,
     far_ref,
+    w_ref,
     dqt_ref,
-    dkp_ref,
-    dvp_ref,
+    away_ref,
     dkl_ref,
     dvl_ref,
     g_ref,
@@ -389,18 +389,20 @@
             0,
         )
         dqt_ref[0, :, here] = low(sum_q[...] * 0.125)
-    dkp_ref[0] = low(sum_kp[...])
-    dvp_ref[0] = low(sum_vp[...])
+    dkp, dvp = low(sum_kp[...]), low(sum_vp[...])
     dkl_ref[0] = low(sum_kl[...])
     dvl_ref[0] = low(sum_vl[...])
     width = x_ref.shape[2]
     own, far = jnp.transpose(x_ref[0]), jnp.transpose(far_ref[0])
     g_ref[:, :width] += nt(own, dqt_ref[0])
-    g_ref[:, width : 2 * width] += nn(own, dkl_ref[0]) + nn(far, dkp_ref[0])
-    g_ref[:, 2 * width :] += nn(own, dvl_ref[0]) + nn(far, dvp_ref[0])
-
-
-def self_backward(qt, kv, kvt, far_kv, far_kvt, grad_out, lse, delta, limits, tiles, x, far_x):
+    g_ref[:, width : 2 * width] += nn(own, dkl_ref[0]) + nn(far, dkp)
+    g_ref[:, 2 * width :] += nn(own, dvl_ref[0]) + nn(far, dvp)
+    away_ref[0] = low(nt(dkp, w_ref[:, :width]) + nt(dvp, w_ref[:, width:]))
+
+
+def self_backward(
+    qt, kv, kvt, far_kv, far_kvt, grad_out, lse, delta, limits, tiles, x, far_x, w_kv
+):
     tq, tk, pairs = 256, 256, HEADS // 2
     micro, width, rows = qt.shape
     tall = pl.BlockSpec((1, width, rows), lambda m, s: (m, 0, 0))
@@ -411,7 +413,6 @@
         functools.partial(self_backward_kernel, tq, tk, pairs),
         out_shape=(
             jax.ShapeDtypeStruct((micro, width, rows), jnp.bfloat16),
-            bf16,
             bf16,
             bf16,
             bf16,
@@ -434,9 +435,12 @@
                 pl.BlockSpec((1, 2, rows), lambda m, s: (m, 0, 0)),
                 long(0),
                 long(0),
+                pl.BlockSpec(
+                    (width, 2 * width), lambda m, s: (0, 0), pipeline_mode=pl.Buffered(1)
+                ),
             ],
             out_specs=[tall]
-            + [long(0)] * 4
+            + [long(0)] * 3
             + [
                 pl.BlockSpec(
                     (width, 3 * width), lambda m, s: (0, 0), pipeline_mode=pl.Buffered(1)
@@ -469,6 +473,7 @@
         limits,
         x,
         far_x,
+        w_kv,
     )
 
 
@@ -571,6 +576,7 @@
     mixed_ref,
     work_ref,
     g_ref,
+    stage_ref,
     sems,
 ):
     micro, tile = pl.program_id(0), pl.program_id(1)
@@ -768,17 +774,16 @@
             column = jnp.sum(gfb_ref[c * chunk : (c + 1) * chunk, :], axis=1, keepdims=True)
             small = jnp.where(lane == par_count + c, column, small)
         g_ref[:, mem_at + 2 * width :] = small
-        slots, step = hidden // width, block
+        slots, step = stage_ref.shape[0], stage_ref.shape[2]
         copies = []
         for number, at in enumerate(range(0, g_ref.shape[1], step)):
             cols = min(step, g_ref.shape[1] - at)
             slot = number % slots
             if number >= slots:
                 copies[number - slots].wait()
-            spot = slice(slot * width, (slot + 1) * width)
-            act_ref[spot, :cols] = low(g_ref[:, at : at + cols])
+            stage_ref[slot, :, :cols] = low(g_ref[:, at : at + cols])
             copy = pltpu.make_async_copy(
-                act_ref.at[spot, :cols], g_out_ref.at[:, at : at + cols], sems.at[slot]
+                stage_ref.at[slot, :, :cols], g_out_ref.at[:, at : at + cols], sems.at[slot]
             )
             copy.start()
             copies.append(copy)
@@ -851,9 +856,10 @@
             pltpu.VMEM((width, block), f32),
             pltpu.VMEM((hidden, block), bf16),
             pltpu.VMEM((width, columns), f32),
-            pltpu.SemaphoreType.DMA((hidden // width,)),
+            pltpu.VMEM((4, width, 256), bf16),
+            pltpu.SemaphoreType.DMA((4,)),
         ],
-        compiler_params=pltpu.CompilerParams(vmem_limit_bytes=61 << 20),
+        compiler_params=pltpu.CompilerParams(vmem_limit_bytes=62 << 20),
         cost_estimate=pl.CostEstimate(
             flops=6 * micro * rows * width * (3 * width + 2 * hidden + 4 * mem_rows),
             bytes_accessed=20 * micro * rows * width + 30 * width * (width + hidden),
@@ -864,21 +870,20 @@
 
 
 def input_grad_kernel(
-    dqt_ref, dk_ref, dv_ref, far_dk_ref, far_dv_ref, w_ref, skip_ref, *others
+    dqt_ref, dk_ref, dv_ref, far_ref, w_ref, skip_ref, *others
 ):
     out_ref = others[-1]
     width = dk_ref.shape[2]
-    dk = low(wide(dk_ref[0]) + wide(far_dk_ref[0]))
-    dv = low(wide(dv_ref[0]) + wide(far_dv_ref[0]))
     out_ref[0] = low(
         nt(jnp.transpose(dqt_ref[0]), w_ref[:, :width])
-        + nt(dk, w_ref[:, width : 2 * width])
-        + nt(dv, w_ref[:, 2 * width :])
+        + nt(dk_ref[0], w_ref[:, width : 2 * width])
+        + nt(dv_ref[0], w_ref[:, 2 * width :])
+        + wide(far_ref[0])
         + skip_ref[0]
     )
 
 
-def input_gradient(first, count, dqt, dk, dv, far_dk, far_dv, w, skip, so_far=None, block=512):
+def input_gradient(first, count, dqt, dk, dv, far, w, skip, so_far=None, block=512):
     micro, rows, width = skip.shape
     row_block = pl.BlockSpec((1, block, width), lambda m, i: (first + m, i, 0))
     before = [] if so_far is None else [so_far]
@@ -887,14 +892,14 @@
         out_shape=jax.ShapeDtypeStruct((micro, rows, width), jnp.bfloat16),
         grid=(count, rows // block),
         in_specs=[pl.BlockSpec((1, width, block), lambda m, i: (first + m, 0, i))]
-        + [row_block] * 4
+        + [row_block] * 3
         + [
             pl.BlockSpec(w.shape, lambda m, i: (0, 0), pipeline_mode=pl.Buffered(1)),
             row_block,
         ]
         + [pl.BlockSpec(memory_space=pl.ANY)] * len(before),
         out_specs=row_block,
-        input_output_aliases={7: 0} if before else {},
+        input_output_aliases={6: 0} if before else {},
         compiler_params=pltpu.CompilerParams(vmem_limit_bytes=VMEM_LIMIT),
         cost_estimate=pl.CostEstimate(
             flops=6 * count * rows * width * width,
@@ -902,7 +907,7 @@
             transcendentals=0,
         ),
         name="input_gradient",
-    )(dqt, dk, dv, far_dk, far_dv, w, skip, *before)
+    )(dqt, dk, dv, far, w, skip, *before)
 
 
 def total_tn(left, right):
@@ -951,7 +956,7 @@
     far_memory = from_partner(memory, axis, 0)
     parts = hidden // width
     small = jnp.concatenate(
-        [p.T for p in small_parts[:4]] + [small_parts[4].reshape(own_rows, -1)], axis=1
+        [jnp.concatenate(small_parts[:4]).T, small_parts[4].reshape(own_rows, -1)], axis=1
     )
     small_cols = small.shape[1]
     rest = lax.all_gather(
@@ -988,13 +993,32 @@
     ) = middle(layer_in, cotangent, self_out, memory, far_memory, rest, hidden)
 
     summed = lax.psum_scatter(g_main, axis, scatter_dimension=0, tiled=True)
-    dqt, far_dk, far_dv, dk, dv, g_late = self_backward(
-        qt, kv, kvt, far_kv, far_kvt, dso, lse, delta, limits, tiles, layer_in, far_x
-    )
-    far_dk, far_dv = continuation_to_prompt((far_dk, far_dv), axis)
+    dqt, away, dk, dv, g_late = self_backward(
+        qt,
+        kv,
+        kvt,
+        far_kv,
+        far_kvt,
+        dso,
+        lse,
+        delta,
+        limits,
+        tiles,
+        layer_in,
+        far_x,
+        first[:, width:],
+    )
     late = TreeScatter(g_late, axis)
+    away = late.send(away)
+    far = continuation_to_prompt(away, axis)
+    late.receive()
+    skip, far_mk, far_mv = late.send((skip, far_mk, far_mv))
     far_mk, far_mv = from_partner((far_mk, far_mv), axis, 0)
-    far_mk = late.send(far_mk)
+    micro = layer_in.shape[0]
+    input_grad = input_gradient(0, micro - 1, dqt, dk, dv, far, first, skip)
+    late.receive(input_grad)
+    skip, far_mk, far_mv = late.send((skip, far_mk, far_mv))
+    input_grad = input_gradient(micro - 1, 1, dqt, dk, dv, far, first, skip, input_grad)
     mem_dk = low(own_mk + wide(far_mk))
     mem_dv = low(own_mv + wide(far_mv))
     at = 2 * hidden + 3 * width
@@ -1002,18 +1026,7 @@
         flat_nt(mem_dk, rest[:, at : at + width])
         + flat_nt(mem_dv, rest[:, at + width : at + 2 * width])
     )
-    late.receive(memory_grad)
-    input_grad = None
-    micro = layer_in.shape[0]
-    for begin, count in ((0, micro - 1), (micro - 1, 1)):
-        skip = late.send(skip)
-        input_grad = input_gradient(
-            begin, count, dqt, dk, dv, far_dk, far_dv, first, skip, input_grad
-        )
-        late.receive(input_grad)
-    s_c = late.finish()
     summed = wide(summed)
-    s_q0, s_k0, s_v0 = (s_c[:, k * width : (k + 1) * width] for k in range(3))
     s_in = jnp.swapaxes(summed[:, :hidden].reshape(own_rows, parts, width), 1, 2)
     s_in = s_in.reshape(own_rows, hidden)
     s_out = summed[:, hidden : 2 * hidden].reshape(w_out.shape)
@@ -1021,6 +1034,9 @@
         summed[:, 2 * hidden + k * width :][:, :width] for k in range(5)
     )
     s_small = summed[:, 2 * hidden + 5 * width :][:, :small_cols]
+    late.receive((input_grad, memory_grad, s_in, s_out, s_small))
+    s_c = late.finish()
+    s_q0, s_k0, s_v0 = (s_c[:, k * width : (k + 1) * width] for k in range(3))
     return (
         final,
         input_grad,

time: 477 us -> 476 us (level)
  starting transfers between devices: 48 us -> 39.6 us
  Pallas kernels: 358 us -> 363 us
    pallas_call x1, Pallas kernels: 94.8 us -> 103 us  [self_backward(): pl.pallas_call(functools.partial(self_backward_kernel, tq, tk, pairs), ou...]
    ppermute x14, waiting for transfers between devices: 11.7 us -> 17.9 us  [shifted(): lax.ppermute(x, axis, [(i, i ^ offset) for i in range(lax.axis_size(axis))])]
    pallas_call x1, Pallas kernels: 176 us -> 170 us  [middle(): pl.pallas_call(middle_kernel, out_shape=[jax.ShapeDtypeStruct((micro, row...]
    ppermute x3, waiting for transfers between devices: 6.1 us -> 0.01 us  [from_partner(): lax.ppermute(x, axis, [(i, i ^ 1 << bit) for i in range(lax.axis_size(axi...]
    ppermute x14, starting transfers between devices: 38.9 us -> 33.5 us  [shifted(): lax.ppermute(x, axis, [(i, i ^ offset) for i in range(lax.axis_size(axis))])]
    unnamed x25 -> x27, local copies, waits for them, and re-layouts: 11.7 us -> 12.7 us
  transfers between devices with their start and end apart: 22 -> 21, of which waited for: 7 -> 5; matrix products, arithmetic and copies ran while one was open for 3% -> 4% of each run, Pallas kernels for 38% -> 40%
where the time goes in v4:
time: 476 us; the launch traced here: 477 us
  Pallas kernels  363 us (76%)
  starting transfers between devices  39.6 us (8%)
  local copies, waits for them, and re-layouts  27.9 us (6%)
  waiting for transfers between devices  18 us (4%)
  between operations  14.8 us (3%)
  other arithmetic  9.54 us (2%)
    pallas_call x1, Pallas kernels, middle(): pl.pallas_call(middle_kernel, out_shape=[jax.ShapeDtypeStruct((micro, row...  170 us
    pallas_call x1, Pallas kernels, self_backward(): pl.pallas_call(functools.partial(self_backward_kernel, tq, tk, pairs), ou...  103 us
    pallas_call x1, Pallas kernels, self_forward(): pl.pallas_call(functools.partial(self_forward_kernel, tq, tk, pairs), out...  60.3 us
    ppermute x14, starting transfers between devices, shifted(): lax.ppermute(x, axis, [(i, i ^ offset) for i in range(lax.axis_size(axis))])  33.5 us
    ppermute x14, waiting for transfers between devices, shifted(): lax.ppermute(x, axis, [(i, i ^ offset) for i in range(lax.axis_size(axis))])  17.9 us
    pallas_call x2, Pallas kernels, input_gradient(): pl.pallas_call(input_grad_kernel, out_shape=jax.ShapeDtypeStruct((micro,...  14.5 us
    pallas_call x1, Pallas kernels, project(): pl.pallas_call(project_kernel, out_shape=(tall(width), long, tall(2 * wid...  14.4 us
    unnamed x27, local copies, waits for them, and re-layouts  12.7 us
  transfers between devices with their start and end apart: 21, of which 5 were waited for; matrix products, arithmetic and copies ran while one was open for 4% of the time, Pallas kernels for 40%

profile of v4, /device:TPU:0, one launch (start us, length us, event | category | flops | bytes accessed | tf_op | source)
XLA Modules:
  0.0 476.7 jit_solution(9136761106884476410)
XLA Ops:
  19.5 5.1 %collective-permute-start.1 = (bf16[1,1,1,16,1536]{4,3,2,1,0:T(8,128)(2,1)S(1)}, bf16[1,1,1,16,1536]{4,3,2,1,0:T(8,128)(2,1)S(1)}, u32[]{:S(2)}, u32[]{:S(2)}) collective-permute-start(bf16[1,1,1,16,1536]{4,3,2,1,0:T(8,128)(2,1)S(1)} %bitcast.87), channel_id=1, source_target_pairs={{0,24},{1,25},{2,26},{3,27},{4,28},{5,29},{6,30},{7,31},{8,16},{9,... | collective-permute-start | bytes 147464 | tf_op jit(solution)/shard_map/ppermute | solution.py:61
  26.5 2.8 collective-permute-start.8
  31.3 2.7 collective-permute-start.4
  35.1 5.5 %collective-permute-done.4 = bf16[4,1,1,16,1536]{4,3,2,1,0:T(8,128)(2,1)S(1)} collective-permute-done((bf16[4,1,1,16,1536]{4,3,2,1,0:T(8,128)(2,1)S(1)}, bf16[4,1,1,16,1536]{4,3,2,1,0:T(8,128)(2,1)S(1)}, u32[]{:S(2)}, u32[]{:S(2)}) %collective-permute-start.4) | collective-permute-done | bytes 196640 | tf_op jit(solution)/shard_map/ppermute | solution.py:61
  40.5 3.5 collective-permute-done.5
  46.8 1.3 pad_maximum_fusion
  48.1 14.4 %project.1 = (bf16[3,512,1024]{2,1,0:T(8,128)(2,1)}, bf16[3,1024,1024]{2,1,0:T(8,128)(2,1)}, bf16[3,1024,1024]{2,1,0:T(8,128)(2,1)}, bf16[3,1024,1024]{2,1,0:T(8,128)(2,1)}, bf16[3,1024,1024]{2,1,0:T(8,128)(2,1)}) custom-call(bf16[3,1024,512]{2,1,0:T(8,128)(2,1)} %x_ref.2, bf16[3,1024,512]{2,1,0:T(8,128)(2,1)} %collective-permute-done.far_ref, ...), custom_call_target="tpu_custom_call" | custom-call | flops 8053063680 | bytes 34603008 | tf_op jit(solution)/shard_map/project/pallas_call | solution.py:157
  62.6 60.3 %self_forward.1 = (f32[3,512,1024]{2,1,0:T(8,128)}, f32[3,8,1024]{2,1,0:T(8,128)}) custom-call(s32[3,4,3]{2,1,0:T(4,128)} %pad_add_fusion.1.tiles, bf16[3,512,1024]{2,1,0:T(8,128)(2,1)} %get-tuple-element.67.qt_ref, bf16[3,1024,1024]{2,1,0:T(8,128)(2,1)} %get-tuple-element.68.kp_ref.vp_ref, bf16[3,1024,1024]{2,1,0:T(8,128)(2,1)} %get-tuple-element.69.kl_ref.vl_ref, ...), custom_call_target="tpu_custom_call" | custom-call | flops 6442450944 | bytes 25165824 | tf_op jit(solution)/shard_map/self_forward/pallas_call | solution.py:258
  123.7 169.9 %middle.1 = (bf16[3,1024,512]{2,1,0:T(8,128)(2,1)}, bf16[3,512,1024]{2,1,0:T(8,128)(2,1)}, f32[3,8,1024]{2,1,0:T(8,128)}, f32[3,1024,512]{2,1,0:T(8,128)}, f32[3...) custom-call(bf16[3,1024,512]{2,1,0:T(8,128)(2,1)} %x_ref.2, ...), custom_call_target="tpu_custom_call" | custom-call | flops 72477573120 | bytes 70778880 | tf_op jit(solution)/shard_map/middle/pallas_call | solution.py:811
  293.7 1.4 copy-done
  296.2 103.4 %self_backward.1 = (bf16[3,512,1024]{2,1,0:T(8,128)(2,1)}, bf16[3,1024,512]{2,1,0:T(8,128)(2,1)}, bf16[3,1024,512]{2,1,0:T(8,128)(2,1)}, bf16[3,1024,512]{2,1,0:T(8,128)(2,1)}, f32[512,1536]{1,0:T(8,128)}) custom-call(s32[3,4,3]{2,1,0:T(4,128)} %pad_add_fusion.1.tiles, bf16[3,512,1024]{2,1,0:T(8,128)(2,1)} %get-tuple-element.67.qt_ref, ...), custom_call_target="tpu_custom_call" | custom-call | flops 16106127360 | bytes 62914560 | tf_op jit(solution)/shard_map/self_backward/pallas_call | solution.py:412
  399.7 2.4 dynamic-slice_convert_fusion
  402.1 1.5 collective-permute-start.9
  403.7 6.0 %collective-permute-done.10 = bf16[4,4,1,16,1536]{4,3,2,1,0:T(8,128)(2,1)} collective-permute-done((bf16[4,4,1,16,1536]{4,3,2,1,0:T(8,128)(2,1)}, bf16[4,4,1,16,1536]{4,3,2,1,0:T(8,128)(2,1)}, u32[]{:S(2)}, u32[]{:S(2)}) %collective-permute-start.10) | collective-permute-done | bytes 786464 | tf_op jit(solution)/shard_map/ppermute | solution.py:61
  409.6 1.9 convert_add_fusion
  411.6 3.4 collective-permute-start.13
  415.0 14.8 %collective-permute-start.14 = (bf16[4,1,1,16,1536]{4,3,2,1,0:T(8,128)(2,1)S(1)}, bf16[4,1,1,16,1536]{4,3,2,1,0:T(8,128)(2,1)S(1)}, u32[]{:S(2)}, u32[]{:S(2)}) collective-permute-start(bf16[4,1,1,16,1536]{4,3,2,1,0:T(8,128)(2,1)S(1)} %get-tuple-element.99), channel_id=1, source_target_pairs={{0,4},{1,5},{2,6},{3,7},{4,0},{5,1},{6,2},{7,3},{8,12},{9,13},{10,... | collective-permute-start | bytes 589832 | tf_op jit(solution)/shard_map/ppermute | solution.py:61
  429.8 1.4 collective-permute-start.15
  432.9 8.9 %input_gradient.2.others_0_ = bf16[3,1024,512]{2,1,0:T(8,128)(2,1)} custom-call(bf16[3,512,1024]{2,1,0:T(8,128)(2,1)} %get-tuple-element.85.dqt_ref, bf16[3,1024,512]{2,1,0:T(8,128)(2,1)} %get-tuple-element.86.dk_ref, bf16[3,1024,512]{2,1,0:T(8,128)(2,1)} %get-tuple-element.87.dv_ref, bf16[3,1024,512]{2,1,0:T(8,128)(2,1)} %copy-done.1, ...), custom_call_target="tpu_custom_call" | custom-call | flops 3221225472 | bytes 18350080 | tf_op jit(solution)/shard_map/input_gradient/pallas_call | solution.py:890
  441.9 2.6 collective-permute-done.15
  444.7 4.3 collective-permute-start.18
  449.0 5.5 %input_gradient.3 = bf16[3,1024,512]{2,1,0:T(8,128)(2,1)} custom-call(bf16[3,512,1024]{2,1,0:T(8,128)(2,1)} %get-tuple-element.85.dqt_ref, bf16[3,1024,512]{2,1,0:T(8,128)(2,1)} %get-tuple-element.86.dk_ref, bf16[3,1024,512]{2,1,0:T(8,128)(2,1)} %get-tuple-element.87.dv_ref, bf16[3,1024,512]{2,1,0:T(8,128)(2,1)} %copy-done.1, ...), custom_call_target="tpu_custom_call", output_to_operand_aliasing={{}: (6, {})} | custom-call | flops 1610612736 | bytes 9961472 | tf_op jit(solution)/shard_map/input_gradient/pallas_call | solution.py:890
  454.6 1.8 fusion
  456.4 2.5 add_convert_fusion
  (116 shorter events, 34.6 us)
Async XLA Ops:
  7.2 115.7 %all-gather.2.cloned.1.call-start = ((), (), s32[]{:S(2)}) async-start(), calls=%async_computation.1 | async-start | bytes 7163904 | tf_op jit(solution)/shard_map/all_gather | solution.py:962
  19.4 439.5 %reduce-scatter.2.cloned.1.call-start = ((), (), s32[]{:S(2)}) async-start(), calls=%async_computation.2 | async-start | bytes 7163904 | tf_op jit(solution)/shard_map/reduce_scatter | solution.py:995
  19.5 11.7 %collective-permute-start.1 = (bf16[1,1,1,16,1536]{4,3,2,1,0:T(8,128)(2,1)S(1)}, bf16[1,1,1,16,1536]{4,3,2,1,0:T(8,128)(2,1)S(1)}, u32[]{:S(2)}, u32[]{:S(2)}) collective-permute-start(bf16[1,1,1,16,1536]{4,3,2,1,0:T(8,128)(2,1)S(1)} %bitcast.87), channel_id=1, source_target_pairs={{0,24},{1,25},{2,26},{3,27},{4,28},{5,29},{6,30},{7,31},{8,16},{9,... | collective-permute-start | bytes 147464 | tf_op jit(solution)/shard_map/ppermute | solution.py:61
  24.6 6.6 %collective-permute-start.2 = (bf16[1,1,1,16,1536]{4,3,2,1,0:T(8,128)(2,1)S(1)}, bf16[1,1,1,16,1536]{4,3,2,1,0:T(8,128)(2,1)S(1)}, u32[]{:S(2)}, u32[]{:S(2)}) collective-permute-start(bf16[1,1,1,16,1536]{4,3,2,1,0:T(8,128)(2,1)S(1)} %bitcast.88), channel_id=1, source_target_pairs={{0,16},{1,17},{2,18},{3,19},{4,20},{5,21},{6,22},{7,23},{8,24},{9,... | collective-permute-start | bytes 147464 | tf_op jit(solution)/shard_map/ppermute | solution.py:61
  24.6 6.7 %collective-permute-start.3 = (bf16[1,1,1,16,1536]{4,3,2,1,0:T(8,128)(2,1)S(1)}, bf16[1,1,1,16,1536]{4,3,2,1,0:T(8,128)(2,1)S(1)}, u32[]{:S(2)}, u32[]{:S(2)}) collective-permute-start(bf16[1,1,1,16,1536]{4,3,2,1,0:T(8,128)(2,1)S(1)} %bitcast.89), channel_id=1, source_target_pairs={{0,8},{1,9},{2,10},{3,11},{4,12},{5,13},{6,14},{7,15},{8,0},{9,1},... | collective-permute-start | bytes 147464 | tf_op jit(solution)/shard_map/ppermute | solution.py:61
  25.2 22.9 %collective-permute-start = (bf16[3,1024,512]{2,1,0:T(8,128)(2,1)}, bf16[3,1024,512]{2,1,0:T(8,128)(2,1)}, u32[]{:S(2)}, u32[]{:S(2)}) collective-permute-start(bf16[3,1024,512]{2,1,0:T(8,128)(2,1)} %x_ref.2), channel_id=1, source_target_pairs={{1,0},{3,2},{5,4},{7,6},{9,8},{11,10},{13,12},{15,14},{17,16},{19,... | collective-permute-start | bytes 9437192 | tf_op jit(solution)/shard_map/ppermute | solution.py:53
  26.5 96.3 %collective-permute-start.8 = (bf16[3,256,512]{2,1,0:T(8,128)(2,1)}, bf16[3,256,512]{2,1,0:T(8,128)(2,1)S(1)}, u32[]{:S(2)}, u32[]{:S(2)}) collective-permute-start(bf16[3,256,512]{2,1,0:T(8,128)(2,1)} %mem_ref), channel_id=1, source_target_pairs={{0,1},{1,0},{2,3},{3,2},{4,5},{5,4},{6,7},{7,6},{8,9},{9,8},{10,11... | collective-permute-start | bytes 2359304 | tf_op jit(solution)/shard_map/ppermute | solution.py:49
  31.3 9.2 %collective-permute-start.4 = (bf16[4,1,1,16,1536]{4,3,2,1,0:T(8,128)(2,1)S(1)}, bf16[4,1,1,16,1536]{4,3,2,1,0:T(8,128)(2,1)S(1)}, u32[]{:S(2)}, u32[]{:S(2)}) collective-permute-start(bf16[4,1,1,16,1536]{4,3,2,1,0:T(8,128)(2,1)S(1)} %pad_maximum_fusion.2), channel_id=1, source_target_pairs={{0,6},{1,7},{2,4},{3,5},{4,2},{5,3},{6,0},{7,1},{8,14},{9,15},{10,... | collective-permute-start | bytes 589832 | tf_op jit(solution)/shard_map/ppermute | solution.py:61
  34.0 10.1 %collective-permute-start.5 = (bf16[4,1,1,16,1536]{4,3,2,1,0:T(8,128)(2,1)S(1)}, bf16[4,1,1,16,1536]{4,3,2,1,0:T(8,128)(2,1)S(1)}, u32[]{:S(2)}, u32[]{:S(2)}) collective-permute-start(bf16[4,1,1,16,1536]{4,3,2,1,0:T(8,128)(2,1)S(1)} %pad_maximum_fusion.2), channel_id=1, source_target_pairs={{0,4},{1,5},{2,6},{3,7},{4,0},{5,1},{6,2},{7,3},{8,12},{9,13},{10,... | collective-permute-start | bytes 589832 | tf_op jit(solution)/shard_map/ppermute | solution.py:61
  34.5 9.6 %collective-permute-start.6 = (bf16[4,1,1,16,1536]{4,3,2,1,0:T(8,128)(2,1)S(1)}, bf16[4,1,1,16,1536]{4,3,2,1,0:T(8,128)(2,1)S(1)}, u32[]{:S(2)}, u32[]{:S(2)}) collective-permute-start(bf16[4,1,1,16,1536]{4,3,2,1,0:T(8,128)(2,1)S(1)} %pad_maximum_fusion.2), channel_id=1, source_target_pairs={{0,2},{1,3},{2,0},{3,1},{4,6},{5,7},{6,4},{7,5},{8,10},{9,11},{10,... | collective-permute-start | bytes 589832 | tf_op jit(solution)/shard_map/ppermute | solution.py:61
  44.3 2.4 collective-permute-start.7
  402.1 29.2 %collective-permute-start.9 = (bf16[3,1024,512]{2,1,0:T(8,128)(2,1)}, bf16[3,1024,512]{2,1,0:T(8,128)(2,1)S(1)}, u32[]{:S(2)}, u32[]{:S(2)}) collective-permute-start(bf16[3,1024,512]{2,1,0:T(8,128)(2,1)} %get-tuple-element.90), channel_id=1, source_target_pairs={{0,1},{2,3},{4,5},{6,7},{8,9},{10,11},{12,13},{14,15},{16,17},{18,... | collective-permute-start | bytes 9437192 | tf_op jit(solution)/shard_map/ppermute | solution.py:57
  403.6 6.1 %collective-permute-start.10 = (bf16[4,4,1,16,1536]{4,3,2,1,0:T(8,128)(2,1)}, bf16[4,4,1,16,1536]{4,3,2,1,0:T(8,128)(2,1)}, u32[]{:S(2)}, u32[]{:S(2)}) collective-permute-start(bf16[4,4,1,16,1536]{4,3,2,1,0:T(8,128)(2,1)} %dynamic-slice_convert_fusion), channel_id=1, source_target_pairs={{0,1},{1,0},{2,3},{3,2},{4,5},{5,4},{6,7},{7,6},{8,9},{9,8},{10,11... | collective-permute-start | bytes 2359304 | tf_op jit(solution)/shard_map/ppermute | solution.py:61
  411.6 30.2 %collective-permute-start.13 = (bf16[4,1,1,16,1536]{4,3,2,1,0:T(8,128)(2,1)S(1)}, bf16[4,1,1,16,1536]{4,3,2,1,0:T(8,128)(2,1)S(1)}, u32[]{:S(2)}, u32[]{:S(2)}) collective-permute-start(bf16[4,1,1,16,1536]{4,3,2,1,0:T(8,128)(2,1)S(1)} %get-tuple-element.98), channel_id=1, source_target_pairs={{0,2},{1,3},{2,0},{3,1},{4,6},{5,7},{6,4},{7,5},{8,10},{9,11},{10,... | collective-permute-start | bytes 589832 | tf_op jit(solution)/shard_map/ppermute | solution.py:61
  415.0 26.8 %collective-permute-start.14 = (bf16[4,1,1,16,1536]{4,3,2,1,0:T(8,128)(2,1)S(1)}, bf16[4,1,1,16,1536]{4,3,2,1,0:T(8,128)(2,1)S(1)}, u32[]{:S(2)}, u32[]{:S(2)}) collective-permute-start(bf16[4,1,1,16,1536]{4,3,2,1,0:T(8,128)(2,1)S(1)} %get-tuple-element.99), channel_id=1, source_target_pairs={{0,4},{1,5},{2,6},{3,7},{4,0},{5,1},{6,2},{7,3},{8,12},{9,13},{10,... | collective-permute-start | bytes 589832 | tf_op jit(solution)/shard_map/ppermute | solution.py:61
  429.8 14.6 %collective-permute-start.15 = (bf16[4,1,1,16,1536]{4,3,2,1,0:T(8,128)(2,1)S(1)}, bf16[4,1,1,16,1536]{4,3,2,1,0:T(8,128)(2,1)S(1)}, u32[]{:S(2)}, u32[]{:S(2)}) collective-permute-start(bf16[4,1,1,16,1536]{4,3,2,1,0:T(8,128)(2,1)S(1)} %get-tuple-element.100), channel_id=1, source_target_pairs={{0,6},{1,7},{2,4},{3,5},{4,2},{5,3},{6,0},{7,1},{8,14},{9,15},{10,... | collective-permute-start | bytes 589832 | tf_op jit(solution)/shard_map/ppermute | solution.py:61
  431.2 13.3 %collective-permute-start.11 = (bf16[3,256,512]{2,1,0:T(8,128)(2,1)}, bf16[3,256,512]{2,1,0:T(8,128)(2,1)S(1)}, u32[]{:S(2)}, u32[]{:S(2)}) collective-permute-start(bf16[3,256,512]{2,1,0:T(8,128)(2,1)} %get-tuple-element.96), channel_id=1, source_target_pairs={{0,1},{1,0},{2,3},{3,2},{4,5},{5,4},{6,7},{7,6},{8,9},{9,8},{10,11... | collective-permute-start | bytes 2359304 | tf_op jit(solution)/shard_map/ppermute | solution.py:49
  431.2 1.7 copy-start.1
  431.2 13.3 %collective-permute-start.12 = (bf16[3,256,512]{2,1,0:T(8,128)(2,1)}, bf16[3,256,512]{2,1,0:T(8,128)(2,1)S(1)}, u32[]{:S(2)}, u32[]{:S(2)}) collective-permute-start(bf16[3,256,512]{2,1,0:T(8,128)(2,1)} %get-tuple-element.97), channel_id=1, source_target_pairs={{0,1},{1,0},{2,3},{3,2},{4,5},{5,4},{6,7},{7,6},{8,9},{9,8},{10,11... | collective-permute-start | bytes 2359304 | tf_op jit(solution)/shard_map/ppermute | solution.py:49
  444.6 10.0 %copy-start.2 = (f32[3,256,512]{2,1,0:T(8,128)S(1)}, f32[3,256,512]{2,1,0:T(8,128)}, u32[]{:S(2)}) copy-start(f32[3,256,512]{2,1,0:T(8,128)} %get-tuple-element.107) | copy-start | bytes 4718596
  444.6 18.5 %collective-permute-start.16 = (bf16[1,1,1,16,1536]{4,3,2,1,0:T(8,128)(2,1)S(1)}, bf16[1,1,1,16,1536]{4,3,2,1,0:T(8,128)(2,1)S(1)}, u32[]{:S(2)}, u32[]{:S(2)}) collective-permute-start(bf16[1,1,1,16,1536]{4,3,2,1,0:T(8,128)(2,1)S(1)} %get-tuple-element.109), channel_id=1, source_target_pairs={{0,8},{1,9},{2,10},{3,11},{4,12},{5,13},{6,14},{7,15},{8,0},{9,1},... | collective-permute-start | bytes 147464 | tf_op jit(solution)/shard_map/ppermute | solution.py:61
  444.7 18.4 %collective-permute-start.17 = (bf16[1,1,1,16,1536]{4,3,2,1,0:T(8,128)(2,1)S(1)}, bf16[1,1,1,16,1536]{4,3,2,1,0:T(8,128)(2,1)S(1)}, u32[]{:S(2)}, u32[]{:S(2)}) collective-permute-start(bf16[1,1,1,16,1536]{4,3,2,1,0:T(8,128)(2,1)S(1)} %get-tuple-element.110), channel_id=1, source_target_pairs={{0,16},{1,17},{2,18},{3,19},{4,20},{5,21},{6,22},{7,23},{8,24},{9,... | collective-permute-start | bytes 147464 | tf_op jit(solution)/shard_map/ppermute | solution.py:61
  444.7 18.3 %collective-permute-start.18 = (bf16[1,1,1,16,1536]{4,3,2,1,0:T(8,128)(2,1)S(1)}, bf16[1,1,1,16,1536]{4,3,2,1,0:T(8,128)(2,1)S(1)}, u32[]{:S(2)}, u32[]{:S(2)}) collective-permute-start(bf16[1,1,1,16,1536]{4,3,2,1,0:T(8,128)(2,1)S(1)} %get-tuple-element.111), channel_id=1, source_target_pairs={{0,24},{1,25},{2,26},{3,27},{4,28},{5,29},{6,30},{7,31},{8,16},{9,... | collective-permute-start | bytes 147464 | tf_op jit(solution)/shard_map/ppermute | solution.py:61
  454.6 1.8 copy-start.3
  (3 other events, 3.0 us)
Sparse Core Ops, SparseCore 0:
  19.5 77.5 all-gather.1
  293.8 150.6 reduce-scatter.1
